TPU v7x, 32 devices: a whole 2x2x4 slice. The times are simulated.
32 devices in a mesh: dp: 16 (over z, y, x), head: 2 (over core).
Axes of the slice: x: 2, y: 2, z: 4, core: 2. Of those that a mesh axis runs over, the one named last changes fastest.
Arguments:
- inputs: bfloat16 [128, 200, 768], P(('dp', 'head')), may hold values from -6 to 6
- masked: int32 [128, 200], P(('dp', 'head')), may hold values 0 or 1
- key_valid: int32 [128, 200], P('dp'), may hold values from 0 to 1, as said below
- rel_index: int32 [200, 200], replicated, may hold values from 0 to 731
- mask_token: float32 [768], replicated, may hold values from -6 to 6
- ln1_gain: float32 [768], replicated, may hold values from 0.25 to 1.75
- ln1_bias: float32 [768], replicated, may hold values from -1.75 to 1.75
- w_qkv: bfloat16 [768, 3, 768], P(None, None, 'head'), may hold values from -0.21875 to 0.21875
- qv_bias: float32 [2, 768], P(None, 'head'), may hold values from -1.75 to 1.75
- rel_table: float32 [732, 12], P(None, 'head'), may hold values from -3 to 3
- w_proj: bfloat16 [768, 768], P('head'), may hold values from -0.875 to 0.875
- proj_bias: float32 [768], replicated, may hold values from -1.75 to 1.75
- gamma1: float32 [768], replicated, may hold values from 0.5 to 1.5
- ln2_gain: float32 [768], replicated, may hold values from 0.25 to 1.75
- ln2_bias: float32 [768], replicated, may hold values from -1.75 to 1.75
- w_fc1: bfloat16 [768, 3072], P(None, ('dp', 'head')), may hold values from -0.21875 to 0.21875
- fc1_bias: bfloat16 [3072], P(('dp', 'head')), may hold values from -1.75 to 1.75
- w_fc2: bfloat16 [3072, 768], P(('dp', 'head')), may hold values from -0.109375 to 0.109375
- fc2_bias: float32 [768], replicated, may hold values from -1.75 to 1.75
- gamma2: float32 [768], replicated, may hold values from 0.5 to 1.5
- cotangent: bfloat16 [128, 200, 768], P(('dp', 'head')), may hold values from -6 to 6
Outputs:
- out: bfloat16 [128, 200, 768], P(('dp', 'head'))
- grad_input: float32 [128, 200, 768], P(('dp', 'head'))
- grad_mask_token: float32 [768], replicated
- grad_ln1_gain: float32 [768], replicated
- grad_ln1_bias: float32 [768], replicated
- grad_qkv: float32 [768, 3, 768], P(None, None, 'head')
- grad_qv_bias: float32 [2, 768], P(None, 'head')
- grad_rel_table: float32 [732, 12], P(None, 'head')
- grad_proj: float32 [768, 768], P('head')
- grad_proj_bias: float32 [768], replicated
- grad_gamma1: float32 [768], replicated
- grad_ln2_gain: float32 [768], replicated
- grad_ln2_bias: float32 [768], replicated
- grad_fc1: float32 [768, 3072], P(None, ('dp', 'head'))
- grad_fc1_bias: float32 [3072], P(('dp', 'head'))
- grad_fc2: float32 [3072, 768], P(('dp', 'head'))
- grad_fc2_bias: float32 [768], replicated
- grad_gamma2: float32 [768], replicated
Inputs may be any that keep to these rules, and one draw needn't show every extreme that they name: In each image the ones of key_valid are a leading run of rows, at least 100 long.
All inputs are finite; a program needn't handle non-finite values. No bound on the sum of `masked` on one device may be relied on, other than what follows from the above.
Results may differ from a plain program's by a relative error of at most 0.012.
The roundings to bfloat16 on the way count: a program that leaves them out, or rounds other values in their place, can miss the bound.
Values may be sent and summed in bfloat16 or wider, within the bound.
A program may use at most 256 MiB of HBM per device.

v0:
```python
import jax
import jax.numpy as jnp
from jax import lax
from jax.sharding import PartitionSpec as P

MBATCH = 2


epsilon = 1e-06
root_half = 0.7071067811865476
highest = lax.Precision.HIGHEST


def layer_norm(values, scale_vec, offset_vec):
    center = values - jnp.mean(values, axis=-1, keepdims=True)
    spread = jnp.mean(center * center, axis=-1, keepdims=True)
    return center * lax.rsqrt(spread + epsilon) * scale_vec + offset_vec


def gelu_exact(values):
    return 0.5 * values * (1.0 + jax.scipy.special.erf(values * root_half))


def block_count():
    return 4


def one_hot_block(rel_index, start, stop, entry_count):
    picked = rel_index[start:stop].reshape(-1)
    entries = lax.broadcasted_iota(jnp.int32, (1, entry_count), 1)
    return (picked[:, None] == entries).astype(jnp.float32)


def table_bias(rel_table, rel_index):
    row_count = rel_index.shape[0]
    entry_count, heads_here = rel_table.shape
    pieces = block_count()
    step_rows = row_count // pieces
    parts_list = []
    for piece_index in range(pieces):
        selector = one_hot_block(
            rel_index, piece_index * step_rows, (piece_index + 1) * step_rows, entry_count
        )
        parts_list.append(
            jnp.einsum(
                "rh,nr->hn",
                rel_table,
                selector,
                precision=highest,
                preferred_element_type=jnp.float32,
            )
        )
    return jnp.concatenate(parts_list, axis=1).reshape(heads_here, row_count, row_count)


def table_grad(score_totals, rel_index, entry_count):
    row_count = rel_index.shape[0]
    pieces = block_count()
    step_rows = row_count // pieces
    width = step_rows * row_count
    total = None
    for piece_index in range(pieces):
        selector = one_hot_block(
            rel_index, piece_index * step_rows, (piece_index + 1) * step_rows, entry_count
        )
        columns = score_totals[:, piece_index * width : (piece_index + 1) * width]
        term = jnp.einsum(
            "hn,nr->rh", columns, selector, precision=highest, preferred_element_type=jnp.float32
        )
        total = term if total is None else total + term
    return total


def score_block(queries, keyset, bias_table, valid_part, score_scale, heads_here):
    count, row_count, columns = queries.shape
    shaped = (count, row_count, heads_here, columns // heads_here)
    scores = (
        jnp.einsum(
            "gqhe,gkhe->ghqk",
            queries.reshape(shaped),
            keyset.reshape(shaped),
            preferred_element_type=jnp.float32,
        )
        * score_scale
    )
    scores = scores + bias_table[None]
    return jnp.where(valid_part[:, None, None, :] > 0, scores, -1e30)


def add_nested(left, right):
    return jax.tree.map(lambda first_val, second_val: first_val + second_val, left, right)


def reduce_end(dp_part, small_part, mlp_part):
    g_qkv, g_qvb, g_table, g_proj = dp_part
    g_mask, g_ln1g, g_ln1b, g_projb, g_gamma1, g_ln2g, g_ln2b, g_fc2b, g_gamma2 = small_part
    g_fc1, g_fc1b, g_fc2 = mlp_part
    summed_dp = lax.psum((g_qkv, g_qvb, g_table, g_proj), "dp")
    summed_small = lax.psum(
        (g_mask, g_ln1g, g_ln1b, g_projb, g_gamma1, g_ln2g, g_ln2b, g_fc2b, g_gamma2),
        ("dp", "head"),
    )
    summed_mlp = (
        lax.psum_scatter(g_fc1, ("dp", "head"), scatter_dimension=1, tiled=True),
        lax.psum_scatter(g_fc1b, ("dp", "head"), scatter_dimension=0, tiled=True),
        lax.psum_scatter(g_fc2, ("dp", "head"), scatter_dimension=0, tiled=True),
    )
    return (tuple(summed_dp), tuple(summed_small), tuple(summed_mlp))


def shards(
    inputs,
    masked,
    key_valid,
    rel_index,
    mask_token,
    ln1_gain,
    ln1_bias,
    w_qkv,
    qv_bias,
    rel_table,
    w_proj,
    proj_bias,
    gamma1,
    ln2_gain,
    ln2_bias,
    w_fc1,
    fc1_bias,
    w_fc2,
    fc2_bias,
    gamma2,
    cotangent,
):
    local_images, row_count, feature_count = inputs.shape
    group_size = lax.axis_size("head")
    part_images = local_images // MBATCH
    heads_here = rel_table.shape[1]
    head_width = w_qkv.shape[2] // heads_here
    score_scale = head_width ** (-0.5)
    bias_table = table_bias(rel_table, rel_index)
    valid_split = key_valid.reshape(group_size, local_images, row_count)
    fetched = (
        lax.all_gather(w_fc1, ("dp", "head"), axis=1, tiled=True),
        lax.all_gather(fc1_bias, ("dp", "head"), axis=0, tiled=True),
        lax.all_gather(w_fc2, ("dp", "head"), axis=0, tiled=True),
    )
    stored = []
    results = []
    for micro_index in range(MBATCH):
        offset = micro_index * part_images
        chosen = masked[offset : offset + part_images].astype(jnp.float32)[..., None]
        hidden_in = (
            inputs[offset : offset + part_images].astype(jnp.float32) * (1.0 - chosen)
            + chosen * mask_token
        )
        normed_local = layer_norm(hidden_in, ln1_gain, ln1_bias).astype(jnp.bfloat16)
        normed = lax.all_gather(normed_local, "head", axis=0, tiled=True)
        valid_part = valid_split[:, offset : offset + part_images].reshape(
            group_size * part_images, row_count
        )
        projected = jnp.einsum("gtd,dce->gtce", normed, w_qkv, preferred_element_type=jnp.float32)
        queries = (projected[:, :, 0] + qv_bias[0]).astype(jnp.bfloat16)
        keyset = projected[:, :, 1].astype(jnp.bfloat16)
        valueset = (projected[:, :, 2] + qv_bias[1]).astype(jnp.bfloat16)
        scores = score_block(queries, keyset, bias_table, valid_part, score_scale, heads_here)
        row_peak = jnp.max(scores, axis=-1, keepdims=True)
        log_total = row_peak + jnp.log(jnp.sum(jnp.exp(scores - row_peak), axis=-1, keepdims=True))
        attn_weights = jnp.exp(scores - log_total).astype(jnp.bfloat16)
        count = queries.shape[0]
        shaped = (count, row_count, heads_here, head_width)
        attended = jnp.einsum(
            "ghqk,gkhe->gqhe",
            attn_weights,
            valueset.reshape(shaped),
            preferred_element_type=jnp.float32,
        )
        attended = attended.reshape(count, row_count, heads_here * head_width).astype(jnp.bfloat16)
        partial_proj = jnp.einsum(
            "gtc,cd->gtd", attended, w_proj, preferred_element_type=jnp.float32
        )
        attn_branch = (
            lax.psum_scatter(partial_proj, "head", scatter_dimension=0, tiled=True) + proj_bias
        )
        residual = hidden_in + gamma1 * attn_branch
        normed2 = layer_norm(residual, ln2_gain, ln2_bias).astype(jnp.bfloat16)
        pre_gelu = (
            jnp.einsum("gtd,df->gtf", normed2, fetched[0], preferred_element_type=jnp.float32)
            + fetched[1]
        )
        active = gelu_exact(pre_gelu).astype(jnp.bfloat16)
        branch = (
            jnp.einsum("gtf,fd->gtd", active, fetched[2], preferred_element_type=jnp.float32)
            + fc2_bias
        )
        results.append((residual + gamma2 * branch).astype(jnp.bfloat16))
        stored.append(
            (
                offset,
                chosen,
                hidden_in,
                normed,
                valid_part,
                queries,
                keyset,
                valueset,
                log_total,
                attended,
                attn_branch,
                residual,
                normed2,
                pre_gelu,
                active,
                branch,
            )
        )
    back_weights = (fetched[0], fetched[2])
    input_grads = []
    totals = None
    for micro_index in range(MBATCH):
        (
            offset,
            chosen,
            hidden_in,
            normed,
            valid_part,
            queries,
            keyset,
            valueset,
            log_total,
            attended,
            attn_branch,
            residual,
            normed2,
            pre_gelu,
            active,
            branch,
        ) = stored[micro_index]
        upstream = cotangent[offset : offset + part_images].astype(jnp.float32)
        g_gamma2 = jnp.sum(upstream * branch, axis=(0, 1))
        grad_branch = (upstream * gamma2).astype(jnp.bfloat16)
        g_fc2b = jnp.sum(grad_branch, axis=(0, 1), dtype=jnp.float32)
        g_fc2 = jnp.einsum("gtf,gtd->fd", active, grad_branch, preferred_element_type=jnp.float32)
        grad_active = jnp.einsum(
            "gtd,fd->gtf", grad_branch, back_weights[1], preferred_element_type=jnp.float32
        )
        gelu_value, gelu_back = jax.vjp(gelu_exact, pre_gelu)
        grad_pre = gelu_back(grad_active)[0].astype(jnp.bfloat16)
        g_fc1b = jnp.sum(grad_pre, axis=(0, 1), dtype=jnp.float32)
        g_fc1 = jnp.einsum("gtd,gtf->df", normed2, grad_pre, preferred_element_type=jnp.float32)
        grad_normed2 = jnp.einsum(
            "gtf,df->gtd", grad_pre, back_weights[0], preferred_element_type=jnp.float32
        )
        norm_value, norm_back = jax.vjp(layer_norm, residual, ln2_gain, ln2_bias)
        grad_res_norm, g_ln2g, g_ln2b = norm_back(grad_normed2)
        grad_residual = upstream + grad_res_norm
        g_gamma1 = jnp.sum(grad_residual * attn_branch, axis=(0, 1))
        grad_proj_rows = (grad_residual * gamma1).astype(jnp.bfloat16)
        g_projb = jnp.sum(grad_proj_rows, axis=(0, 1), dtype=jnp.float32)
        grad_proj_full = lax.all_gather(grad_proj_rows, "head", axis=0, tiled=True)
        g_proj = jnp.einsum(
            "gtc,gtd->cd", attended, grad_proj_full, preferred_element_type=jnp.float32
        )
        grad_attended = jnp.einsum(
            "gtd,cd->gtc", grad_proj_full, w_proj, preferred_element_type=jnp.float32
        ).astype(jnp.bfloat16)
        count = queries.shape[0]
        shaped = (count, row_count, heads_here, head_width)
        scores = score_block(queries, keyset, bias_table, valid_part, score_scale, heads_here)
        soft_probs = jnp.exp(scores - log_total)
        soft_low = soft_probs.astype(jnp.bfloat16)
        grad_att4 = grad_attended.reshape(shaped)
        grad_value = jnp.einsum(
            "ghqk,gqhe->gkhe", soft_low, grad_att4, preferred_element_type=jnp.float32
        ).astype(jnp.bfloat16)
        grad_probs = jnp.einsum(
            "gqhe,gkhe->ghqk",
            grad_att4,
            valueset.reshape(shaped),
            preferred_element_type=jnp.float32,
        )
        row_delta = jnp.sum(soft_probs * grad_probs, axis=-1, keepdims=True)
        grad_scores = (soft_probs * (grad_probs - row_delta)).astype(jnp.bfloat16)
        score_totals = jnp.sum(grad_scores, axis=0, dtype=jnp.float32).reshape(
            heads_here, row_count * row_count
        )
        g_table = table_grad(score_totals, rel_index, rel_table.shape[0])
        grad_query = (
            jnp.einsum(
                "ghqk,gkhe->gqhe",
                grad_scores,
                keyset.reshape(shaped),
                preferred_element_type=jnp.float32,
            )
            * score_scale
        ).astype(jnp.bfloat16)
        grad_key = (
            jnp.einsum(
                "ghqk,gqhe->gkhe",
                grad_scores,
                queries.reshape(shaped),
                preferred_element_type=jnp.float32,
            )
            * score_scale
        ).astype(jnp.bfloat16)
        flat_cols = heads_here * head_width
        grad_stack = jnp.stack(
            (
                grad_query.reshape(count, row_count, flat_cols),
                grad_key.reshape(count, row_count, flat_cols),
                grad_value.reshape(count, row_count, flat_cols),
            ),
            axis=2,
        )
        g_qkv = jnp.einsum("gtd,gtce->dce", normed, grad_stack, preferred_element_type=jnp.float32)
        g_qvb = jnp.stack(
            (
                jnp.sum(grad_stack[:, :, 0], axis=(0, 1), dtype=jnp.float32),
                jnp.sum(grad_stack[:, :, 2], axis=(0, 1), dtype=jnp.float32),
            )
        )
        grad_normed_part = jnp.einsum(
            "gtce,dce->gtd", grad_stack, w_qkv, preferred_element_type=jnp.float32
        )
        grad_normed = lax.psum_scatter(grad_normed_part, "head", scatter_dimension=0, tiled=True)
        norm_first, norm_back_first = jax.vjp(layer_norm, hidden_in, ln1_gain, ln1_bias)
        grad_hid_norm, g_ln1g, g_ln1b = norm_back_first(grad_normed)
        grad_hidden = grad_hid_norm + grad_residual
        input_grads.append(grad_hidden * (1.0 - chosen))
        g_mask = jnp.sum(grad_hidden * chosen, axis=(0, 1))
        dp_part = (g_qkv, g_qvb, g_table, g_proj)
        small_part = (g_mask, g_ln1g, g_ln1b, g_projb, g_gamma1, g_ln2g, g_ln2b, g_fc2b, g_gamma2)
        mlp_part = (g_fc1, g_fc1b, g_fc2)
        reduced_part = (dp_part, small_part, mlp_part)
        if micro_index == 0:
            totals = reduced_part
        else:
            totals = add_nested(totals, reduced_part)
    final_sums = reduce_end(totals[0], totals[1], totals[2])
    dp_sum, small_sum, mlp_sum = final_sums
    g_qkv, g_qvb, g_table, g_proj = dp_sum
    g_mask, g_ln1g, g_ln1b, g_projb, g_gamma1, g_ln2g, g_ln2b, g_fc2b, g_gamma2 = small_sum
    g_fc1, g_fc1b, g_fc2 = mlp_sum
    return (
        jnp.concatenate(results, axis=0),
        jnp.concatenate(input_grads, axis=0),
        g_mask,
        g_ln1g,
        g_ln1b,
        g_qkv,
        g_qvb,
        g_table,
        g_proj,
        g_projb,
        g_gamma1,
        g_ln2g,
        g_ln2b,
        g_fc1,
        g_fc1b,
        g_fc2,
        g_fc2b,
        g_gamma2,
    )


def solution(mesh):
    in_specs = (
        P(("dp", "head"), None, None),
        P(("dp", "head"), None),
        P("dp", None),
        P(),
        P(),
        P(),
        P(),
        P(None, None, "head"),
        P(None, "head"),
        P(None, "head"),
        P("head", None),
        P(),
        P(),
        P(),
        P(),
        P(None, ("dp", "head")),
        P(("dp", "head")),
        P(("dp", "head"), None),
        P(),
        P(),
        P(("dp", "head"), None, None),
    )
    out_specs = (
        P(("dp", "head"), None, None),
        P(("dp", "head"), None, None),
        P(),
        P(),
        P(),
        P(None, None, "head"),
        P(None, "head"),
        P(None, "head"),
        P("head", None),
        P(),
        P(),
        P(),
        P(),
        P(None, ("dp", "head")),
        P(("dp", "head")),
        P(("dp", "head"), None),
        P(),
        P(),
    )
    return jax.shard_map(shards, mesh=mesh, in_specs=in_specs, out_specs=out_specs, check_vma=False)
```

profile of v0, /device:TPU:0, one launch (start us, length us, event | category | flops | bytes accessed | tf_op | source)
XLA Modules:
  0.0 751.6 jit_solution(7338352959528180767)
XLA Ops:
  15.9 15.1 %fusion.24 = f32[6,10000]{1,0:T(8,128)} fusion(f32[732,6]{0,1:T(8,128)} %param.30, s32[10000]{0:T(1024)S(1)} %eq.32), kind=kOutput, calls=%fused_computation.28 | convolution fusion | flops 534360000 | bytes 297568 | tf_op jit(solution)/shard_map/rh,nr->hn/dot_general | solution.py:45
  31.0 13.8 %fusion.25 = f32[6,10000]{1,0:T(8,128)S(1)} fusion(f32[732,6]{0,1:T(8,128)S(1)} %copy-done.96, s32[10000]{0:T(1024)S(1)} %eq.36), kind=kOutput, calls=%fused_computation.29 | convolution fusion | flops 534360000 | bytes 297568 | tf_op jit(solution)/shard_map/rh,nr->hn/dot_general | solution.py:45
  50.1 14.4 %fusion.26 = f32[6,10000]{1,0:T(8,128)S(1)} fusion(f32[732,6]{0,1:T(8,128)} %param.30, s32[10000]{0:T(1024)S(1)} %eq.40), kind=kOutput, calls=%fused_computation.30 | convolution fusion | flops 534360000 | bytes 297568 | tf_op jit(solution)/shard_map/rh,nr->hn/dot_general | solution.py:45
  66.7 13.6 %fusion.27 = f32[6,10000]{1,0:T(8,128)S(1)} fusion(f32[732,6]{0,1:T(8,128)S(1)} %copy-done.97, s32[10000]{0:T(1024)S(1)} %eq.44), kind=kOutput, calls=%fused_computation.31 | convolution fusion | flops 534360000 | bytes 297568 | tf_op jit(solution)/shard_map/rh,nr->hn/dot_general | solution.py:45
  114.0 43.3 %all-reduce = bf16[3072]{0:T(1024)(128)(2,1)S(1)} all-reduce(bf16[3072]{0:T(1024)(128)(2,1)S(1)} %dynamic-update-slice), channel_id=1, replica_groups=mesh['dp'=16,'head'=2] {'dp','head'}, use_global_device_ids=true, to_apply=%add | all-reduce | flops 3072 | bytes 12288
  160.4 22.3 %all-gather.9.cloned.1.call-done = bf16[768,3072]{0,1:T(8,128)(2,1)} async-done(((bf16[768,96]{0,1:T(8,128)(2,1)}), bf16[768,3072]{0,1:T(8,128)(2,1)}) %all-gather.9.cloned.1.call-update) | async-done | bytes 4718608 | tf_op jit(solution)/shard_map/all_gather | solution.py:143
  189.8 57.9 %all-gather.11.cloned.1.call-done = bf16[3072,768]{1,0:T(8,128)(2,1)} async-done(((bf16[96,768]{1,0:T(8,128)(2,1)}), bf16[3072,768]{1,0:T(8,128)(2,1)}) %all-gather.11.cloned.1.call-update) | async-done | bytes 4718608 | tf_op jit(solution)/shard_map/all_gather | solution.py:145
  247.7 7.2 convert_reduce_fusion.1
  262.0 7.2 all-gather.15.cloned.1.call-done
  300.6 11.3 %reduce-scatter.11.cloned.1.call-done = f32[2,200,768]{2,1,0:T(8,128)} async-done(((f32[4,200,768]{2,1,0:T(8,128)}), f32[2,200,768]{2,1,0:T(8,128)}) %reduce-scatter.11.cloned.1.call-update) | async-done | bytes 1228816 | tf_op jit(solution)/shard_map/reduce_scatter | solution.py:324
  318.1 10.4 %all-gather.13.cloned.1.call-done = bf16[4,200,768]{2,1,0:T(8,128)(2,1)} async-done(((bf16[2,200,768]{2,1,0:T(8,128)(2,1)}), bf16[4,200,768]{2,1,0:T(8,128)(2,1)}) %all-gather.13.cloned.1.call-update) | async-done | bytes 1228816 | tf_op jit(solution)/shard_map/all_gather | solution.py:157
  352.7 11.1 %reduce-scatter.9.cloned.1.call-done = f32[2,200,768]{2,1,0:T(8,128)} async-done(((f32[4,200,768]{2,1,0:T(8,128)}), f32[2,200,768]{2,1,0:T(8,128)}) %reduce-scatter.9.cloned.1.call-update) | async-done | bytes 1228816 | tf_op jit(solution)/shard_map/reduce_scatter | solution.py:182
  387.0 10.2 %all-gather.17.cloned.1.call-done = bf16[4,200,768]{2,1,0:T(8,128)(2,1)} async-done(((bf16[2,200,768]{2,1,0:T(8,128)(2,1)}), bf16[4,200,768]{2,1,0:T(8,128)(2,1)}) %all-gather.17.cloned.1.call-update) | async-done | bytes 1228816 | tf_op jit(solution)/shard_map/all_gather | solution.py:259
  469.8 8.2 %fusion.1 = f32[732,6]{0,1:T(8,128)S(1)} fusion(s32[10000]{0:T(1024)S(1)} %copy-done.68, f32[6,40000]{1,0:T(8,128)S(1)} %reshape.279), kind=kOutput, calls=%fused_computation.2 | convolution fusion | flops 534360000 | bytes 382112 | tf_op jit(solution)/shard_map/hn,nr->rh/dot_general | solution.py:67
  478.0 8.4 %fusion.4 = f32[732,6]{0,1:T(8,128)S(1)} fusion(s32[10000]{0:T(1024)S(1)} %copy-done.70, f32[6,40000]{1,0:T(8,128)S(1)} %reshape.279), kind=kOutput, calls=%fused_computation.6 | convolution fusion | flops 534360000 | bytes 382112 | tf_op jit(solution)/shard_map/hn,nr->rh/dot_general | solution.py:67
  486.5 8.4 %fusion.7 = f32[732,6]{0,1:T(8,128)S(1)} fusion(s32[10000]{0:T(1024)S(1)} %copy-done.66, f32[6,40000]{1,0:T(8,128)S(1)} %reshape.279), kind=kOutput, calls=%fused_computation.10 | convolution fusion | flops 534360000 | bytes 382112 | tf_op jit(solution)/shard_map/hn,nr->rh/dot_general | solution.py:67
  500.6 8.2 %fusion = f32[732,6]{0,1:T(8,128)S(1)} fusion(s32[10000]{0:T(1024)S(1)} %copy-done.68, f32[6,40000]{1,0:T(8,128)S(1)} %reshape.280), kind=kOutput, calls=%fused_computation.1 | convolution fusion | flops 534360000 | bytes 382112 | tf_op jit(solution)/shard_map/hn,nr->rh/dot_general | solution.py:67
  508.8 8.6 %fusion.3 = f32[732,6]{0,1:T(8,128)S(1)} fusion(s32[10000]{0:T(1024)S(1)} %copy-done.70, f32[6,40000]{1,0:T(8,128)S(1)} %reshape.280), kind=kOutput, calls=%fused_computation.5 | convolution fusion | flops 534360000 | bytes 382112 | tf_op jit(solution)/shard_map/hn,nr->rh/dot_general | solution.py:67
  517.4 8.4 %fusion.6 = f32[732,6]{0,1:T(8,128)S(1)} fusion(s32[10000]{0:T(1024)S(1)} %copy-done.66, f32[6,40000]{1,0:T(8,128)S(1)} %reshape.280), kind=kOutput, calls=%fused_computation.9 | convolution fusion | flops 534360000 | bytes 382112 | tf_op jit(solution)/shard_map/hn,nr->rh/dot_general | solution.py:67
  525.8 8.2 %fusion.92 = f32[732,6]{0,1:T(8,128)S(1)} fusion(f32[732,6]{0,1:T(8,128)S(1)} %fusion, f32[732,6]{0,1:T(8,128)S(1)} %fusion.3, f32[732,6]{0,1:T(8,128)S(1)} %fusion.6, s32[10000]{0:T(1024)S(1)} %copy-done.64, f32[6,40000]{1,0:T(8,128)S(1)} %reshape.280), kind=kOutput, calls=%fused_computation.177 | convolution fusion | flops 534373184 | bytes 455840 | tf_op jit(solution)/shard_map/hn,nr->rh/dot_general | solution.py:67
  534.1 9.5 %fusion.89 = f32[732,6]{0,1:T(8,128)S(1)} fusion(f32[732,6]{0,1:T(8,128)S(1)} %fusion.92, f32[732,6]{0,1:T(8,128)S(1)} %fusion.1, f32[732,6]{0,1:T(8,128)S(1)} %fusion.4, f32[732,6]{0,1:T(8,128)S(1)} %fusion.7, s32[10000]{0:T(1024)S(1)} %copy-done.64, f32[6,40000]{1,0:T(8,128)} %copy-done.37), kind=kOutput, calls=%fused_computation.174 | convolution fusion | flops 534377568 | bytes 451424 | tf_op jit(solution)/shard_map/hn,nr->rh/dot_general | solution.py:67
  543.6 78.8 %all-reduce.3 = (f32[2,384]{1,0:T(2,128)}, f32[732,6]{0,1:T(8,128)}) all-reduce(f32[2,384]{1,0:T(2,128)S(1)} %maximum_add_fusion, f32[732,6]{0,1:T(8,128)S(1)} %fusion.89), channel_id=1, replica_groups=mesh['dp'=16,'head'=2] {'dp'}, use_global_device_ids=true, to_apply=%region_40.41 | all-reduce | flops 5160 | bytes 41280 | tf_op jit(solution)/shard_map/psum | solution.py:98
  629.6 39.0 %all-reduce.2 = (f32[768]{0:T(1024)}, f32[768]{0:T(1024)}, f32[768]{0:T(1024)}, f32[768]{0:T(1024)}, f32[768]{0:T(1024)}, /*index=5*/f32[768]{0:T(1024)}, f32[76...) all-reduce(f32[768]{0:T(1024)S(1)} %add.379, ...), channel_id=1, replica_groups=mesh['dp'=16,'head'=2] {'dp','head'}, use_global_device_ids=true, to_apply=%region_28.29 | all-reduce | flops 9984 | bytes 79872 | tf_op jit(solution)/shard_map/psum | solution.py:99
  672.6 65.8 %reduce-scatter.17.cloned.1.call-done = f32[96,768]{1,0:T(8,128)} async-done(((f32[3072,768]{1,0:T(8,128)}), f32[96,768]{1,0:T(8,128)}) %reduce-scatter.17.cloned.1.call-update) | async-done | bytes 294928 | tf_op jit(solution)/shard_map/reduce_scatter | solution.py:106
  (395 shorter events, 244.7 us)
Async XLA Ops:
  8.1 80.5 %all-gather.7.cloned.1.call-start = ((), (), s32[]{:S(2)}) async-start(), calls=%async_computation.6 | async-start | bytes 1843200 | tf_op jit(solution)/shard_map/all_gather | solution.py:157
  9.0 305.5 %copy-start.54 = (f32[2,200]{1,0:T(2,128)}, f32[2,200]{1,0:T(2,128)S(1)}, u32[]{:S(2)}) copy-start(f32[2,200]{1,0:T(2,128)S(1)} %get-tuple-element.94) | copy-start | bytes 4804
  9.8 304.7 %copy-start.56 = (f32[2,200]{1,0:T(2,128)}, f32[2,200]{1,0:T(2,128)S(1)}, u32[]{:S(2)}) copy-start(f32[2,200]{1,0:T(2,128)S(1)} %get-tuple-element.92) | copy-start | bytes 4804
  11.2 303.3 %copy-start.58 = (f32[2,200]{1,0:T(2,128)}, f32[2,200]{1,0:T(2,128)S(1)}, u32[]{:S(2)}) copy-start(f32[2,200]{1,0:T(2,128)S(1)} %broadcast_multiply_fusion.5) | copy-start | bytes 4804
  12.9 301.6 %copy-start.73 = (f32[2,200]{1,0:T(2,128)}, f32[2,200]{1,0:T(2,128)S(1)}, u32[]{:S(2)}) copy-start(f32[2,200]{1,0:T(2,128)S(1)} %fusion.121) | copy-start | bytes 4804
  14.8 142.5 %reduce-scatter.7.cloned.1.call-start = ((), (), s32[]{:S(2)}) async-start(), calls=%async_computation.7 | async-start | bytes 3686400 | tf_op jit(solution)/shard_map/reduce_scatter | solution.py:182
  112.5 70.2 %all-gather.9.cloned.1.call-start = ((), (), s32[]{:S(2)}) async-start(), calls=%async_computation.8 | async-start | bytes 4866048 | tf_op jit(solution)/shard_map/all_gather | solution.py:143
  113.1 134.6 %all-gather.11.cloned.1.call-start = ((), (), s32[]{:S(2)}) async-start(), calls=%async_computation.9 | async-start | bytes 4866048 | tf_op jit(solution)/shard_map/all_gather | solution.py:145
  113.7 155.4 %all-gather.15.cloned.1.call-start = ((), (), s32[]{:S(2)}) async-start(), calls=%async_computation.12 | async-start | bytes 1843200 | tf_op jit(solution)/shard_map/all_gather | solution.py:259
  261.4 50.5 %reduce-scatter.11.cloned.1.call-start = ((), (), s32[]{:S(2)}) async-start(), calls=%async_computation.13 | async-start | bytes 3686400 | tf_op jit(solution)/shard_map/reduce_scatter | solution.py:324
  300.6 28.0 %all-gather.13.cloned.1.call-start = ((), (), s32[]{:S(2)}) async-start(), calls=%async_computation.10 | async-start | bytes 1843200 | tf_op jit(solution)/shard_map/all_gather | solution.py:157
  317.9 45.9 %reduce-scatter.9.cloned.1.call-start = ((), (), s32[]{:S(2)}) async-start(), calls=%async_computation.11 | async-start | bytes 3686400 | tf_op jit(solution)/shard_map/reduce_scatter | solution.py:182
  352.4 44.8 %all-gather.17.cloned.1.call-start = ((), (), s32[]{:S(2)}) async-start(), calls=%async_computation.14 | async-start | bytes 1843200 | tf_op jit(solution)/shard_map/all_gather | solution.py:259
  386.5 235.9 %reduce-scatter.13.cloned.1.call-start = ((), (), s32[]{:S(2)}) async-start(), calls=%async_computation.15 | async-start | bytes 3686400 | tf_op jit(solution)/shard_map/reduce_scatter | solution.py:324
  428.5 244.0 %all-reduce.7.cloned.1.call-start = ((), (), s32[]{:S(2)}) async-start(), calls=%async_computation.18 | async-start | bytes 9437184 | tf_op jit(solution)/shard_map/psum | solution.py:98
  441.9 230.6 %reduce-scatter.15.cloned.1.call-start = ((), (), s32[]{:S(2)}) async-start(), calls=%async_computation.16 | async-start | bytes 9732096 | tf_op jit(solution)/shard_map/reduce_scatter | solution.py:104
  453.2 285.2 %reduce-scatter.17.cloned.1.call-start = ((), (), s32[]{:S(2)}) async-start(), calls=%async_computation.17 | async-start | bytes 9732096 | tf_op jit(solution)/shard_map/reduce_scatter | solution.py:106
  534.0 88.4 %copy-start.18 = (f32[2,200,768]{2,1,0:T(8,128)S(1)}, f32[2,200,768]{2,1,0:T(8,128)}, u32[]{:S(2)}) copy-start(f32[2,200,768]{2,1,0:T(8,128)} %reduce-scatter.11.cloned.1.call-done) | copy-start | bytes 3686404
  534.0 88.4 %copy-start.52 = (f32[768]{0:T(1024)S(1)}, f32[768]{0:T(1024)}, u32[]{:S(2)}) copy-start(f32[768]{0:T(1024)} %param.26) | copy-start | bytes 9220
  534.0 88.4 %copy-start.55 = (f32[2,200]{1,0:T(2,128)S(1)}, f32[2,200]{1,0:T(2,128)}, u32[]{:S(2)}) copy-start(f32[2,200]{1,0:T(2,128)} %copy-done.54) | copy-start | bytes 4804
  534.1 88.4 %copy-start.57 = (f32[2,200]{1,0:T(2,128)S(1)}, f32[2,200]{1,0:T(2,128)}, u32[]{:S(2)}) copy-start(f32[2,200]{1,0:T(2,128)} %copy-done.56) | copy-start | bytes 4804
  534.1 88.4 %copy-start.59 = (f32[2,200]{1,0:T(2,128)S(1)}, f32[2,200]{1,0:T(2,128)}, u32[]{:S(2)}) copy-start(f32[2,200]{1,0:T(2,128)} %copy-done.58) | copy-start | bytes 4804
  534.1 88.4 %copy-start.61 = (f32[2,200]{1,0:T(2,128)S(1)}, f32[2,200]{1,0:T(2,128)}, u32[]{:S(2)}) copy-start(f32[2,200]{1,0:T(2,128)} %copy-done.60) | copy-start | bytes 4804
  534.1 88.4 %copy-start.74 = (f32[2,200]{1,0:T(2,128)S(1)}, f32[2,200]{1,0:T(2,128)}, u32[]{:S(2)}) copy-start(f32[2,200]{1,0:T(2,128)} %copy-done.73) | copy-start | bytes 4804
  (99 other events, 885.4 us)
Sparse Core Ops, SparseCore 0:
  14.9 11.9 all-gather.6
  112.6 12.7 reduce-scatter.6
  261.6 7.5 all-gather.14
  300.7 11.1 reduce-scatter.10
  318.0 10.5 all-gather.12
  352.5 11.1 reduce-scatter.8
  386.7 10.5 all-gather.16
  428.7 11.1 reduce-scatter.12
  453.3 144.2 reduce-scatter.14
  604.0 134.3 reduce-scatter.16
Sparse Core Ops, SparseCore 1:
  115.9 66.8 all-gather.8
  185.5 62.1 all-gather.10
  442.0 200.4 all-reduce.6
where the time goes:
time: 763 us; the launch traced here: 752 us
  matrix products  252 us (33%)
  waiting for transfers between devices  197 us (26%)
  blocking collectives  161 us (21%)
  local copies, waits for them, and re-layouts  82.8 us (11%)
  other arithmetic  39 us (5%)
  between operations  17.7 us (2%)
    psum x1, blocking collectives, reduce_end(): summed_dp = lax.psum((g_qkv, g_qvb, g_table, g_proj), 'dp')  78.8 us
    dot_general x8, matrix products, table_grad(): jnp.einsum('hn,nr->rh', columns, selector, precision=highest, preferred_e...  67.8 us
    reduce_scatter x1, waiting for transfers between devices, reduce_end(): lax.psum_scatter(g_fc2, ('dp', 'head'), scatter_dimension=0, tiled=True)  65.8 us
    all_gather x1, waiting for transfers between devices, shards(): lax.all_gather(w_fc2, ('dp', 'head'), axis=0, tiled=True)  57.9 us
    dot_general x4, matrix products, table_bias(): jnp.einsum('rh,nr->hn', rel_table, selector, precision=highest, preferred...  56.8 us
    unnamed x1, blocking collectives  43.3 us
    psum x1, blocking collectives, reduce_end(): lax.psum((g_mask, g_ln1g, g_ln1b, g_projb, g_gamma1, g_ln2g, g_ln2b, g_fc...  39 us
    unnamed x228, local copies, waits for them, and re-layouts  27.3 us
  transfers between devices with their start and end apart: 13, of which 8 were waited for; matrix products, arithmetic and copies ran while one was open for 27% of the time, Pallas kernels for 0%

commit v1 on v0

v1 whole, which is shorter than its diff:
```python
import functools
import jax
import jax.numpy as jnp
from jax import lax
from jax.experimental import pallas as pl
from jax.experimental.pallas import tpu as pltpu
from jax.sharding import PartitionSpec as P

F32 = jnp.float32
BF16 = jnp.bfloat16
EPS = 1e-06
LANES = 128
V_MASK, V_G1, V_B1, V_PB, V_GA1, V_G2, V_B2, V_FB2, V_GA2, V_QB, V_VB = range(11)
S_GA2, S_FB2, S_LG2, S_LB2, S_GA1, S_PB = range(6)
T_MASK, T_LG1, T_LB1, T_QB, T_VB = range(5)


def dot(a, b):
    return jnp.dot(a, b, preferred_element_type=F32)


def dot_nt(a, b):
    return lax.dot_general(a, b, (((1,), (1,)), ((), ())), preferred_element_type=F32)


def dot_tn(a, b):
    return lax.dot_general(a, b, (((0,), (0,)), ((), ())), preferred_element_type=F32)


def norm_parts(v):
    c = v - jnp.mean(v, axis=-1, keepdims=True)
    r = lax.rsqrt(jnp.mean(c * c, axis=-1, keepdims=True) + EPS)
    return c * r, r


def norm_back(n, r, y, gain):
    yg = y * gain
    return r * (
        yg - jnp.mean(yg, axis=-1, keepdims=True) - n * jnp.mean(yg * n, axis=-1, keepdims=True)
    )


def low_half(shape):
    return lax.broadcasted_iota(jnp.int32, shape, 1) < (LANES // 2)


def attn_forward_kernel(
    x_ref, ch_ref, valid_ref, idx_ref, tab_ref, vec_ref, w_ref, wp_ref,
    normed_ref, q_ref, k_ref, v_ref, p_ref, att_ref, attn_ref, res_ref, n2_ref,
    bias_ref,
):
    images, rows, width = x_ref.shape
    rp = normed_ref.shape[0] // images
    keys = k_ref.shape[1]
    heads = bias_ref.shape[0]
    hw = width // heads
    scale = hw ** -0.5
    chunks = tab_ref.shape[1]

    def gather_head(h, carry):
        for half in range(keys // LANES):
            idx = idx_ref[:, half * LANES:(half + 1) * LANES]
            low = idx & (LANES - 1)
            high = idx >> 7
            acc = jnp.zeros(idx.shape, F32)
            for c in range(chunks):
                row = jnp.broadcast_to(tab_ref[h, c:c + 1, :], idx.shape)
                got = jnp.take_along_axis(row, low, axis=1)
                acc = jnp.where(high == c, got, acc)
            bias_ref[h, :, half * LANES:(half + 1) * LANES] = acc
        return carry

    lax.fori_loop(0, heads, gather_head, 0)

    normed_ref[...] = jnp.zeros_like(normed_ref)
    n2_ref[...] = jnp.zeros_like(n2_ref)
    res_ref[...] = jnp.zeros_like(res_ref)

    def hidden_of(i):
        ch = ch_ref[i]
        return x_ref[i].astype(F32) * (1.0 - ch) + ch * vec_ref[V_MASK:V_MASK + 1, :]

    def first_norm(i, carry):
        n, _ = norm_parts(hidden_of(i))
        out = n * vec_ref[V_G1:V_G1 + 1, :] + vec_ref[V_B1:V_B1 + 1, :]
        normed_ref[pl.ds(pl.multiple_of(i * rp, 16), rows), :] = out.astype(BF16)
        return carry

    lax.fori_loop(0, images, first_norm, 0)

    zeros_tail = jnp.zeros((images, keys - rp, width), BF16)
    k_ref[:, rp:, :] = zeros_tail
    v_ref[:, rp:, :] = zeros_tail
    for c, (dst, brow) in enumerate(((q_ref, V_QB), (k_ref, None), (v_ref, V_VB))):
        for nb in range(width // 256):
            cols = slice(nb * 256, (nb + 1) * 256)
            acc = dot(normed_ref[...], w_ref[c, :, cols])
            if brow is not None:
                acc = acc + vec_ref[brow:brow + 1, cols]
            acc = acc.astype(BF16)
            for i in range(images):
                dst[i, :rp, cols] = acc[i * rp:(i + 1) * rp]

    def attend(t, carry):
        i = t // (heads // 2)
        j = t % (heads // 2)
        lanes = pl.ds(pl.multiple_of(j * LANES, LANES), LANES)
        qp = q_ref[i, :, lanes]
        kp = k_ref[i, :, lanes]
        vp = v_ref[i, :, lanes]
        lo = low_half((rp, LANES))
        ok = valid_ref[i] > 0
        outs = []
        for s in range(2):
            qs = jnp.where(lo if s == 0 else jnp.logical_not(lo), qp, jnp.zeros_like(qp))
            sc = dot_nt(qs, kp) * scale + bias_ref[2 * j + s]
            sc = jnp.where(ok, sc, -1e30)
            e = jnp.exp(sc - jnp.max(sc, axis=-1, keepdims=True))
            prob = e * (1.0 / jnp.sum(e, axis=-1, keepdims=True))
            p_ref[i, 2 * j + s] = prob
            outs.append(dot(prob.astype(BF16), vp))
        att = jnp.where(lo, outs[0], outs[1]).astype(BF16)
        att_ref[pl.ds(pl.multiple_of(i * rp, 16), rp), lanes] = att
        return carry

    lax.fori_loop(0, images * (heads // 2), attend, 0)

    def finish(i, carry):
        at = pl.multiple_of(i * rp, 16)
        branch = dot(att_ref[pl.ds(at, rp), :], wp_ref[...]) + vec_ref[V_PB:V_PB + 1, :]
        attn_ref[pl.ds(at, rp), :] = branch
        res = hidden_of(i) + vec_ref[V_GA1:V_GA1 + 1, :] * branch[:rows]
        res_ref[pl.ds(at, rows), :] = res
        n, _ = norm_parts(res)
        out = n * vec_ref[V_G2:V_G2 + 1, :] + vec_ref[V_B2:V_B2 + 1, :]
        n2_ref[pl.ds(at, rows), :] = out.astype(BF16)
        return carry

    lax.fori_loop(0, images, finish, 0)


def vmem(n):
    return [pl.BlockSpec(memory_space=pltpu.VMEM)] * n


def attn_forward(x, ch, valid, idx, tab, vec, w, wp, heads):
    images, rows, width = x.shape
    rp, keys = idx.shape
    flat = images * rp
    sd = jax.ShapeDtypeStruct
    return pl.pallas_call(
        attn_forward_kernel,
        name="attn_forward",
        out_shape=(
            sd((flat, width), BF16), sd((images, rp, width), BF16), sd((images, keys, width), BF16),
            sd((images, keys, width), BF16), sd((images, heads, rp, keys), F32),
            sd((flat, width), BF16), sd((flat, width), F32), sd((flat, width), F32),
            sd((flat, width), BF16),
        ),
        in_specs=vmem(8), out_specs=vmem(9),
        scratch_shapes=[pltpu.VMEM((heads, rp, keys), F32)],
        compiler_params=pltpu.CompilerParams(vmem_limit_bytes=60 * 2**20),
    )(x, ch, valid, idx, tab, vec, w, wp)


def mlp_kernel(
    n2_ref, res_ref, attn_ref, cot_ref, vec_ref, b1_ref, w1_ref, w2_ref,
    g1_ref, g2_ref, gb1_ref, out_ref, dres_ref, dproj_ref, small_ref,
    db_ref, act_ref, dpre_ref, branch_ref, dn_ref,
):
    images, rows, width = cot_ref.shape
    flat = n2_ref.shape[0]
    rp = flat // images
    step = pl.program_id(0)
    steps = pl.num_programs(0)

    @pl.when(step == 0)
    def _():
        db_ref[...] = jnp.zeros_like(db_ref)
        branch_ref[...] = jnp.zeros_like(branch_ref)
        dn_ref[...] = jnp.zeros_like(dn_ref)

        def fill(i, carry):
            up = cot_ref[i].astype(F32) * vec_ref[V_GA2:V_GA2 + 1, :]
            db_ref[pl.ds(pl.multiple_of(i * rp, 16), rows), :] = up.astype(BF16)
            return carry

        lax.fori_loop(0, images, fill, 0)

    def tile(i, gb1):
        at = pl.ds(pl.multiple_of(i * rp, 16), rp)
        pre = dot_nt(n2_ref[at, :], w1_ref[...]) + b1_ref[...]
        cdf = 0.5 * (1.0 + lax.erf(pre * 0.7071067811865476))
        slope = cdf + pre * (0.3989422804014327 * jnp.exp(-0.5 * pre * pre))
        act = (pre * cdf).astype(BF16)
        act_ref[at, :] = act
        dpre = (dot_nt(db_ref[at, :], w2_ref[...]) * slope).astype(BF16)
        dpre_ref[at, :] = dpre
        branch_ref[at, :] += dot(act, w2_ref[...])
        dn_ref[at, :] += dot(dpre, w1_ref[...])
        return gb1 + jnp.sum(dpre.astype(F32), axis=0, keepdims=True)

    gb1_ref[...] = lax.fori_loop(0, images, tile, jnp.zeros(gb1_ref.shape, F32))
    g2_ref[...] = dot_tn(act_ref[...], db_ref[...]).astype(BF16)
    g1_ref[...] = dot_tn(dpre_ref[...], n2_ref[...]).astype(BF16)

    @pl.when(step == steps - 1)
    def _():
        dproj_ref[...] = jnp.zeros_like(dproj_ref)
        dres_ref[...] = jnp.zeros_like(dres_ref)
        small_ref[...] = jnp.zeros_like(small_ref)

        def add(row, value):
            small_ref[row:row + 1, :] += jnp.sum(value, axis=0, keepdims=True)

        def finish(i, carry):
            at = pl.multiple_of(i * rp, 16)
            here = pl.ds(at, rows)
            up = cot_ref[i].astype(F32)
            branch = branch_ref[here, :] + vec_ref[V_FB2:V_FB2 + 1, :]
            res = res_ref[here, :]
            out_ref[i] = (res + vec_ref[V_GA2:V_GA2 + 1, :] * branch).astype(BF16)
            add(S_GA2, up * branch)
            add(S_FB2, (up * vec_ref[V_GA2:V_GA2 + 1, :]).astype(BF16).astype(F32))
            n, r = norm_parts(res)
            dn = dn_ref[here, :]
            add(S_LG2, dn * n)
            add(S_LB2, dn)
            dres = up + norm_back(n, r, dn, vec_ref[V_G2:V_G2 + 1, :])
            dres_ref[here, :] = dres
            add(S_GA1, dres * attn_ref[here, :])
            dproj = (dres * vec_ref[V_GA1:V_GA1 + 1, :]).astype(BF16)
            dproj_ref[here, :] = dproj
            add(S_PB, dproj.astype(F32))
            return carry

        lax.fori_loop(0, images, finish, 0)


def mlp(n2, res, attn, cot, vec, b1, w1, w2, block):
    images, rows, width = cot.shape
    flat = n2.shape[0]
    ff = w1.shape[0]
    sd = jax.ShapeDtypeStruct
    whole = lambda a: pl.BlockSpec(a.shape, lambda s: (0,) * a.ndim, pipeline_mode=pl.Buffered(1))
    outs = (
        sd((ff, width), BF16), sd((ff, width), BF16), sd((1, ff), F32), sd(cot.shape, BF16),
        sd((flat, width), F32), sd((flat, width), BF16), sd((8, width), F32),
    )
    part = pl.BlockSpec((block, width), lambda s: (s, 0))
    return pl.pallas_call(
        mlp_kernel,
        name="mlp",
        grid=(ff // block,),
        out_shape=outs,
        in_specs=[whole(n2), whole(res), whole(attn), whole(cot), whole(vec),
                  pl.BlockSpec((1, block), lambda s: (0, s)), part, part],
        out_specs=[part, part, pl.BlockSpec((1, block), lambda s: (0, s)), whole(outs[3]),
                   whole(outs[4]), whole(outs[5]), whole(outs[6])],
        scratch_shapes=[
            pltpu.VMEM((flat, width), BF16), pltpu.VMEM((flat, block), BF16),
            pltpu.VMEM((flat, block), BF16), pltpu.VMEM((flat, width), F32),
            pltpu.VMEM((flat, width), F32),
        ],
        compiler_params=pltpu.CompilerParams(vmem_limit_bytes=60 * 2**20),
    )(n2, res, attn, cot, vec, b1, w1, w2)


def attn_backward_kernel(
    x_ref, ch_ref, idx_ref, vec_ref, w_ref, wp_ref, normed_ref, q_ref, k_ref, v_ref, p_ref,
    att_ref, dres_ref, dproj_ref,
    gx_ref, gw_ref, gt_ref, small_ref,
    dat_ref, dqkv_ref, ds_ref, nt_ref, dpt_ref,
):
    images, rows, width = x_ref.shape
    flat = normed_ref.shape[0]
    rp = flat // images
    keys = k_ref.shape[1]
    heads = ds_ref.shape[0]
    scale = (width // heads) ** -0.5
    j = pl.program_id(0)
    pairs = pl.num_programs(0)

    @pl.when(j == 0)
    def _():
        for i in range(images):
            at = slice(i * rp, (i + 1) * rp)
            dat_ref[at, :] = dot_nt(dproj_ref[at, :], wp_ref[...]).astype(BF16)
        nt_ref[...] = normed_ref[...].T
        dpt_ref[...] = dproj_ref[...].T
        small_ref[...] = jnp.zeros_like(small_ref)

    lanes = pl.ds(pl.multiple_of(j * LANES, LANES), LANES)
    ds_ref[2 * j] = jnp.zeros((rp, keys), F32)
    ds_ref[2 * j + 1] = jnp.zeros((rp, keys), F32)

    def image(i, carry):
        at = pl.ds(pl.multiple_of(i * rp, 16), rp)
        qp = q_ref[i, :, lanes]
        kp = k_ref[i, :, lanes]
        vp = v_ref[i, :, lanes]
        da = dat_ref[at, lanes]
        lo = low_half((rp, LANES))
        dv, dq, dk = [], [], []
        for s in range(2):
            das = jnp.where(lo if s == 0 else jnp.logical_not(lo), da, jnp.zeros_like(da))
            prob = p_ref[i, s]
            dp = dot_nt(das, vp)
            dsc = prob * (dp - jnp.sum(prob * dp, axis=-1, keepdims=True))
            dsb = dsc.astype(BF16)
            ds_ref[2 * j + s] += dsb.astype(F32)
            dv.append(dot_tn(prob.astype(BF16), da))
            dq.append(dot(dsb, kp))
            dk.append(dot_tn(dsb, qp))
        lok = low_half((keys, LANES))
        dqkv_ref[0, at, lanes] = (jnp.where(lo, dq[0], dq[1]) * scale).astype(BF16)
        dqkv_ref[1, at, lanes] = (jnp.where(lok, dk[0], dk[1]) * scale)[:rp].astype(BF16)
        dqkv_ref[2, at, lanes] = jnp.where(lok, dv[0], dv[1])[:rp].astype(BF16)
        return carry

    lax.fori_loop(0, images, image, 0)
    for c in range(3):
        gw_ref[0, c] = dot(nt_ref[...], dqkv_ref[c, :, lanes]).astype(BF16)
    gw_ref[0, 3] = dot(dpt_ref[...], att_ref[:, lanes]).astype(BF16)

    @pl.when(j == pairs - 1)
    def _():
        def column(row, c):
            def body(i, acc):
                part = dqkv_ref[c, pl.ds(pl.multiple_of(i * rp, 16), rp), :].astype(F32)
                return acc + jnp.sum(part, axis=0, keepdims=True)
            small_ref[row:row + 1, :] = lax.fori_loop(0, images, body, jnp.zeros((1, width), F32))

        column(T_QB, 0)
        column(T_VB, 2)

        def finish(i, carry):
            at = pl.multiple_of(i * rp, 16)
            here = pl.ds(at, rp)
            dn = dot_nt(dqkv_ref[0, here, :], w_ref[0])
            dn += dot_nt(dqkv_ref[1, here, :], w_ref[1])
            dn += dot_nt(dqkv_ref[2, here, :], w_ref[2])
            dn = dn[:rows]
            ch = ch_ref[i]
            hidden = x_ref[i].astype(F32) * (1.0 - ch) + ch * vec_ref[V_MASK:V_MASK + 1, :]
            n, r = norm_parts(hidden)
            dh = dres_ref[pl.ds(at, rows), :] + norm_back(n, r, dn, vec_ref[V_G1:V_G1 + 1, :])
            gx_ref[i] = dh * (1.0 - ch)
            for row, value in ((T_MASK, dh * ch), (T_LG1, dn * n), (T_LB1, dn)):
                small_ref[row:row + 1, :] += jnp.sum(value, axis=0, keepdims=True)
            return carry

        lax.fori_loop(0, images, finish, 0)

        a_iota = lax.broadcasted_iota(jnp.int32, (8, keys), 0)
        b_iota = lax.broadcasted_iota(jnp.int32, (LANES, keys), 0)

        def scatter(t, acc):
            idx = jnp.broadcast_to(idx_ref[pl.ds(t, 1), :], (8, keys))
            pick = (idx >> 7) == a_iota
            low = jnp.broadcast_to(idx_ref[pl.ds(t, 1), :] & (LANES - 1), (LANES, keys))
            one = (low == b_iota).astype(F32).astype(BF16)
            tiles = []
            for h in range(heads):
                row = jnp.broadcast_to(ds_ref[h, pl.ds(t, 1), :], (8, keys))
                tiles.append(jnp.where(pick, row, 0.0))
            left = jnp.concatenate(tiles, axis=0)
            high = left.astype(BF16)
            rest = (left - high.astype(F32)).astype(BF16)
            return acc + dot_nt(high, one) + dot_nt(rest, one)

        gt_ref[...] = lax.fori_loop(0, rows, scatter, jnp.zeros((heads * 8, LANES), F32))


def attn_backward(x, ch, idx, vec, w, wp, normed, q, k, v, p, att, dres, dproj, heads):
    images, rows, width = x.shape
    rp, keys = idx.shape
    flat = images * rp
    sd = jax.ShapeDtypeStruct
    whole = lambda a: pl.BlockSpec(a.shape, lambda s: (0,) * a.ndim, pipeline_mode=pl.Buffered(1))
    outs = (
        sd((images, rows, width), F32), sd((heads // 2, 4, width, LANES), BF16),
        sd((heads * 8, LANES), F32), sd((8, width), F32),
    )
    args = (x, ch, idx, vec, w, wp, normed, q, k, v)
    return pl.pallas_call(
        attn_backward_kernel,
        name="attn_backward",
        grid=(heads // 2,),
        out_shape=outs,
        in_specs=[whole(a) for a in args]
        + [pl.BlockSpec((images, 2, rp, keys), lambda s: (0, s, 0, 0)), whole(att), whole(dres), whole(dproj)],
        out_specs=[whole(outs[0]), pl.BlockSpec((1, 4, width, LANES), lambda s: (s, 0, 0, 0)),
                   whole(outs[2]), whole(outs[3])],
        scratch_shapes=[
            pltpu.VMEM((flat, width), BF16), pltpu.VMEM((3, flat, width), BF16),
            pltpu.VMEM((heads, rp, keys), F32), pltpu.VMEM((width, flat), BF16),
            pltpu.VMEM((width, flat), BF16),
        ],
        compiler_params=pltpu.CompilerParams(vmem_limit_bytes=60 * 2**20),
    )(*args, p, att, dres, dproj)


MESHID = pl.DeviceIdType.MESH


def here():
    dp = lax.axis_index("dp")
    head = lax.axis_index("head")
    return dp // 4, (dp // 2) % 2, dp % 2, head


def at_dp(z, y, x):
    return {"dp": (z * 2 + y) * 2 + x}


def partners(depth):
    z, y, x, head = here()
    found = [at_dp(z, y, 1 - x), at_dp(z, 1 - y, x), {"head": 1 - head}]
    for k in range(1, depth):
        found.append(at_dp((z + k) % depth, y, x))
    return found


def greet(depth):
    barrier = pltpu.get_barrier_semaphore()
    found = partners(depth)
    for dev in found:
        pl.semaphore_signal(barrier, inc=1, device_id=dev, device_id_type=MESHID)
    pl.semaphore_wait(barrier, len(found))


class Wire:
    def __init__(self, send, recv):
        self.send, self.recv, self.next, self.open = send, recv, 0, []

    def slot(self):
        self.next += 1
        return self.next - 1

    def start(self, i, src, dst, dev):
        copy = pltpu.make_async_remote_copy(
            src_ref=src, dst_ref=dst, send_sem=self.send.at[i], recv_sem=self.recv.at[i],
            device_id=dev, device_id_type=MESHID,
        )
        copy.start()
        self.open.append(copy)

    def arrived(self, i, ref, dev):
        pltpu.make_async_remote_copy(
            src_ref=ref, dst_ref=ref, send_sem=self.send.at[i], recv_sem=self.recv.at[i],
            device_id=dev, device_id_type=MESHID,
        ).wait_recv()

    def sent(self):
        for copy in self.open:
            copy.wait_send()
        self.open = []


def hops(p, y, x):
    ey, ex = (1 - y, x), (y, 1 - x)
    return (ey, ex) if p == 0 else (ex, ey)


def gather_stages(wire, depth, own, slot, column=None):
    z, y, x, head = here()
    ids = {}
    for p in range(2):
        for k in range(depth):
            for kind in "zabc":
                ids[p, kind, k] = wire.slot()
        if column is not None:
            for kind in range(4):
                ids[p, "s", kind] = wire.slot()
    zk = lambda k: (z + depth - k) % depth

    def start_square(p, k, src):
        (ay, ax), (by, bx) = hops(p, y, x)
        src = slot(p, zk(k), y, x) if src is None else src
        wire.start(ids[p, "a", k], src, slot(p, zk(k), y, x), at_dp(z, ay, ax))
        wire.start(ids[p, "b", k], src, slot(p, zk(k), y, x), at_dp(z, by, bx))

    def begin():
        for k in range(1, depth):
            for p in range(2):
                wire.start(ids[p, "z", k], own(p), slot(p, z, y, x), at_dp((z + k) % depth, y, x))
        for p in range(2):
            start_square(p, 0, own(p))

    def from_column(k):
        def run():
            for p in range(2):
                wire.arrived(ids[p, "z", k], slot(p, zk(k), y, x), at_dp(zk(k), y, x))
                start_square(p, k, None)
        return run

    def from_first(k):
        def run():
            for p in range(2):
                (ay, ax), (by, bx) = hops(p, y, x)
                wire.arrived(ids[p, "a", k], slot(p, zk(k), ay, ax), at_dp(z, ay, ax))
                wire.start(ids[p, "c", k], slot(p, zk(k), ay, ax), slot(p, zk(k), ay, ax), at_dp(z, by, bx))
        return run

    def from_second(kind):
        def run():
            for p in range(2):
                (ay, ax), (by, bx) = hops(p, y, x)
                cy, cx = (by, bx) if kind == "b" else (1 - y, 1 - x)
                for k in range(depth):
                    wire.arrived(ids[p, kind, k], slot(p, zk(k), cy, cx), at_dp(z, by, bx))
        return run

    def across(which):
        def run():
            for p in range(2):
                (ay, ax), (by, bx) = hops(p, y, x)
                cy, cx = ((y, x), (ay, ax), (by, bx), (1 - y, 1 - x))[which]
                block = column(p, cy, cx, head)
                wire.start(ids[p, "s", which], block, block, {"head": 1 - head})
        return run

    def crossed():
        for which in range(4):
            for p in range(2):
                (ay, ax), (by, bx) = hops(p, y, x)
                cy, cx = ((y, x), (ay, ax), (by, bx), (1 - y, 1 - x))[which]
                wire.arrived(ids[p, "s", which], column(p, cy, cx, 1 - head), {"head": 1 - head})

    stages = [begin]
    stages += [from_column(k) for k in range(1, depth)]
    if column is not None:
        stages.append(across(0))
    stages += [from_first(k) for k in range(depth)]
    if column is not None:
        stages.append(across(1))
    stages.append(from_second("b"))
    if column is not None:
        stages.append(across(2))
    stages.append(from_second("c"))
    if column is not None:
        stages.append(across(3))
        stages.append(crossed)
    return stages


def add_into(dst, src):
    total = dst[...].astype(F32) + src[...].astype(F32)
    dst[...] = total.astype(dst.dtype)


class ScatterSum:
    def __init__(self, wire, depth, theirs, pair_in, mine, square_in, line_in, column_in, store):
        self.__dict__.update(locals())
        self.ids = {}
        for p in range(2):
            for kind in ["h", "a", "b"] + list(range(1, depth)):
                self.ids[p, kind] = wire.slot()

    def pair(self):
        head = here()[3]
        for p in range(2):
            self.wire.start(self.ids[p, "h"], self.theirs(p), self.pair_in(p), {"head": 1 - head})

    def first(self):
        z, y, x, head = here()
        for p in range(2):
            self.wire.arrived(self.ids[p, "h"], self.pair_in(p), {"head": 1 - head})
            add_into(self.mine(p, None, None, None), self.pair_in(p))
            if p == 0:
                self.wire.start(self.ids[p, "a"], self.mine(p, None, None, 1 - x), self.square_in(p), at_dp(z, y, 1 - x))
            else:
                self.wire.start(self.ids[p, "a"], self.mine(p, None, 1 - y, None), self.square_in(p), at_dp(z, 1 - y, x))

    def second(self):
        z, y, x, head = here()
        for p in range(2):
            if p == 0:
                self.wire.arrived(self.ids[p, "a"], self.square_in(p), at_dp(z, y, 1 - x))
                add_into(self.mine(p, None, None, x), self.square_in(p))
                self.wire.start(self.ids[p, "b"], self.mine(p, None, 1 - y, x), self.line_in(p), at_dp(z, 1 - y, x))
            else:
                self.wire.arrived(self.ids[p, "a"], self.square_in(p), at_dp(z, 1 - y, x))
                add_into(self.mine(p, None, y, None), self.square_in(p))
                self.wire.start(self.ids[p, "b"], self.mine(p, None, y, 1 - x), self.line_in(p), at_dp(z, y, 1 - x))

    def third(self):
        z, y, x, head = here()
        for p in range(2):
            self.wire.arrived(self.ids[p, "b"], self.line_in(p), at_dp(z, 1 - y, x) if p == 0 else at_dp(z, y, 1 - x))
            add_into(self.mine(p, None, y, x), self.line_in(p))
            for k in range(1, self.depth):
                to = (z + k) % self.depth
                self.wire.start(self.ids[p, k], self.mine(p, to, y, x), self.column_in(p, k), at_dp(to, y, x))

    def last(self):
        z, y, x, head = here()
        for p in range(2):
            total = self.mine(p, z, y, x)[...].astype(F32)
            for k in range(1, self.depth):
                self.wire.arrived(self.ids[p, k], self.column_in(p, k), at_dp((z + self.depth - k) % self.depth, y, x))
                total = total + self.column_in(p, k)[...].astype(F32)
            self.store(p, total)


class SmallSum:
    def __init__(self, wire, depth, bufs, line):
        self.wire, self.depth, self.bufs, self.line = wire, depth, bufs, line
        self.ids = [wire.slot() for _ in range(3 + depth)]

    def devices(self):
        z, y, x, head = here()
        return [{"head": 1 - head}, at_dp(z, y, 1 - x), at_dp(z, 1 - y, x)]

    def send(self, n):
        self.wire.start(self.ids[n], self.bufs.at[2 * n], self.bufs.at[2 * n + 1], self.devices()[n])

    def take(self, n):
        self.wire.arrived(self.ids[n], self.bufs.at[2 * n + 1], self.devices()[n])
        self.bufs[2 * n + 2] = self.bufs[2 * n] + self.bufs[2 * n + 1]

    def stages(self):
        def begin():
            self.send(0)

        def middle(n):
            def run():
                self.take(n - 1)
                self.send(n)
            return run

        def column():
            z, y, x, head = here()
            self.take(2)
            self.line[z] = self.bufs[6]
            for k in range(1, self.depth):
                self.wire.start(self.ids[2 + k], self.bufs.at[6], self.line.at[z], at_dp((z + k) % self.depth, y, x))

        return [begin, middle(1), middle(2), column]

    def result(self):
        z, y, x, head = here()
        for k in range(1, self.depth):
            back = (z + self.depth - k) % self.depth
            self.wire.arrived(self.ids[2 + k], self.line.at[back], at_dp(back, y, x))
        total = self.line[0]
        for n in range(1, self.depth):
            total = total + self.line[n]
        return total


def ag_kernel(own_ref, bias_ref, b1_ref, b2_ref, bsum_ref, bufs, line, send, recv, lsem):
    depth = b1_ref.shape[0]
    z, y, x, head = here()
    full = (b1_ref, b2_ref)
    own = lambda p: own_ref.at[p]
    slot = lambda p, zz, yy, xx: full[p].at[zz, yy, xx, head]
    column = lambda p, yy, xx, hd: full[p].at[:, yy, xx, hd]
    greet(depth)
    local = [pltpu.make_async_copy(own(p), slot(p, z, y, x), lsem.at[p]) for p in range(2)]
    for c in local:
        c.start()
    wire = Wire(send, recv)
    bufs[0] = bias_ref[...]
    small = SmallSum(wire, depth, bufs, line)
    stages = gather_stages(wire, depth, own, slot, column)
    extra = small.stages()
    for n, s in enumerate(stages):
        if n == 1:
            for c in local:
                c.wait()
        s()
        if n < len(extra):
            extra[n]()
    bsum_ref[...] = small.result()
    wire.sent()


def ag(own, bias, depth, heads):
    shape = jax.ShapeDtypeStruct((depth, 2, 2, heads) + own.shape[1:], own.dtype)
    any_ = pl.BlockSpec(memory_space=pl.ANY)
    n = 2 * (4 * depth + 4) + 3 + depth
    return pl.pallas_call(
        ag_kernel, name="gather_ff", out_shape=(shape, shape, jax.ShapeDtypeStruct(bias.shape, F32)),
        in_specs=[any_] + vmem(1), out_specs=[any_, any_] + vmem(1),
        scratch_shapes=[pltpu.VMEM((7,) + bias.shape, F32), pltpu.VMEM((depth,) + bias.shape, F32), pltpu.SemaphoreType.DMA((n,)), pltpu.SemaphoreType.DMA((n,)), pltpu.SemaphoreType.DMA((2,))],
        compiler_params=pltpu.CompilerParams(collective_id=1, has_side_effects=True),
    )(own, bias)


def rs_kernel(chunk, g1_ref, g2_ref, o_ref, mine, pair_in, square_in, line_in, column_in, send, recv, lsem):
    depth = g1_ref.shape[0]
    z, y, x, head = here()
    gs = (g1_ref, g2_ref)
    greet(depth)
    local = [pltpu.make_async_copy(gs[p].at[:, :, :, head], mine.at[p], lsem.at[p]) for p in range(2)]
    for c in local:
        c.start()
    wire = Wire(send, recv)
    every = lambda v: slice(None) if v is None else v
    sums = []
    for r in range(mine.shape[4] // chunk):
        rows = pl.ds(r * chunk, chunk)

        def store(p, total, rows=rows):
            o_ref[p, rows, :] = total
        sums.append(ScatterSum(
            wire, depth,
            theirs=lambda p, rows=rows: gs[p].at[:, :, :, 1 - head, rows],
            pair_in=lambda p, rows=rows: pair_in.at[p, :, :, :, rows],
            mine=lambda p, zz, yy, xx, rows=rows: mine.at[p, every(zz), every(yy), every(xx), rows],
            square_in=lambda p, r=r: square_in.at[p, r],
            line_in=lambda p, r=r: line_in.at[p, r],
            column_in=lambda p, k, r=r: column_in.at[p, r, k - 1],
            store=store,
        ))
    for s in sums:
        s.pair()
    for c in local:
        c.wait()
    for name in ("first", "second", "third", "last"):
        for s in sums:
            getattr(s, name)()
    wire.sent()


def rs(g1, g2, chunk):
    depth, heads, rows, width = g1.shape[0], g1.shape[3], g1.shape[4], g1.shape[5]
    pieces = rows // chunk
    any_ = pl.BlockSpec(memory_space=pl.ANY)
    n = 2 * pieces * (2 + depth)
    return pl.pallas_call(
        functools.partial(rs_kernel, chunk), name="scatter_ff",
        out_shape=jax.ShapeDtypeStruct((2, rows, width), F32),
        in_specs=[any_, any_], out_specs=pl.BlockSpec(memory_space=pltpu.VMEM),
        scratch_shapes=[
            pltpu.VMEM((2, depth, 2, 2, rows, width), BF16), pltpu.VMEM((2, depth, 2, 2, rows, width), BF16),
            pltpu.VMEM((2, pieces, depth, 2, chunk, width), BF16), pltpu.VMEM((2, pieces, depth, chunk, width), BF16),
            pltpu.VMEM((2, pieces, depth - 1, chunk, width), BF16),
            pltpu.SemaphoreType.DMA((n,)), pltpu.SemaphoreType.DMA((n,)), pltpu.SemaphoreType.DMA((2,))],
        compiler_params=pltpu.CompilerParams(collective_id=2, has_side_effects=True, vmem_limit_bytes=50 * 2**20),
    )(g1, g2)


def ar_kernel(g_ref, small_ref, full_ref, sum_ref, mine, pair_in, square_in, line_in, column_in, bufs, line, send, recv, lsem):
    pieces, depth = mine.shape[0], mine.shape[3]
    z, y, x, head = here()
    greet(depth)
    local = [pltpu.make_async_copy(g_ref.at[head, m], mine.at[m], lsem.at[m]) for m in range(pieces)]
    for c in local:
        c.start()
    wire = Wire(send, recv)
    every = lambda v: slice(None) if v is None else v
    bufs[0] = small_ref[...]
    small = SmallSum(wire, depth, bufs, line)
    sums = []
    for m in range(pieces):
        def store(p, total, m=m):
            full_ref[m, p, :, z, y, x] = total.astype(BF16)
        sums.append(ScatterSum(
            wire, depth,
            theirs=lambda p, m=m: g_ref.at[1 - head, m, p],
            pair_in=lambda p, m=m: pair_in.at[m, p],
            mine=lambda p, zz, yy, xx, m=m: mine.at[m, p, :, every(zz), every(yy), every(xx)],
            square_in=lambda p, m=m: square_in.at[p, m],
            line_in=lambda p, m=m: line_in.at[p, m],
            column_in=lambda p, k, m=m: column_in.at[p, m, k - 1],
            store=store,
        ))
    extra = small.stages()
    for s in sums:
        s.pair()
    for c in local:
        c.wait()
    for n, name in enumerate(("first", "second", "third", "last")):
        extra[n]()
        for s in sums:
            getattr(s, name)()
    stages = gather_stages(
        wire, depth,
        own=lambda p: full_ref.at[:, p, :, z, y, x],
        slot=lambda p, zz, yy, xx: full_ref.at[:, p, :, zz, yy, xx],
    )
    for s in stages:
        s()
    sum_ref[...] = small.result()
    wire.sent()


def ar(g, small, depth):
    pieces, (rows, lanes) = g.shape[1], g.shape[-2:]
    any_ = pl.BlockSpec(memory_space=pl.ANY)
    n = 2 * pieces * (2 + depth) + 2 * 4 * depth + 3 + depth
    one = (pieces, 2, 2, depth, 2, 2, rows, lanes)
    return pl.pallas_call(
        ar_kernel, name="sum_weights",
        out_shape=(jax.ShapeDtypeStruct(one, BF16), jax.ShapeDtypeStruct(small.shape, F32)),
        in_specs=[any_] + vmem(1), out_specs=vmem(2),
        scratch_shapes=[
            pltpu.VMEM(one, BF16), pltpu.VMEM(one, BF16),
            pltpu.VMEM((2, pieces, 2, depth, 2, rows, lanes), BF16), pltpu.VMEM((2, pieces, 2, depth, rows, lanes), BF16),
            pltpu.VMEM((2, pieces, depth - 1, 2, rows, lanes), BF16),
            pltpu.VMEM((7,) + small.shape, F32), pltpu.VMEM((depth,) + small.shape, F32),
            pltpu.SemaphoreType.DMA((n,)), pltpu.SemaphoreType.DMA((n,)), pltpu.SemaphoreType.DMA((pieces,))],
        compiler_params=pltpu.CompilerParams(collective_id=3, has_side_effects=True, vmem_limit_bytes=50 * 2**20),
    )(g, small)


def pack(rows, count):
    width = rows[0].shape[0]
    return jnp.concatenate([jnp.stack(rows), jnp.zeros((count - len(rows), width), F32)])


def shards(
    inputs, masked, key_valid, rel_index, mask_token, ln1_gain, ln1_bias, w_qkv, qv_bias, rel_table,
    w_proj, proj_bias, gamma1, ln2_gain, ln2_bias, w_fc1, fc1_bias, w_fc2, fc2_bias, gamma2, cotangent,
):
    images, rows, width = inputs.shape
    dp, hn = lax.axis_size("dp"), lax.axis_size("head")
    me, head = lax.axis_index("dp"), lax.axis_index("head")
    depth = dp // 4
    share = w_fc2.shape[0]
    ff = share * dp * hn
    entries, heads = rel_table.shape[0], rel_table.shape[1] * hn
    rp, keys = -(-rows // 16) * 16, -(-rows // LANES) * LANES
    direct = hn == 2 and dp == 16 and share % 32 == 0 and width % (16 * dp) == 0

    w = lax.all_gather(jnp.transpose(w_qkv, (1, 0, 2)), "head", axis=2, tiled=True)
    wp = lax.all_gather(w_proj, "head", axis=0, tiled=True)
    tab_rows = -(-entries // LANES)
    tab = jnp.pad(rel_table.T, ((0, 0), (0, tab_rows * LANES - entries)))
    mixed = jnp.concatenate([tab.reshape(-1), qv_bias.reshape(-1)])
    mixed = lax.all_gather(mixed, "head", axis=0)
    cut = tab.size
    tab = mixed[:, :cut].reshape(heads, tab_rows, LANES)
    qvb = jnp.transpose(mixed[:, cut:].reshape(hn, 2, width // hn), (1, 0, 2)).reshape(2, width)
    vec = pack([mask_token, ln1_gain, ln1_bias, proj_bias, gamma1, ln2_gain, ln2_bias, fc2_bias, gamma2, qvb[0], qvb[1]], 16)
    ch = masked.astype(F32)[..., None]
    valid = lax.dynamic_slice_in_dim(key_valid, head * images, images, 0)
    valid = jnp.pad(valid, ((0, 0), (0, keys - rows)))[:, None, :]
    idx = jnp.pad(rel_index, ((0, rp - rows), (0, keys - rows)))

    if direct:
        own = jnp.stack([w_fc1.T, w_fc2])
        spot = jnp.zeros((ff,), F32)
        spot = lax.dynamic_update_slice(spot, fc1_bias.astype(F32), ((me * hn + head) * share,))
        w1, w2, b1 = ag(own, spot.reshape(8, ff // 8), depth, hn)
        w1, w2, b1 = w1.reshape(ff, width), w2.reshape(ff, width), b1.reshape(1, ff)
    else:
        w1 = lax.all_gather(w_fc1.T, ("dp", "head"), axis=0, tiled=True)
        w2 = lax.all_gather(w_fc2, ("dp", "head"), axis=0, tiled=True)
        b1 = lax.all_gather(fc1_bias, ("dp", "head"), axis=0, tiled=True).astype(F32)[None]

    normed, q, k, v, p, att, attn, res, n2 = attn_forward(inputs, ch, valid, idx, tab, vec, w, wp, heads)
    block = ff // 4
    g1, g2, gb1, out, dres, dproj, small2 = mlp(n2, res, attn, cotangent, vec, b1, w1, w2, block)
    gx, gw, gt, small1 = attn_backward(inputs, ch, idx, vec, w, wp, normed, q, k, v, p, att, dres, dproj, heads)

    small = jnp.concatenate([small1, small2, gt.reshape(-1, width), gb1.reshape(-1, width)])
    if direct:
        cut_ff = (depth, 2, 2, hn, share, width)
        gff = rs(g1.reshape(cut_ff), g2.reshape(cut_ff), 32)
        g_fc1, g_fc2 = gff[0], gff[1]
        per = heads // 2 // hn
        full, small = ar(gw.reshape(hn, per, 2, 2, depth, 2, 2, width // dp, LANES), small, depth)
        full = full.reshape(per, 4, width, LANES).astype(F32)
    else:
        g_fc1 = lax.psum_scatter(g1.astype(F32), ("dp", "head"), scatter_dimension=0, tiled=True)
        g_fc2 = lax.psum_scatter(g2.astype(F32), ("dp", "head"), scatter_dimension=0, tiled=True)
        full = lax.psum(lax.psum_scatter(gw.astype(F32), "head", scatter_dimension=0, tiled=True), "dp")
        small = lax.psum(small, ("dp", "head"))
    g_qkv = jnp.transpose(full[:, :3], (2, 1, 0, 3)).reshape(width, 3, -1)
    g_proj = jnp.transpose(full[:, 3], (0, 2, 1)).reshape(-1, width)
    s1, s2 = small[:8], small[8:16]
    tables = small[16:16 + gt.size // width].reshape(hn, heads // hn, -1)
    g_table = lax.dynamic_index_in_dim(tables, head, 0, keepdims=False)[:, :entries].T
    g_b1 = lax.dynamic_slice_in_dim(small[16 + gt.size // width:].reshape(-1), (me * hn + head) * share, share)
    g_qvb = lax.dynamic_slice_in_dim(s1[T_QB:T_VB + 1], head * (width // hn), width // hn, 1)
    return (
        out, gx, s1[T_MASK], s1[T_LG1], s1[T_LB1], g_qkv, g_qvb, g_table, g_proj, s2[S_PB], s2[S_GA1],
        s2[S_LG2], s2[S_LB2], g_fc1.T, g_b1, g_fc2, s2[S_FB2], s2[S_GA2],
    )


def solution(mesh):
    in_specs = (
        P(("dp", "head"), None, None),
        P(("dp", "head"), None),
        P("dp", None),
        P(),
        P(),
        P(),
        P(),
        P(None, None, "head"),
        P(None, "head"),
        P(None, "head"),
        P("head", None),
        P(),
        P(),
        P(),
        P(),
        P(None, ("dp", "head")),
        P(("dp", "head")),
        P(("dp", "head"), None),
        P(),
        P(),
        P(("dp", "head"), None, None),
    )
    out_specs = (
        P(("dp", "head"), None, None),
        P(("dp", "head"), None, None),
        P(),
        P(),
        P(),
        P(None, None, "head"),
        P(None, "head"),
        P(None, "head"),
        P("head", None),
        P(),
        P(),
        P(),
        P(),
        P(None, ("dp", "head")),
        P(("dp", "head")),
        P(("dp", "head"), None),
        P(),
        P(),
    )
    return jax.shard_map(shards, mesh=mesh, in_specs=in_specs, out_specs=out_specs, check_vma=False)
```

time: 763 us -> 427 us (0.56); the launches traced: 752 us -> 427 us
  Pallas kernels: 0 us -> 380 us
  matrix products: 252 us -> 0 us
  waiting for transfers between devices: 197 us -> 1.38 us
  blocking collectives: 161 us -> 1.95 us
  local copies, waits for them, and re-layouts: 82.8 us -> 24.1 us
  other arithmetic: 39 us -> 4.82 us
    pallas_call x0 -> x6, Pallas kernels: none -> 380 us  [the longest x1 84.1 us: attn_backward(): pl.pallas_call(attn_backward_kernel, name='attn_backward', grid=(heads //...]
    dot_general x48 -> x0, matrix products: 252 us -> none  [the longest x8 67.8 us: table_grad(): jnp.einsum('hn,nr->rh', columns, selector, precision=highest, preferred_e...]
    psum x2 -> x0, blocking collectives: 118 us -> none  [the longest x1 78.8 us: reduce_end(): summed_dp = lax.psum((g_qkv, g_qvb, g_table, g_proj), 'dp')]
    all_gather x6 -> x2, waiting for transfers between devices: 108 us -> 0.01 us  [the longest x1 0.01 us: shards(): wp = lax.all_gather(w_proj, 'head', axis=0, tiled=True)]
    reduce_scatter x6 -> x0, waiting for transfers between devices: 88.2 us -> none  [the longest x1 65.8 us: reduce_end(): lax.psum_scatter(g_fc2, ('dp', 'head'), scatter_dimension=0, tiled=True)]
    unnamed x1 -> x0, blocking collectives: 43.3 us -> none
    reduce_sum x19 -> x0, other arithmetic: 28.4 us -> none  [the longest x5 10.1 us: layer_norm(): return center * lax.rsqrt(spread + epsilon) * scale_vec + offset_vec]
    slice x12 -> x7, local copies, waits for them, and re-layouts: 21.2 us -> 2.17 us  [the longest x1 0.66 us: shards(): s2[S_GA2]]
  transfers between devices with their start and end apart: 13 -> 2, of which waited for: 8 -> 0; matrix products, arithmetic and copies ran while one was open for 27% -> 2% of each run, Pallas kernels for 0% -> 13%
where the time goes in v1:
time: 427 us
  Pallas kernels  380 us (89%)
  local copies, waits for them, and re-layouts  24.1 us (6%)
  between operations  14.5 us (3%)
  other arithmetic  4.82 us (1%)
    pallas_call x1, Pallas kernels, attn_backward(): pl.pallas_call(attn_backward_kernel, name='attn_backward', grid=(heads //...  84.1 us
    pallas_call x1, Pallas kernels, ar(): pl.pallas_call(ar_kernel, name='sum_weights', out_shape=(jax.ShapeDtypeSt...  77.1 us
    pallas_call x1, Pallas kernels, rs(): pl.pallas_call(functools.partial(rs_kernel, chunk), name='scatter_ff', ou...  67.7 us
    pallas_call x1, Pallas kernels, ag(): pl.pallas_call(ag_kernel, name='gather_ff', out_shape=(shape, shape, jax....  55.5 us
    pallas_call x1, Pallas kernels, attn_forward(): pl.pallas_call(attn_forward_kernel, name='attn_forward', out_shape=(sd((f...  50.3 us
    pallas_call x1, Pallas kernels, mlp(): pl.pallas_call(mlp_kernel, name='mlp', grid=(ff // block,), out_shape=out...  45.2 us
    unnamed x50, local copies, waits for them, and re-layouts  9.63 us
  transfers between devices with their start and end apart: 2, of which 0 were waited for; matrix products, arithmetic and copies ran while one was open for 2% of the time, Pallas kernels for 13%

profile of v1, /device:TPU:0, one launch (start us, length us, event | category | flops | bytes accessed | tf_op | source)
XLA Modules:
  0.0 426.8 jit_solution(12116472316395146218)
XLA Ops:
  7.4 0.7 all-gather.7.cloned.1.call-update
  8.1 0.7 all-gather.5.cloned.1.call-update
  8.9 0.7 pad.14
  9.7 1.9 all-gather.1
  12.5 1.0 copy.47.ch_ref
  14.1 0.7 pad.13.idx_ref
  15.5 0.7 pad_maximum_fusion.own_ref
  16.3 55.5 %gather_ff.1 = (bf16[4,2,2,2,96,768]{5,4,3,2,1,0:T(8,128)(2,1)}, bf16[4,2,2,2,96,768]{5,4,3,2,1,0:T(8,128)(2,1)}, f32[8,384]{1,0:T(8,128)}) custom-call(bf16[2,96,768]{2,1,0:T(8,128)(2,1)} %pad_maximum_fusion.own_ref, f32[8,384]{1,0:T(8,128)} %reshape.97.bias_ref), custom_call_target="tpu_custom_call" | custom-call | tf_op jit(solution)/shard_map/gather_ff/pallas_call | solution.py:684
  71.8 1.3 copy.56
  73.1 1.3 concatenate.10.vec_ref
  74.4 50.3 %attn_forward.1 = (bf16[832,768]{1,0:T(8,128)(2,1)}, bf16[4,208,768]{2,1,0:T(8,128)(2,1)}, bf16[4,256,768]{2,1,0:T(8,128)(2,1)}, bf16[4,256,768]{2,1,0:T(8,128)(...) custom-call(bf16[4,200,768]{2,1,0:T(8,128)(2,1)} %x_ref.3, ...), custom_call_target="tpu_custom_call" | custom-call | tf_op jit(solution)/shard_map/attn_forward/pallas_call | solution.py:151
  124.8 45.2 %mlp.1 = (bf16[3072,768]{1,0:T(8,128)(2,1)}, bf16[3072,768]{1,0:T(8,128)(2,1)}, f32[1,3072]{1,0:T(1,128)}, bf16[4,200,768]{2,1,0:T(8,128)(2,1)}, f32[832,768]{1,...) custom-call(bf16[832,768]{1,0:T(8,128)(2,1)} %get-tuple-element.43.n2_ref, f32[832,768]{1,0:T(8,128)} %get-tuple-element.44.res_ref, ...), custom_call_target="tpu_custom_call" | custom-call | tf_op jit(solution)/shard_map/mlp/pallas_call | solution.py:251
  170.0 84.1 %attn_backward.1 = (f32[4,200,768]{2,1,0:T(8,128)}, bf16[6,4,768,128]{3,2,1,0:T(8,128)(2,1)}, f32[96,128]{1,0:T(8,128)}, f32[8,768]{1,0:T(8,128)}) custom-call(bf16[4,200,768]{2,1,0:T(8,128)(2,1)} %x_ref.3, f32[4,200,1]{2,1,0:T(8,128)} %copy.47.ch_ref, s32[208,256]{1,0:T(8,128)} %pad.13.idx_ref, f32[16,768]{1,0:T(8,128)} %concatenate.10.vec_ref, ...), custom_call_target="tpu_custom_call" | custom-call | tf_op jit(solution)/shard_map/attn_backward/pallas_call | solution.py:386
  254.1 0.8 reshape.102
  255.4 0.7 reduce.21
  256.1 0.7 pad_maximum_fusion.1.small_ref
  256.9 77.1 %sum_weights.1 = (bf16[3,2,2,4,2,2,48,128]{7,6,5,4,3,2,1,0:T(8,128)(2,1)S(1)}, f32[36,768]{1,0:T(8,128)S(1)}) custom-call(bf16[2,3,2,2,4,2,2,48,128]{8,7,6,5,4,3,2,1,0:T(8,128)(2,1)} %bitcast.53, f32[36,768]{1,0:T(8,128)S(1)} %pad_maximum_fusion.1.small_ref), custom_call_target="tpu_custom_call" | custom-call | tf_op jit(solution)/shard_map/sum_weights/pallas_call | solution.py:796
  334.2 2.6 convert.1
  338.7 67.7 %scatter_ff.1 = f32[2,96,768]{2,1,0:T(8,128)S(1)} custom-call(bf16[4,2,2,2,96,768]{5,4,3,2,1,0:T(8,128)(2,1)} %bitcast.51, bf16[4,2,2,2,96,768]{5,4,3,2,1,0:T(8,128)(2,1)} %bitcast.52), custom_call_target="tpu_custom_call" | custom-call | tf_op jit(solution)/shard_map/scatter_ff/pallas_call | solution.py:733
  406.4 0.8 slice_bitcast_fusion.1
  407.2 3.0 copy.53
  410.2 5.2 %copy.51 = f32[768,3,384]{2,0,1:T(8,128)} copy(f32[768,3,384]{0,2,1:T(8,128)} %bitcast.50) | data formatting | bytes 7077888
  415.4 1.4 slice_bitcast_fusion
  416.7 1.4 copy.50
  (87 shorter events, 6.8 us)
Async XLA Ops:
  7.2 4.5 %copy-start = (s32[8,200]{1,0:T(8,128)S(1)}, s32[8,200]{1,0:T(8,128)}, u32[]{:S(2)}) copy-start(s32[8,200]{1,0:T(8,128)} %param.23) | copy-start | bytes 19204
  7.2 2.4 copy-start.19
  7.2 5.1 %copy-start.9 = (f32[768]{0:T(1024)S(1)}, f32[768]{0:T(1024)}, u32[]{:S(2)}) copy-start(f32[768]{0:T(1024)} %param.25) | copy-start | bytes 9220
  7.2 5.1 %copy-start.10 = (f32[768]{0:T(1024)S(1)}, f32[768]{0:T(1024)}, u32[]{:S(2)}) copy-start(f32[768]{0:T(1024)} %param.26) | copy-start | bytes 9220
  7.2 5.1 %copy-start.11 = (f32[768]{0:T(1024)S(1)}, f32[768]{0:T(1024)}, u32[]{:S(2)}) copy-start(f32[768]{0:T(1024)} %param.27) | copy-start | bytes 9220
  7.3 5.1 %copy-start.12 = (f32[768]{0:T(1024)S(1)}, f32[768]{0:T(1024)}, u32[]{:S(2)}) copy-start(f32[768]{0:T(1024)} %param.32) | copy-start | bytes 9220
  7.3 5.1 %copy-start.13 = (f32[768]{0:T(1024)S(1)}, f32[768]{0:T(1024)}, u32[]{:S(2)}) copy-start(f32[768]{0:T(1024)} %param.33) | copy-start | bytes 9220
  7.3 5.1 %copy-start.14 = (f32[768]{0:T(1024)S(1)}, f32[768]{0:T(1024)}, u32[]{:S(2)}) copy-start(f32[768]{0:T(1024)} %param.34) | copy-start | bytes 9220
  7.3 5.2 %copy-start.15 = (f32[768]{0:T(1024)S(1)}, f32[768]{0:T(1024)}, u32[]{:S(2)}) copy-start(f32[768]{0:T(1024)} %param.35) | copy-start | bytes 9220
  7.3 5.2 %copy-start.16 = (f32[768]{0:T(1024)S(1)}, f32[768]{0:T(1024)}, u32[]{:S(2)}) copy-start(f32[768]{0:T(1024)} %param.39) | copy-start | bytes 9220
  7.3 5.2 %copy-start.17 = (f32[768]{0:T(1024)S(1)}, f32[768]{0:T(1024)}, u32[]{:S(2)}) copy-start(f32[768]{0:T(1024)} %param.40) | copy-start | bytes 9220
  7.3 5.2 %copy-start.18 = (s32[4,200]{1,0:T(4,128)S(1)}, s32[4,200]{1,0:T(4,128)}, u32[]{:S(2)}) copy-start(s32[4,200]{1,0:T(4,128)} %param.22) | copy-start | bytes 9604
  7.3 6.8 %copy-start.2 = (s32[200,200]{1,0:T(8,128)S(1)}, s32[200,200]{1,0:T(8,128)}, u32[]{:S(2)}) copy-start(s32[200,200]{1,0:T(8,128)} %param.24) | copy-start | bytes 480004
  7.3 7.5 %copy-start.20 = (bf16[96]{0:T(256)(128)(2,1)S(1)}, bf16[96]{0:T(256)(128)(2,1)}, u32[]{:S(2)}) copy-start(bf16[96]{0:T(256)(128)(2,1)} %param.37) | copy-start | bytes 580
  7.3 8.2 %copy-start.5 = (bf16[768,96]{0,1:T(8,128)(2,1)S(1)}, bf16[768,96]{0,1:T(8,128)(2,1)}, u32[]{:S(2)}) copy-start(bf16[768,96]{0,1:T(8,128)(2,1)} %param.36) | copy-start | bytes 442372
  7.4 8.2 %copy-start.4 = (bf16[96,768]{1,0:T(8,128)(2,1)S(1)}, bf16[96,768]{1,0:T(8,128)(2,1)}, u32[]{:S(2)}) copy-start(bf16[96,768]{1,0:T(8,128)(2,1)} %param.38) | copy-start | bytes 442372
  7.4 67.0 %all-gather.7.cloned.1.call-start = ((), (), s32[]{:S(2)}) async-start(), calls=%async_computation.1 | async-start | bytes 1769472 | tf_op jit(solution)/shard_map/all_gather | solution.py:830
  8.1 66.3 %all-gather.5.cloned.1.call-start = ((), (), s32[]{:S(2)}) async-start(), calls=%async_computation | async-start | bytes 5308416 | tf_op jit(solution)/shard_map/all_gather | solution.py:829
  170.0 85.4 %copy-start.8 = (f32[1,3072]{1,0:T(1,128)S(1)}, f32[1,3072]{1,0:T(1,128)}, u32[]{:S(2)}) copy-start(f32[1,3072]{1,0:T(1,128)} %get-tuple-element.63) | copy-start | bytes 36868
  170.0 86.1 %copy-start.7 = (f32[8,768]{1,0:T(8,128)S(1)}, f32[8,768]{1,0:T(8,128)}, u32[]{:S(2)}) copy-start(f32[8,768]{1,0:T(8,128)} %get-tuple-element.61) | copy-start | bytes 73732
  410.2 9.7 %copy-start.1 = (s32[8,200]{1,0:T(8,128)S(1)}, s32[8,200]{1,0:T(8,128)}, u32[]{:S(2)}) copy-start(s32[8,200]{1,0:T(8,128)} %param.23) | copy-start | bytes 19204
  415.4 2.7 copy-start.3
  415.4 3.4 copy-start.6
Sparse Core Ops, SparseCore 0:
  9.7 11.9 all-gather.6
  23.2 13.7 all-gather.4

commit v2 on v0

v2 whole, which is shorter than its diff:
```python
import functools
import types
import jax
import jax.numpy as jnp
from jax import lax
from jax.experimental import pallas as pl
from jax.experimental.pallas import tpu as pltpu
from jax.sharding import PartitionSpec as P

F32 = jnp.float32
BF16 = jnp.bfloat16
EPS = 1e-06
LANES = 128
V_MASK, V_G1, V_B1, V_PB, V_GA1, V_G2, V_B2, V_FB2, V_GA2 = range(9)
S_GA2, S_FB2, S_LG2, S_LB2, S_GA1, S_PB = range(6)
T_MASK, T_LG1, T_LB1, T_QB, T_VB = range(5)


def dot(a, b):
    return jnp.dot(a, b, preferred_element_type=F32)


def dot_nt(a, b):
    return lax.dot_general(a, b, (((1,), (1,)), ((), ())), preferred_element_type=F32)


def dot_tn(a, b):
    return lax.dot_general(a, b, (((0,), (0,)), ((), ())), preferred_element_type=F32)


def norm_parts(v):
    c = v - jnp.mean(v, axis=-1, keepdims=True)
    r = lax.rsqrt(jnp.mean(c * c, axis=-1, keepdims=True) + EPS)
    return c * r, r


def norm_back(n, r, y, gain):
    yg = y * gain
    return r * (
        yg - jnp.mean(yg, axis=-1, keepdims=True) - n * jnp.mean(yg * n, axis=-1, keepdims=True)
    )


def low_half(shape):
    return lax.broadcasted_iota(jnp.int32, shape, 1) < (LANES // 2)

MESHID = pl.DeviceIdType.MESH


def here():
    dp = lax.axis_index("dp")
    return dp // 4, (dp // 2) % 2, dp % 2, lax.axis_index("head")


def at_dp(z, y, x):
    return {"dp": (z * 2 + y) * 2 + x}


def greet(depth):
    z, y, x, head = here()
    found = [at_dp(z, y, 1 - x), at_dp(z, 1 - y, x), {"head": 1 - head}]
    found += [at_dp((z + k) % depth, y, x) for k in range(1, depth)]
    barrier = pltpu.get_barrier_semaphore()
    for dev in found:
        pl.semaphore_signal(barrier, inc=1, device_id=dev, device_id_type=MESHID)
    pl.semaphore_wait(barrier, len(found))


class Wire:
    def __init__(self, send, recv):
        self.send, self.recv, self.next, self.open = send, recv, 0, []

    def slot(self):
        self.next += 1
        return self.next - 1

    def copy(self, i, src, dst, dev):
        return pltpu.make_async_remote_copy(
            src_ref=src, dst_ref=dst, send_sem=self.send.at[i], recv_sem=self.recv.at[i],
            device_id=dev, device_id_type=MESHID,
        )

    def start(self, i, make):
        self.copy(i, *make()).start()
        self.open.append((i, make))

    def arrived(self, i, ref, dev):
        self.copy(i, ref, ref, dev).wait_recv()

    def sent(self):
        for i, make in self.open:
            self.copy(i, *make()).wait_send()
        self.open = []


class Local:
    def __init__(self, sems):
        self.sems, self.next, self.open = sems, 0, []

    def start(self, make):
        i = self.next
        self.next += 1
        pltpu.make_async_copy(*make(), self.sems.at[i]).start()
        wait = lambda: pltpu.make_async_copy(*make(), self.sems.at[i]).wait()
        self.open.append(wait)
        return wait


def hops(p, y, x):
    ey, ex = (1 - y, x), (y, 1 - x)
    return (ey, ex) if p == 0 else (ex, ey)


def gather_stages(wire, depth, own, slot, column=None):
    z, y, x, head = here()
    ids = {}
    for p in range(2):
        for k in range(depth):
            for kind in "zabc":
                ids[p, kind, k] = wire.slot()
        for kind in range(0 if column is None else 4):
            ids[p, "s", kind] = wire.slot()
    up = lambda k: (z + k) % depth
    down = lambda k: (z + depth - k) % depth

    def columns(p):
        (ay, ax), (by, bx) = hops(p, y, x)
        return (y, x), (ay, ax), (by, bx), (1 - y, 1 - x)

    def send_up(p, k):
        wire.start(ids[p, "z", k], lambda: (own(p), slot(p, z, y, x), at_dp(up(k), y, x)))

    def send_square(p, k, kind, col, to, first=False):
        def make():
            cs = columns(p)
            dst = slot(p, down(k), *cs[col])
            return own(p) if first else dst, dst, at_dp(z, *cs[to])
        wire.start(ids[p, kind, k], make)

    def wait(p, k, kind, col, frm):
        cs = columns(p)
        dev = at_dp(down(k), y, x) if frm is None else at_dp(z, *cs[frm])
        wire.arrived(ids[p, kind, k], slot(p, down(k), *cs[col]), dev)

    def begin():
        for k in range(1, depth):
            for p in range(2):
                send_up(p, k)
        for p in range(2):
            send_square(p, 0, "a", 0, 1, True)
            send_square(p, 0, "b", 0, 2, True)

    def from_column(k):
        for p in range(2):
            wait(p, k, "z", 0, None)
            send_square(p, k, "a", 0, 1)
            send_square(p, k, "b", 0, 2)

    def from_first(k):
        for p in range(2):
            wait(p, k, "a", 1, 1)
            send_square(p, k, "c", 1, 2)

    def from_second(kind, col):
        for p in range(2):
            for k in range(depth):
                wait(p, k, kind, col, 2)

    def across(which):
        for p in range(2):
            def make(p=p):
                block = column(p, *columns(p)[which], head)
                return block, block, {"head": 1 - head}
            wire.start(ids[p, "s", which], make)

    def crossed():
        for which in range(4):
            for p in range(2):
                wire.arrived(ids[p, "s", which], column(p, *columns(p)[which], 1 - head), {"head": 1 - head})

    part = functools.partial
    stages = {"begin": begin, "b": part(from_second, "b", 2), "c": part(from_second, "c", 3), "crossed": crossed}
    for k in range(depth):
        stages["z%d" % k] = part(from_column, k)
        stages["a%d" % k] = part(from_first, k)
        stages["s%d" % k] = part(across, k)
    return stages


def add_into(dst, src):
    dst[...] = (dst[...].astype(F32) + src[...].astype(F32)).astype(dst.dtype)


class SquareSum:
    def __init__(self, wire, theirs, mine, pair_in, square_in, line_in):
        self.wire, self.theirs, self.mine = wire, theirs, mine
        self.pair_in, self.square_in, self.line_in = pair_in, square_in, line_in
        self.ids = {(p, kind): wire.slot() for p in range(2) for kind in "hab"}
        self.place = here()

    def devices(self, p):
        z, y, x, head = self.place
        ex, ey = at_dp(z, y, 1 - x), at_dp(z, 1 - y, x)
        return (ex, ey) if p == 0 else (ey, ex)

    def pair(self):
        for p in range(2):
            self.wire.start(self.ids[p, "h"], lambda p=p: (self.theirs(p), self.pair_in(p), {"head": 1 - self.place[3]}))

    def first(self):
        z, y, x, head = self.place
        for p in range(2):
            self.wire.arrived(self.ids[p, "h"], self.pair_in(p), {"head": 1 - head})
            add_into(self.mine(p, None, None), self.pair_in(p))

            def make(p=p):
                src = self.mine(p, None, 1 - x) if p == 0 else self.mine(p, 1 - y, None)
                return src, self.square_in(p), self.devices(p)[0]
            self.wire.start(self.ids[p, "a"], make)

    def second(self):
        z, y, x, head = self.place
        for p in range(2):
            self.wire.arrived(self.ids[p, "a"], self.square_in(p), self.devices(p)[0])
            add_into(self.mine(p, None, x) if p == 0 else self.mine(p, y, None), self.square_in(p))

            def make(p=p):
                src = self.mine(p, 1 - y, x) if p == 0 else self.mine(p, y, 1 - x)
                return src, self.line_in(p), self.devices(p)[1]
            self.wire.start(self.ids[p, "b"], make)

    def third(self):
        z, y, x, head = self.place
        for p in range(2):
            self.wire.arrived(self.ids[p, "b"], self.line_in(p), self.devices(p)[1])
            add_into(self.mine(p, y, x), self.line_in(p))


class ColumnSum:
    def __init__(self, wire, depth, part, column_in):
        self.wire, self.depth, self.part, self.column_in = wire, depth, part, column_in
        self.ids = {(p, k): wire.slot() for p in range(2) for k in range(1, depth)}
        self.place = here()

    def make(self, p, k):
        z, y, x, head = self.place
        to = (z + k) % self.depth
        return self.part(p, to), self.column_in(p, k), at_dp(to, y, x)

    def send(self, when=None):
        z = self.place[0]
        for p in range(2):
            for k in range(1, self.depth):
                go = lambda p=p, k=k: self.wire.copy(self.ids[p, k], *self.make(p, k)).start()
                if when is None:
                    go()
                else:
                    pl.when(when((z + k) % self.depth))(go)

    def opened(self):
        for p in range(2):
            for k in range(1, self.depth):
                self.wire.open.append((self.ids[p, k], functools.partial(self.make, p, k)))

    def total(self, p):
        z, y, x, head = self.place
        acc = self.part(p, z)[...].astype(F32)
        for k in range(1, self.depth):
            back = at_dp((z + self.depth - k) % self.depth, y, x)
            self.wire.arrived(self.ids[p, k], self.column_in(p, k), back)
            acc = acc + self.column_in(p, k)[...].astype(F32)
        return acc


class TargetSum:
    def __init__(self, wire, depth, t, part, column_in):
        self.wire, self.depth, self.t, self.part, self.column_in = wire, depth, t, part, column_in
        self.ids = [wire.slot() for _ in range(2 * (depth - 1))]
        self.place = here()

    def copy(self, p):
        z, y, x, head = self.place
        k = (z + self.depth - self.t) % self.depth - 1
        k = jnp.maximum(k, 0)
        return self.wire.copy(self.ids[p * (self.depth - 1)] + k, self.part(p), self.column_in.at[p, k], at_dp(self.t, y, x))

    def away(self, action):
        @pl.when(self.place[0] != self.t)
        def _():
            for p in range(2):
                action(self.copy(p))

    def send(self):
        self.away(lambda copy: copy.start())

    def sent(self):
        self.away(lambda copy: copy.wait_send())

    def total(self, store):
        z, y, x, head = self.place

        @pl.when(z == self.t)
        def _():
            for p in range(2):
                acc = self.part(p)[...].astype(F32)
                for k in range(self.depth - 1):
                    back = at_dp((self.t + k + 1) % self.depth, y, x)
                    self.wire.arrived(self.ids[p * (self.depth - 1) + k], self.column_in.at[p, k], back)
                    acc = acc + self.column_in[p, k].astype(F32)
                store(p, acc)


class SmallSum:
    def __init__(self, wire, depth, bufs, line):
        self.wire, self.depth, self.bufs, self.line = wire, depth, bufs, line
        self.ids = [wire.slot() for _ in range(2 + depth)]
        self.place = here()

    def devices(self):
        z, y, x, head = self.place
        return [{"head": 1 - head}, at_dp(z, y, 1 - x), at_dp(z, 1 - y, x)]

    def send(self, n):
        self.wire.start(self.ids[n], lambda: (self.bufs.at[2 * n], self.bufs.at[2 * n + 1], self.devices()[n]))

    def take(self, n):
        self.wire.arrived(self.ids[n], self.bufs.at[2 * n + 1], self.devices()[n])
        self.bufs[2 * n + 2] = self.bufs[2 * n] + self.bufs[2 * n + 1]

    def begin(self):
        self.send(0)

    def middle(self, n):
        self.take(n - 1)
        self.send(n)

    def column(self):
        z, y, x, head = self.place
        self.take(2)
        self.line[z] = self.bufs[6]
        for k in range(1, self.depth):
            self.wire.start(
                self.ids[2 + k],
                lambda k=k: (self.bufs.at[6], self.line.at[z], at_dp((z + k) % self.depth, y, x)),
            )

    def result(self):
        z, y, x, head = self.place
        for k in range(1, self.depth):
            back = (z + self.depth - k) % self.depth
            self.wire.arrived(self.ids[2 + k], self.line.at[back], at_dp(back, y, x))
        total = self.line[0]
        for n in range(1, self.depth):
            total = total + self.line[n]
        return total


def bind(names, refs):
    assert len(names) == len(refs)
    return types.SimpleNamespace(**dict(zip(names, refs)))


def spread_mask(masked, tmp, ch):
    images, rows = masked.shape
    tmp[...] = jnp.zeros_like(tmp)
    tmp[0:images, 0:rows] = masked[...].astype(F32)
    turned = tmp[...].T
    for i in range(images):
        ch[i] = turned[0:rows, i:i + 1]


def pad_index(raw, idx):
    idx[...] = jnp.zeros_like(idx)
    idx[0:raw.shape[0], 0:raw.shape[1]] = raw[...]


def run_all(stages):
    for stage in stages:
        stage()


def vmem(n):
    return [pl.BlockSpec(memory_space=pltpu.VMEM)] * n


ANY = pl.BlockSpec(memory_space=pl.ANY)
sd = jax.ShapeDtypeStruct
dma = lambda n: pltpu.SemaphoreType.DMA((n,))


def whole(a):
    return pl.BlockSpec(a.shape, lambda s: (0,) * len(a.shape), pipeline_mode=pl.Buffered(1))


FWD_IN = ("x", "masked", "kv", "raw", "vec")
FWD_OUT = ("normed", "q", "k", "v", "p", "att", "attn", "res", "n2")
FWD_SCR = ("bias", "idx", "valid", "tmp", "ch", "lsem")


def attn_forward_kernel(direct, *refs):
    hbm = tuple(n + "_hbm" for n in FWD_OUT[:6])
    if direct:
        names = FWD_IN + ("mixown", "wown", "wpown", "own1", "own2", "spot") + hbm + FWD_OUT[6:]
        names += ("w", "wp", "w1", "w2", "b1") + FWD_OUT[:6] + FWD_SCR + ("mix", "bufs", "line", "send", "recv")
    else:
        names = FWD_IN + ("mix", "w", "wp") + hbm + FWD_OUT[6:] + FWD_OUT[:6] + FWD_SCR
    r = bind(names, refs)
    images, rows, width = r.x.shape
    rp = r.normed.shape[0] // images
    keys = r.k.shape[1]
    heads = r.bias.shape[0]
    scale = (width // heads) ** -0.5
    here_heads = heads // r.mix.shape[0]
    own_tiles = width // r.mix.shape[0] // LANES
    chunks = (r.mix.shape[1] - 2 * own_tiles) // here_heads

    plan = {}
    local = Local(r.lsem)
    head = lax.axis_index("head")
    if direct:
        depth = r.w1.shape[0]
        z, y, x, head = here()
        half = r.wown.shape[2]
        cols = pl.ds(pl.multiple_of(head * half, LANES), half)
        prows = pl.ds(pl.multiple_of(head * half, LANES), half)
        full = (r.w1, r.w2)
        wire = Wire(r.send, r.recv)
        greet(depth)
        other = {"head": 1 - head}
        swaps = [
            (r.mixown, r.mix.at[head], r.mix.at[1 - head]),
            (r.wown, r.w.at[:, :, cols], r.w.at[:, :, pl.ds(pl.multiple_of((1 - head) * half, LANES), half)]),
            (r.wpown, r.wp.at[prows], r.wp.at[pl.ds(pl.multiple_of((1 - head) * half, LANES), half)]),
        ]
        swap_ids = [wire.slot() for _ in swaps]
        for i, (src, dst, back) in zip(swap_ids, swaps):
            wire.start(i, lambda src=src, dst=dst: (src, dst, other))
        for src, dst, back in swaps:
            local.start(lambda src=src, dst=dst: (src, dst))
        slot = lambda p, zz, yy, xx: full[p].at[zz, yy, xx, head]
        own = (r.own1, r.own2)
        for p in range(2):
            local.start(lambda p=p: (own[p], slot(p, z, y, x)))
        r.bufs[0] = r.spot[...]
        small = SmallSum(wire, depth, r.bufs, r.line)
        g = gather_stages(
            wire, depth, own=lambda p: own[p], slot=slot,
            column=lambda p, yy, xx, hd: full[p].at[:, yy, xx, hd],
        )
        g["begin"]()
        small.begin()
        middle = functools.partial
        plan = {
            "g1": [g["z1"], g["a0"]], "g2": [middle(small.middle, 1)],
            "p1": [g["z2"], g["a1"], middle(small.middle, 2)],
            "t1": [g["z3"], g["a2"], g["s0"], small.column], "t4": [g["a3"], g["s1"]],
            "t5": [g["b"], g["s2"]], "t6": [g["c"], g["s3"]],
        }

    def tick(point):
        run_all(plan.get(point, ()))

    spread_mask(r.masked, r.tmp, r.ch)
    pad_index(r.raw, r.idx)
    r.valid[...] = jnp.zeros_like(r.valid)
    r.valid[0:r.kv.shape[0], 0:rows] = r.kv[...]
    r.normed[...] = jnp.zeros_like(r.normed)
    r.n2[...] = jnp.zeros_like(r.n2)
    r.res[...] = jnp.zeros_like(r.res)

    def hidden_of(i):
        ch = r.ch[i]
        return r.x[i].astype(F32) * (1.0 - ch) + ch * r.vec[V_MASK:V_MASK + 1, :]

    def first_norm(i, carry):
        n, _ = norm_parts(hidden_of(i))
        out = n * r.vec[V_G1:V_G1 + 1, :] + r.vec[V_B1:V_B1 + 1, :]
        r.normed[pl.ds(pl.multiple_of(i * rp, 16), rows), :] = out.astype(BF16)
        return carry

    lax.fori_loop(0, images, first_norm, 0)
    if direct:
        for wait in local.open:
            wait()
        local.open = []
        wire.arrived(swap_ids[0], swaps[0][2], other)
    send_out = lambda name, at=slice(None): local.start(
        lambda: (getattr(r, name).at[at], getattr(r, name + "_hbm").at[at]))
    send_out("normed")

    def gather_head(h, carry):
        for half in range(keys // LANES):
            idx = r.idx[:, half * LANES:(half + 1) * LANES]
            low = idx & (LANES - 1)
            high = idx >> 7
            acc = jnp.zeros(idx.shape, F32)
            for c in range(chunks):
                row = r.mix[h // here_heads, pl.ds((h % here_heads) * chunks + c, 1), :]
                got = jnp.take_along_axis(jnp.broadcast_to(row, idx.shape), low, axis=1)
                acc = jnp.where(high == c, got, acc)
            r.bias[h, :, half * LANES:(half + 1) * LANES] = acc
        return carry

    groups = 3
    for n in range(groups):
        lax.fori_loop(n * heads // groups, (n + 1) * heads // groups, gather_head, 0)
        tick("g%d" % n)

    if direct:
        for n in (1, 2):
            wire.arrived(swap_ids[n], swaps[n][2], other)
    zeros_tail = jnp.zeros((images, keys - rp, width), BF16)
    r.k[:, rp:, :] = zeros_tail
    r.v[:, rp:, :] = zeros_tail

    def bias_row(kind, nb):
        tiles = []
        for t in (2 * nb, 2 * nb + 1):
            at = here_heads * chunks + kind * own_tiles + t % own_tiles
            tiles.append(r.mix[t // own_tiles, at:at + 1, :])
        return jnp.concatenate(tiles, axis=1)

    for c, (dst, kind) in enumerate(((r.q, 0), (r.k, None), (r.v, 1))):
        for nb in range(width // 256):
            cols = slice(nb * 256, (nb + 1) * 256)
            acc = dot(r.normed[...], r.w[c, :, cols])
            if kind is not None:
                acc = acc + bias_row(kind, nb)
            acc = acc.astype(BF16)
            for i in range(images):
                dst[i, :rp, cols] = acc[i * rp:(i + 1) * rp]
        send_out("qkv"[c])
        tick("p%d" % c)

    def attend(t, carry):
        i = t // (heads // 2)
        j = t % (heads // 2)
        lanes = pl.ds(pl.multiple_of(j * LANES, LANES), LANES)
        qp = r.q[i, :, lanes]
        kp = r.k[i, :, lanes]
        vp = r.v[i, :, lanes]
        lo = low_half((rp, LANES))
        ok = r.valid[pl.ds(head * images + i, 1), :] > 0
        outs = []
        for s in range(2):
            qs = jnp.where(lo if s == 0 else jnp.logical_not(lo), qp, jnp.zeros_like(qp))
            sc = dot_nt(qs, kp) * scale + r.bias[2 * j + s]
            sc = jnp.where(ok, sc, -1e30)
            e = jnp.exp(sc - jnp.max(sc, axis=-1, keepdims=True))
            prob = e * (1.0 / jnp.sum(e, axis=-1, keepdims=True))
            r.p[i, 2 * j + s] = prob
            outs.append(dot(prob.astype(BF16), vp))
        att = jnp.where(lo, outs[0], outs[1]).astype(BF16)
        r.att[pl.ds(pl.multiple_of(i * rp, 16), rp), lanes] = att
        return carry

    work = images * (heads // 2)
    for n in range(2 * images):
        lax.fori_loop(n * work // (2 * images), (n + 1) * work // (2 * images), attend, 0)
        if n % 2:
            send_out("p", n // 2)
        tick("t%d" % n)
    send_out("att")

    def finish(i, carry):
        at = pl.multiple_of(i * rp, 16)
        branch = dot(r.att[pl.ds(at, rp), :], r.wp[...]) + r.vec[V_PB:V_PB + 1, :]
        r.attn[pl.ds(at, rp), :] = branch
        res = hidden_of(i) + r.vec[V_GA1:V_GA1 + 1, :] * branch[:rows]
        r.res[pl.ds(at, rows), :] = res
        n, _ = norm_parts(res)
        out = n * r.vec[V_G2:V_G2 + 1, :] + r.vec[V_B2:V_B2 + 1, :]
        r.n2[pl.ds(at, rows), :] = out.astype(BF16)
        return carry

    lax.fori_loop(0, images, finish, 0)
    if direct:
        g["crossed"]()
        r.b1[...] = small.result()
        wire.sent()
    for wait in local.open:
        wait()


def attn_forward(direct, x, masked, kv, raw, vec, heads, extra, rp, keys, depth):
    images, rows, width = x.shape
    flat = images * rp
    outs = [
        sd((flat, width), BF16), sd((images, rp, width), BF16), sd((images, keys, width), BF16),
        sd((images, keys, width), BF16), sd((images, heads, rp, keys), F32),
        sd((flat, width), BF16), sd((flat, width), F32), sd((flat, width), F32), sd((flat, width), BF16),
    ]
    tall = -(-max(kv.shape[0], images) // 8) * 8
    scratch = [pltpu.VMEM(o.shape, o.dtype) for o in outs[:6]] + [
        pltpu.VMEM((heads, rp, keys), F32), pltpu.VMEM((rp, keys), jnp.int32), pltpu.VMEM((tall, keys), jnp.int32),
        pltpu.VMEM((tall, keys), F32), pltpu.VMEM((images, rows, 1), F32), dma(16),
    ]
    in_specs, out_specs = vmem(5), [ANY] * 6 + vmem(3)
    params = {}
    if direct:
        mixown, wown, wpown, own1, own2, spot = extra
        part = sd((depth, 2, 2, 2) + own1.shape, BF16)
        outs += [sd((3, width, width), BF16), sd((width, width), BF16), part, part, sd(spot.shape, F32)]
        in_specs += vmem(6)
        out_specs += vmem(2) + [ANY, ANY] + vmem(1)
        n = 3 + 2 * (4 * depth + 4) + 2 + depth
        scratch += [
            pltpu.VMEM((2,) + mixown.shape, F32), pltpu.VMEM((7,) + spot.shape, F32),
            pltpu.VMEM((depth,) + spot.shape, F32), dma(n), dma(n),
        ]
        params = dict(collective_id=1, has_side_effects=True)
    else:
        in_specs += vmem(3)
    return pl.pallas_call(
        functools.partial(attn_forward_kernel, direct), name="attn_forward",
        out_shape=tuple(outs), in_specs=in_specs, out_specs=out_specs, scratch_shapes=scratch,
        compiler_params=pltpu.CompilerParams(vmem_limit_bytes=60 * 2**20, **params),
    )(x, masked, kv, raw, vec, *extra)


MLP_IN = ("n2", "res", "attn", "cot", "vec", "b1", "w1", "w2")
MLP_OUT = ("gb1", "out", "dres", "dproj", "small")
MLP_SCR = ("db", "act", "dpre", "branch", "dn")
MLP_COMM = ("g", "pair_in", "square_in", "line_in", "column", "column_in", "send", "recv", "lsem")


def level_of(step, steps):
    return jnp.where(step == 0, 0, jnp.where(step == 1, steps - 1, step - 1))


def mlp_kernel(direct, *refs):
    if direct:
        r = bind(MLP_IN + ("sums", "glast", "gff") + MLP_OUT + MLP_SCR + MLP_COMM, refs)
    else:
        r = bind(MLP_IN + ("g1", "g2") + MLP_OUT + MLP_SCR, refs)
    images, rows, width = r.cot.shape
    flat = r.n2.shape[0]
    rp = flat // images
    step = pl.program_id(0)
    steps = pl.num_programs(0)
    plan = {}
    if direct:
        depth = r.g.shape[0]
        done = depth - 1
        wire = Wire(r.send, r.recv)
        z, y, x, head = here()
        every = lambda v: slice(None) if v is None else v
        chunks = [
            SquareSum(
                wire,
                theirs=lambda p, t=t: r.g.at[t, p, :, :, 1 - head],
                mine=lambda p, yy, xx, t=t: r.g.at[t, p, every(yy), every(xx), head],
                pair_in=lambda p, t=t: r.pair_in.at[t, p],
                square_in=lambda p, t=t: r.square_in.at[t, p],
                line_in=lambda p, t=t: r.line_in.at[t, p],
            )
            for t in range(done)
        ]
        ends = [
            TargetSum(wire, depth, t, part=lambda p, n=n: r.column.at[n, p], column_in=r.column_in.at[n])
            for n, t in enumerate((0, depth - 1))
        ]

        def close(n):
            chunks[n].third()
            for p in range(2):
                if n < 2:
                    r.column[n, p] = r.g[n, p, y, x, head]
                else:
                    r.sums[p] = r.g[n, p, y, x, head]
            if n < 2:
                ends[n].send()

        def last_block():
            return pltpu.make_async_copy(r.g.at[done], r.glast, r.lsem.at[0])

        def end():
            r.gff[...] = jnp.zeros_like(r.gff)

            def keep(p, value):
                r.gff[p] = value
            for t in ends:
                t.total(keep)
                t.sent()
            wire.sent()
            last_block().wait()

        part = functools.partial
        plan = {
            (0, 0): [part(greet, depth)], (0, 4): [chunks[0].pair],
            (1, 1): [chunks[0].first], (1, 4): [chunks[1].pair, chunks[0].second],
            (2, 1): [chunks[1].first], (2, 2): [part(close, 0)], (2, 4): [chunks[2].pair, chunks[1].second],
            (3, 1): [chunks[2].first], (3, 2): [part(close, 1)], (3, 4): [lambda: last_block().start(), chunks[2].second],
            (3, 5): [part(close, 2)], (3, 6): [end],
        }

    def tick(point):
        for (s, at), stages in sorted(plan.items(), key=lambda kv: kv[0]):
            if at == point:
                pl.when(step == s)(functools.partial(run_all, stages))

    tick(0)

    @pl.when(step == 0)
    def _():
        r.db[...] = jnp.zeros_like(r.db)
        r.branch[...] = jnp.zeros_like(r.branch)
        r.dn[...] = jnp.zeros_like(r.dn)

        def fill(i, carry):
            up = r.cot[i].astype(F32) * r.vec[V_GA2:V_GA2 + 1, :]
            r.db[pl.ds(pl.multiple_of(i * rp, 16), rows), :] = up.astype(BF16)
            return carry

        lax.fori_loop(0, images, fill, 0)

    def tile(i, gb1):
        at = pl.ds(pl.multiple_of(i * rp, 16), rp)
        pre = dot_nt(r.n2[at, :], r.w1[...]) + r.b1[...]
        cdf = 0.5 * (1.0 + lax.erf(pre * 0.7071067811865476))
        slope = cdf + pre * (0.3989422804014327 * jnp.exp(-0.5 * pre * pre))
        act = (pre * cdf).astype(BF16)
        r.act[at, :] = act
        dpre = (dot_nt(r.db[at, :], r.w2[...]) * slope).astype(BF16)
        r.dpre[at, :] = dpre
        r.branch[at, :] += dot(act, r.w2[...])
        r.dn[at, :] += dot(dpre, r.w1[...])
        return gb1 + jnp.sum(dpre.astype(F32), axis=0, keepdims=True)

    gb1 = lax.fori_loop(0, images // 2, tile, jnp.zeros(r.gb1.shape, F32))
    tick(1)
    r.gb1[...] = lax.fori_loop(images // 2, images, tile, gb1)
    tick(2)

    def store(p, value):
        if not direct:
            (r.g1, r.g2)[p][...] = value
            return
        r.g[step, p] = value.reshape(r.g.shape[2:])

    store(1, dot_tn(r.act[...], r.db[...]).astype(BF16))
    tick(3)
    store(0, dot_tn(r.dpre[...], r.n2[...]).astype(BF16))
    tick(4)

    @pl.when(step == steps - 1)
    def _():
        r.dproj[...] = jnp.zeros_like(r.dproj)
        r.dres[...] = jnp.zeros_like(r.dres)
        r.small[...] = jnp.zeros_like(r.small)

        def add(row, value):
            r.small[row:row + 1, :] += jnp.sum(value, axis=0, keepdims=True)

        def finish(i, carry):
            at = pl.multiple_of(i * rp, 16)
            span = pl.ds(at, rows)
            up = r.cot[i].astype(F32)
            branch = r.branch[span, :] + r.vec[V_FB2:V_FB2 + 1, :]
            res = r.res[span, :]
            r.out[i] = (res + r.vec[V_GA2:V_GA2 + 1, :] * branch).astype(BF16)
            add(S_GA2, up * branch)
            add(S_FB2, (up * r.vec[V_GA2:V_GA2 + 1, :]).astype(BF16).astype(F32))
            n, inv = norm_parts(res)
            dn = r.dn[span, :]
            add(S_LG2, dn * n)
            add(S_LB2, dn)
            dres = up + norm_back(n, inv, dn, r.vec[V_G2:V_G2 + 1, :])
            r.dres[span, :] = dres
            add(S_GA1, dres * r.attn[span, :])
            dproj = (dres * r.vec[V_GA1:V_GA1 + 1, :]).astype(BF16)
            r.dproj[span, :] = dproj
            add(S_PB, dproj.astype(F32))
            return carry

        lax.fori_loop(0, images, finish, 0)

    tick(5)
    tick(6)


def mlp(direct, n2, res, attn, cot, vec, b1, w1, w2, steps):
    images, rows, width = cot.shape
    flat = n2.shape[0]
    ff = w1.shape[0]
    block = ff // steps
    share = block // 8
    part = pl.BlockSpec((block, width), lambda s: (level_of(s, steps), 0))
    line = pl.BlockSpec((1, block), lambda s: (0, level_of(s, steps)))
    outs = [sd((1, ff), F32), sd(cot.shape, BF16), sd((flat, width), F32), sd((flat, width), BF16), sd((8, width), F32)]
    specs = [line] + [whole(o) for o in outs[1:]]
    scratch = [
        pltpu.VMEM((flat, width), BF16), pltpu.VMEM((flat, block), BF16), pltpu.VMEM((flat, block), BF16),
        pltpu.VMEM((flat, width), F32), pltpu.VMEM((flat, width), F32),
    ]
    params = {}
    if direct:
        first = [sd((2, share, width), BF16), sd((2, 2, 2, 2, share, width), BF16), sd((2, share, width), F32)]
        outs, specs = first + outs, [whole(first[0]), ANY, whole(first[2])] + specs
        n = 6 * (steps - 1) + 4 * (steps - 1)
        scratch += [
            pltpu.VMEM((steps, 2, 2, 2, 2, share, width), BF16), pltpu.VMEM((steps - 1, 2, 2, 2, share, width), BF16),
            pltpu.VMEM((steps - 1, 2, 2, share, width), BF16), pltpu.VMEM((steps - 1, 2, share, width), BF16),
            pltpu.VMEM((2, 2, share, width), BF16), pltpu.VMEM((2, 2, steps - 1, share, width), BF16),
            dma(n), dma(n), dma(1),
        ]
        params = dict(collective_id=2, has_side_effects=True)
    else:
        outs, specs = [sd((ff, width), BF16)] * 2 + outs, [part, part] + specs
    return pl.pallas_call(
        functools.partial(mlp_kernel, direct), name="mlp", grid=(steps,), out_shape=tuple(outs),
        in_specs=[whole(n2), whole(res), whole(attn), whole(cot), whole(vec), line, part, part],
        out_specs=specs, scratch_shapes=scratch,
        compiler_params=pltpu.CompilerParams(vmem_limit_bytes=60 * 2**20, **params),
    )(n2, res, attn, cot, vec, b1, w1, w2)


BWD_IN = ("x", "masked", "raw", "vec", "w", "wp", "normed", "q", "k", "v", "p", "att", "dres", "dproj")
BWD_SCR = ("dat", "dqkv", "ds", "nt", "dpt", "idx", "tmp", "ch")
BWD_COMM = ("g", "pair_in", "square_in", "line_in", "column_in", "ff", "ffpair", "ffsquare", "ffline", "ffcol", "ffcolumn")


def attn_backward_kernel(direct, *refs):
    if direct:
        names = BWD_IN + ("sums", "glast", "gffin", "s2", "gb1", "gx", "full", "gff", "small") + BWD_SCR + BWD_COMM
        r = bind(names + ("bufs", "line", "tsum", "gathered", "send", "recv", "lsem"), refs)
    else:
        r = bind(BWD_IN + ("gx", "gw", "gt", "tsum") + BWD_SCR, refs)
    images, rows, width = r.x.shape
    flat = r.normed.shape[0]
    rp = flat // images
    keys = r.k.shape[1]
    heads = r.ds.shape[0]
    scale = (width // heads) ** -0.5
    step = pl.program_id(0)
    pairs = heads // 2
    per = pairs // 2
    j = (step % 2) * per + step // 2
    plan = {}

    if direct:
        z, y, x, head = here()
        depth = r.g.shape[4]
        wire = Wire(r.send, r.recv)
        every = lambda v: slice(None) if v is None else v
        ff = SquareSum(
            wire,
            theirs=lambda p: r.glast.at[p, :, :, 1 - head],
            mine=lambda p, yy, xx: r.ff.at[p, every(yy), every(xx)],
            pair_in=lambda p: r.ffpair.at[p], square_in=lambda p: r.ffsquare.at[p], line_in=lambda p: r.ffline.at[p],
        )
        between = [
            TargetSum(wire, depth, n + 1, part=lambda p, n=n: r.ffcol.at[n, p], column_in=r.ffcolumn.at[n])
            for n in range(2)
        ]
        squares, lines, gathers = [], [], []
        for m in range(per):
            squares.append(SquareSum(
                wire,
                theirs=lambda p, m=m: r.g.at[m, 1 - head, p],
                mine=lambda p, yy, xx, m=m: r.g.at[m, head, p, :, :, every(yy), every(xx)],
                pair_in=lambda p, m=m: r.pair_in.at[m, p],
                square_in=lambda p, m=m: r.square_in.at[m, p], line_in=lambda p, m=m: r.line_in.at[m, p],
            ))
            lines.append(ColumnSum(
                wire, depth, part=lambda p, zz, m=m: r.g.at[m, head, p, :, zz, y, x],
                column_in=lambda p, k, m=m: r.column_in.at[m, p, k - 1],
            ))
            lanes_m = slice(m * LANES, (m + 1) * LANES)
            slot = lambda p, zz, yy, xx, lanes_m=lanes_m: r.gathered.at[p, :, zz, yy, xx, :, lanes_m]
            gathers.append(gather_stages(wire, depth, own=lambda p, slot=slot: slot(p, z, y, x), slot=slot))
        small = SmallSum(wire, depth, r.bufs, r.line)
        part = functools.partial

        def ff_begin():
            greet(depth)
            ff.pair()
            for p in range(2):
                own_block(p).start()
                r.ffcol[0, p] = r.sums[p]
            between[0].send()

        def own_block(p):
            return pltpu.make_async_copy(r.glast.at[p, :, :, head], r.ff.at[p], r.lsem.at[p])

        def ff_first():
            for p in range(2):
                own_block(p).wait()
            ff.first()

        def ff_third():
            ff.third()
            for p in range(2):
                r.ffcol[1, p] = r.ff[p, y, x]
            between[1].send()

        def ff_last():
            r.gff[...] = r.gffin[...]

            def keep(p, value):
                r.gff[p] = value
            for t in between:
                t.total(keep)
                t.sent()

        def third(m):
            squares[m].third()
            lines[m].send()
            lines[m].opened()

        def last(m):
            for p in range(2):
                r.gathered[p, :, z, y, x, :, m * LANES:(m + 1) * LANES] = lines[m].total(p).astype(BF16)
            gathers[m]["begin"]()

        g0, g1, g2 = gathers
        plan = {
            (0, 0): [ff_begin], (0, 1): [ff_first], (1, 2): [ff.second], (1, 4): [squares[0].pair],
            (2, 3): [ff_third, squares[0].first], (3, 4): [squares[1].pair, squares[0].second],
            (4, 3): [squares[1].first], (4, 4): [part(third, 0)],
            (5, 4): [squares[2].pair, squares[1].second, part(last, 0)],
            (5, 6): [squares[2].first, part(third, 1)], (5, 7): [g0["z1"], g0["z2"], g0["z3"]], (5, 8): [part(last, 1)],
            (5, 9): [squares[2].second, g0["a0"], g0["a1"], g0["a2"], g0["a3"]], (5, 10): [g1["z1"], g1["z2"], g1["z3"]],
            (5, 11): [part(third, 2), g0["b"], g0["c"]], (5, 12): [g1["a0"], g1["a1"], g1["a2"], g1["a3"]], (5, 13): [ff_last],
        }

    def tick(point):
        for (s, at), stages in plan.items():
            if at == point:
                pl.when(step == s)(functools.partial(run_all, stages))

    tick(0)

    @pl.when(step == 0)
    def _():
        for i in range(images):
            at = slice(i * rp, (i + 1) * rp)
            r.dat[at, :] = dot_nt(r.dproj[at, :], r.wp[...]).astype(BF16)
        spread_mask(r.masked, r.tmp, r.ch)
        pad_index(r.raw, r.idx)
        r.nt[...] = r.normed[...].T
        r.dpt[...] = r.dproj[...].T
        r.tsum[...] = jnp.zeros_like(r.tsum)

    tick(1)
    lanes = pl.ds(pl.multiple_of(j * LANES, LANES), LANES)
    r.ds[2 * j] = jnp.zeros((rp, keys), F32)
    r.ds[2 * j + 1] = jnp.zeros((rp, keys), F32)

    def image(i, carry):
        at = pl.ds(pl.multiple_of(i * rp, 16), rp)
        qp = r.q[i, :, lanes]
        kp = r.k[i, :, lanes]
        vp = r.v[i, :, lanes]
        da = r.dat[at, lanes]
        lo = low_half((rp, LANES))
        dv, dq, dk = [], [], []
        for s in range(2):
            das = jnp.where(lo if s == 0 else jnp.logical_not(lo), da, jnp.zeros_like(da))
            prob = r.p[i, s]
            dp = dot_nt(das, vp)
            dsc = prob * (dp - jnp.sum(prob * dp, axis=-1, keepdims=True))
            dsb = dsc.astype(BF16)
            r.ds[2 * j + s] += dsb.astype(F32)
            dv.append(dot_tn(prob.astype(BF16), da))
            dq.append(dot(dsb, kp))
            dk.append(dot_tn(dsb, qp))
        lok = low_half((keys, LANES))
        r.dqkv[0, at, lanes] = (jnp.where(lo, dq[0], dq[1]) * scale).astype(BF16)
        r.dqkv[1, at, lanes] = (jnp.where(lok, dk[0], dk[1]) * scale)[:rp].astype(BF16)
        r.dqkv[2, at, lanes] = jnp.where(lok, dv[0], dv[1])[:rp].astype(BF16)
        return carry

    lax.fori_loop(0, images // 2, image, 0)
    tick(2)
    lax.fori_loop(images // 2, images, image, 0)
    tick(3)

    def store(c, value):
        value = value.astype(BF16)
        if direct:
            r.g[step // 2, step % 2, c // 2, c % 2] = value.reshape(r.g.shape[4:])
        else:
            r.gw[0, c] = value

    for c in range(3):
        store(c, dot(r.nt[...], r.dqkv[c, :, lanes]))
    store(3, dot(r.dpt[...], r.att[:, lanes]))
    tick(4)

    @pl.when(step == pairs - 1)
    def _():
        def now(point):
            if direct:
                run_all(plan.get((pairs - 1, point), ()))

        def column(row, c):
            def body(i, acc):
                piece = r.dqkv[c, pl.ds(pl.multiple_of(i * rp, 16), rp), :].astype(F32)
                return acc + jnp.sum(piece, axis=0, keepdims=True)
            r.tsum[row:row + 1, :] = lax.fori_loop(0, images, body, jnp.zeros((1, width), F32))

        column(T_QB, 0)
        column(T_VB, 2)

        def finish(i, carry):
            at = pl.multiple_of(i * rp, 16)
            span = pl.ds(at, rp)
            dn = dot_nt(r.dqkv[0, span, :], r.w[0])
            dn += dot_nt(r.dqkv[1, span, :], r.w[1])
            dn += dot_nt(r.dqkv[2, span, :], r.w[2])
            dn = dn[:rows]
            ch = r.ch[i]
            hidden = r.x[i].astype(F32) * (1.0 - ch) + ch * r.vec[V_MASK:V_MASK + 1, :]
            n, inv = norm_parts(hidden)
            dh = r.dres[pl.ds(at, rows), :] + norm_back(n, inv, dn, r.vec[V_G1:V_G1 + 1, :])
            r.gx[i] = dh * (1.0 - ch)
            for row, value in ((T_MASK, dh * ch), (T_LG1, dn * n), (T_LB1, dn)):
                r.tsum[row:row + 1, :] += jnp.sum(value, axis=0, keepdims=True)
            return carry

        for i in range(images):
            lax.fori_loop(i, i + 1, finish, 0)
            now(5 + i)

        a_iota = lax.broadcasted_iota(jnp.int32, (8, keys), 0)
        b_iota = lax.broadcasted_iota(jnp.int32, (LANES, keys), 0)

        def scatter(t, acc):
            at = pl.ds(pl.multiple_of(t * 8, 8), 8)
            idx = r.idx[at, :]
            high, low = idx >> 7, idx & (LANES - 1)
            tiles = [r.ds[h, at, :] for h in range(heads)]
            lefts, rests, ones = [], [], []
            for s in range(8):
                pick = jnp.broadcast_to(high[s:s + 1], (8, keys)) == a_iota
                ones.append((jnp.broadcast_to(low[s:s + 1], (LANES, keys)) == b_iota).astype(F32).astype(BF16))
                left = jnp.concatenate(
                    [jnp.where(pick, jnp.broadcast_to(tile[s:s + 1], (8, keys)), 0.0) for tile in tiles], axis=0)
                top = left.astype(BF16)
                lefts.append(top)
                rests.append((left - top.astype(F32)).astype(BF16))
            one = jnp.concatenate(ones, axis=1)
            return acc + dot_nt(jnp.concatenate(lefts, axis=1), one) + dot_nt(jnp.concatenate(rests, axis=1), one)

        table = jnp.zeros((heads * 8, LANES), F32)
        blocks = rp // 8
        for part_ in range(5):
            table = lax.fori_loop(part_ * blocks // 5, (part_ + 1) * blocks // 5, scatter, table)
            now(9 + part_)
        if not direct:
            r.gt[...] = table
            return
        wide = width // LANES
        tall = heads * 8 // wide
        r.bufs[0, 0:8] = r.tsum[...]
        r.bufs[0, 8:16] = r.s2[...]
        at = 16
        for t in range(wide):
            r.bufs[0, at:at + tall, t * LANES:(t + 1) * LANES] = table[t * tall:(t + 1) * tall]
        at += tall
        r.bufs[0, at:at + r.gb1.shape[0]] = r.gb1[...]
        small.begin()
        last(2)
        small.middle(1)
        run_all([g1["b"], g1["c"]])
        run_all(g2["z%d" % k] for k in range(1, depth))
        small.middle(2)
        run_all(g2["a%d" % k] for k in range(depth))
        small.column()
        run_all([g2["b"], g2["c"]])
        r.full[...] = r.gathered[...]
        r.small[...] = small.result()
        wire.sent()


def attn_backward(direct, args, heads, extra, rp, keys, depth):
    x, masked, raw, vec, w, wp, normed, q, k, v, p, att, dres, dproj = args
    images, rows, width = x.shape
    flat = images * rp
    pairs = heads // 2
    per = pairs // 2
    order = lambda s: (s % 2) * per + s // 2
    outs = [sd((images, rows, width), F32)]
    specs = [whole(outs[0])]
    scratch = [
        pltpu.VMEM((flat, width), BF16), pltpu.VMEM((3, flat, width), BF16), pltpu.VMEM((heads, rp, keys), F32),
        pltpu.VMEM((width, flat), BF16), pltpu.VMEM((width, flat), BF16), pltpu.VMEM((rp, keys), jnp.int32),
        pltpu.VMEM((-(-images // 8) * 8, keys), F32), pltpu.VMEM((images, rows, 1), F32),
    ]
    params = {}
    if direct:
        sums, glast, gffin, s2, gb1 = extra
        share = glast.shape[-2]
        own = width // (4 * depth)
        total = 16 + heads * 8 * LANES // width + gb1.shape[0]
        more = [sd((2, 2, depth, 2, 2, own, per * LANES), BF16), sd((2, share, width), F32), sd((total, width), F32)]
        outs += more
        specs += [whole(o) for o in more]
        n = 6 + 4 * (depth - 1) + per * (6 + 2 * (depth - 1) + 8 * depth) + 2 + depth
        scratch += [pltpu.VMEM(s, BF16) for s in (
            (per, 2, 2, 2, depth, 2, 2, own, LANES), (per, 2, 2, depth, 2, 2, own, LANES),
            (per, 2, 2, depth, 2, own, LANES), (per, 2, 2, depth, own, LANES), (per, 2, depth - 1, 2, own, LANES),
            (2, 2, 2, share, width), (2, 2, 2, share, width), (2, 2, share, width), (2, share, width),
            (2, 2, share, width), (2, 2, depth - 1, share, width),
        )]
        scratch += [pltpu.VMEM(s, F32) for s in ((7, total, width), (depth, total, width), (8, width))]
        scratch += [pltpu.VMEM(more[0].shape, BF16), dma(n), dma(n), dma(2)]
        params = dict(collective_id=3, has_side_effects=True)
    else:
        more = [sd((pairs, 4, width, LANES), BF16), sd((heads * 8, LANES), F32), sd((8, width), F32)]
        outs += more
        specs += [pl.BlockSpec((1, 4, width, LANES), lambda s: (order(s), 0, 0, 0)), whole(more[1]), whole(more[2])]
    return pl.pallas_call(
        functools.partial(attn_backward_kernel, direct), name="attn_backward", grid=(pairs,), out_shape=tuple(outs),
        in_specs=[whole(a) for a in args[:10]]
        + [pl.BlockSpec((images, 2, rp, keys), lambda s: (0, order(s), 0, 0))] + [whole(a) for a in args[11:]]
        + [ANY if n == 1 else whole(a) for n, a in enumerate(extra)],
        out_specs=specs, scratch_shapes=scratch,
        compiler_params=pltpu.CompilerParams(vmem_limit_bytes=62 * 2**20, **params),
    )(*args, *extra)


def pack(rows, count):
    width = rows[0].shape[0]
    return jnp.concatenate(rows + [jnp.zeros(((count - len(rows)) * width,), F32)]).reshape(count, width)


def shards(
    inputs, masked, key_valid, rel_index, mask_token, ln1_gain, ln1_bias, w_qkv, qv_bias, rel_table,
    w_proj, proj_bias, gamma1, ln2_gain, ln2_bias, w_fc1, fc1_bias, w_fc2, fc2_bias, gamma2, cotangent,
):
    images, rows, width = inputs.shape
    dp, hn = lax.axis_size("dp"), lax.axis_size("head")
    me, head = lax.axis_index("dp"), lax.axis_index("head")
    depth = dp // 4
    share = w_fc2.shape[0]
    ff = share * dp * hn
    entries, heads = rel_table.shape[0], rel_table.shape[1] * hn
    rp, keys = -(-rows // 16) * 16, -(-rows // LANES) * LANES
    direct = hn == 2 and dp == 16 and ff % (8 * share) == 0 and share % 16 == 0 and width % (16 * dp) == 0

    tab_rows = -(-entries // LANES)
    tab = jnp.pad(rel_table.T, ((0, 0), (0, tab_rows * LANES - entries)))
    mix = jnp.concatenate([tab.reshape(-1, LANES), qv_bias.reshape(-1, LANES)])
    vec = pack([mask_token, ln1_gain, ln1_bias, proj_bias, gamma1, ln2_gain, ln2_bias, fc2_bias, gamma2], 16)
    w3 = jnp.transpose(w_qkv, (1, 0, 2))

    if direct:
        spot_shape = (8, ff // 8)
        owner = (lax.broadcasted_iota(jnp.int32, spot_shape, 0) * (ff // 8) + lax.broadcasted_iota(jnp.int32, spot_shape, 1)) // share
        spot = jnp.where(owner == me * hn + head, jnp.tile(fc1_bias.astype(F32), ff // 8 // share)[None], 0.0)
        extra = (mix, w3, w_proj, w_fc1.T, w_fc2, spot)
        got = attn_forward(True, inputs, masked, key_valid, rel_index, vec, heads, extra, rp, keys, depth)
        normed, q, k, v, p, att, attn, res, n2, w, wp, w1, w2, b1 = got
        w1, w2, b1 = w1.reshape(ff, width), w2.reshape(ff, width), b1.reshape(1, ff)
    else:
        w = lax.all_gather(w3, "head", axis=2, tiled=True)
        wp = lax.all_gather(w_proj, "head", axis=0, tiled=True)
        w1 = lax.all_gather(w_fc1.T, ("dp", "head"), axis=0, tiled=True)
        w2 = lax.all_gather(w_fc2, ("dp", "head"), axis=0, tiled=True)
        b1 = lax.all_gather(fc1_bias, ("dp", "head"), axis=0, tiled=True).astype(F32)[None]
        extra = (lax.all_gather(mix, "head", axis=0), w, wp)
        got = attn_forward(False, inputs, masked, key_valid, rel_index, vec, heads, extra, rp, keys, depth)
        normed, q, k, v, p, att, attn, res, n2 = got

    steps = 4
    got = mlp(direct, n2, res, attn, cotangent, vec, b1, w1, w2, steps)
    gb1, out, dres, dproj, s2 = got[-5:]
    args = (inputs, masked, rel_index, vec, w, wp, normed, q, k, v, p, att, dres, dproj)
    if direct:
        extra = got[:3] + (s2, gb1.reshape(-1, width))
        gx, full, gff, small = attn_backward(True, args, heads, extra, rp, keys, depth)
        g_fc1, g_fc2 = gff[0], gff[1]
        full = full.reshape(4, width, -1).astype(F32)
        g_qkv, g_proj = full[:3], full[3].T
        s1, s2 = small[:8], small[8:16]
        wide = width // LANES
        tall = heads * 8 // wide
        table = jnp.transpose(small[16:16 + tall].reshape(tall, wide, LANES), (1, 0, 2)).reshape(heads, -1)
        g_b1 = small[16 + tall:].reshape(-1)
    else:
        ga, gb = got[:2]
        gx, gw, gt, s1 = attn_backward(False, args, heads, (), rp, keys, depth)
        g_fc1 = lax.psum_scatter(ga.astype(F32), ("dp", "head"), scatter_dimension=0, tiled=True)
        g_fc2 = lax.psum_scatter(gb.astype(F32), ("dp", "head"), scatter_dimension=0, tiled=True)
        full = lax.psum(lax.psum_scatter(gw.astype(F32), "head", scatter_dimension=0, tiled=True), "dp")
        full = jnp.transpose(full, (1, 2, 0, 3)).reshape(4, width, -1)
        g_qkv, g_proj = full[:3], full[3].T
        s1, s2, table, g_b1 = lax.psum((s1, s2, gt.reshape(heads, -1), gb1.reshape(-1)), ("dp", "head"))
    g_table = lax.dynamic_slice_in_dim(table, head * (heads // hn), heads // hn, 0)[:, :entries].T
    g_b1 = lax.dynamic_slice_in_dim(g_b1, (me * hn + head) * share, share)
    g_qvb = lax.dynamic_slice_in_dim(s1[T_QB:T_VB + 1], head * (width // hn), width // hn, 1)
    return (
        out, gx, s1[T_MASK], s1[T_LG1], s1[T_LB1], jnp.transpose(g_qkv, (1, 0, 2)), g_qvb, g_table, g_proj,
        s2[S_PB], s2[S_GA1], s2[S_LG2], s2[S_LB2], g_fc1.T, g_b1, g_fc2, s2[S_FB2], s2[S_GA2],
    )


def solution(mesh):
    in_specs = (
        P(("dp", "head"), None, None),
        P(("dp", "head"), None),
        P("dp", None),
        P(),
        P(),
        P(),
        P(),
        P(None, None, "head"),
        P(None, "head"),
        P(None, "head"),
        P("head", None),
        P(),
        P(),
        P(),
        P(),
        P(None, ("dp", "head")),
        P(("dp", "head")),
        P(("dp", "head"), None),
        P(),
        P(),
        P(("dp", "head"), None, None),
    )
    out_specs = (
        P(("dp", "head"), None, None),
        P(("dp", "head"), None, None),
        P(),
        P(),
        P(),
        P(None, None, "head"),
        P(None, "head"),
        P(None, "head"),
        P("head", None),
        P(),
        P(),
        P(),
        P(),
        P(None, ("dp", "head")),
        P(("dp", "head")),
        P(("dp", "head"), None),
        P(),
        P(),
    )
    return jax.shard_map(shards, mesh=mesh, in_specs=in_specs, out_specs=out_specs, check_vma=False)
```

time: 763 us -> 261 us (0.34); the launches traced: 752 us -> 261 us
  matrix products: 252 us -> 0 us
  Pallas kernels: 0 us -> 232 us
  waiting for transfers between devices: 197 us -> 0 us
  blocking collectives: 161 us -> 0 us
  local copies, waits for them, and re-layouts: 82.8 us -> 23 us
  other arithmetic: 39 us -> 4.66 us
  between operations: 17.7 us -> 0.75 us
    dot_general x48 -> x0, matrix products: 252 us -> none  [the longest x8 67.8 us: table_grad(): jnp.einsum('hn,nr->rh', columns, selector, precision=highest, preferred_e...]
    pallas_call x0 -> x3, Pallas kernels: none -> 232 us  [the longest x1 106 us: attn_backward(): pl.pallas_call(functools.partial(attn_backward_kernel, direct), name='att...]
    psum x2 -> x0, blocking collectives: 118 us -> none  [the longest x1 78.8 us: reduce_end(): summed_dp = lax.psum((g_qkv, g_qvb, g_table, g_proj), 'dp')]
    all_gather x6 -> x0, waiting for transfers between devices: 108 us -> none  [the longest x1 57.9 us: shards(): lax.all_gather(w_fc2, ('dp', 'head'), axis=0, tiled=True)]
    reduce_scatter x6 -> x0, waiting for transfers between devices: 88.2 us -> none  [the longest x1 65.8 us: reduce_end(): lax.psum_scatter(g_fc2, ('dp', 'head'), scatter_dimension=0, tiled=True)]
    unnamed x1 -> x0, blocking collectives: 43.3 us -> none
    reduce_sum x19 -> x0, other arithmetic: 28.4 us -> none  [the longest x5 10.1 us: layer_norm(): return center * lax.rsqrt(spread + epsilon) * scale_vec + offset_vec]
    slice x12 -> x5, local copies, waits for them, and re-layouts: 21.2 us -> 0.75 us  [the longest x1 0.66 us: shards(): s2[S_GA2]]
  transfers between devices with their start and end apart: 13 -> 0, of which waited for: 8 -> 0; matrix products, arithmetic and copies ran while one was open for 27% -> 0% of each run, Pallas kernels for 0% -> 0%
where the time goes in v2:
time: 261 us
  Pallas kernels  232 us (89%)
  local copies, waits for them, and re-layouts  23 us (9%)
  other arithmetic  4.66 us (2%)
    pallas_call x1, Pallas kernels, attn_backward(): pl.pallas_call(functools.partial(attn_backward_kernel, direct), name='att...  106 us
    pallas_call x1, Pallas kernels, attn_forward(): pl.pallas_call(functools.partial(attn_forward_kernel, direct), name='attn...  63.7 us
    pallas_call x1, Pallas kernels, mlp(): pl.pallas_call(functools.partial(mlp_kernel, direct), name='mlp', grid=(s...  63 us
    unnamed x21, local copies, waits for them, and re-layouts  13.5 us

profile of v2, /device:TPU:0, one launch (start us, length us, event | category | flops | bytes accessed | tf_op | source)
XLA Modules:
  0.0 260.6 jit_solution(11491831578409527773)
XLA Ops:
  1.4 0.7 fusion.1.refs_10_
  2.1 0.7 constant_dynamic-update-slice_fusion.8
  2.8 0.7 constant_dynamic-update-slice_fusion.7
  3.5 0.7 constant_dynamic-update-slice_fusion.6
  4.2 0.7 constant_dynamic-update-slice_fusion.5
  4.9 0.7 constant_dynamic-update-slice_fusion.4
  5.6 0.7 constant_dynamic-update-slice_fusion.3
  6.3 0.7 constant_dynamic-update-slice_fusion.2
  6.9 0.7 constant_dynamic-update-slice_fusion.1
  7.6 0.7 constant_dynamic-update-slice_fusion
  9.0 0.7 pad.4
  9.7 0.7 reshape.73
  11.0 63.7 %attn_forward.1 = (bf16[832,768]{1,0:T(8,128)(2,1)}, bf16[4,208,768]{2,1,0:T(8,128)(2,1)}, bf16[4,256,768]{2,1,0:T(8,128)(2,1)}, bf16[4,256,768]{2,1,0:T(8,128)(...) custom-call(bf16[4,200,768]{2,1,0:T(8,128)(2,1)} %refs_0_.3, ...), custom_call_target="tpu_custom_call" | custom-call | tf_op jit(solution)/shard_map/attn_forward/pallas_call | solution.py:614
  74.7 1.3 copy.45
  76.1 63.0 %mlp.1 = (bf16[2,96,768]{2,1,0:T(8,128)(2,1)}, bf16[2,2,2,2,96,768]{5,4,3,2,1,0:T(8,128)(2,1)}, f32[2,96,768]{2,1,0:T(8,128)}, f32[1,3072]{1,0:T(1,128)}, bf16[4...) custom-call(bf16[832,768]{1,0:T(8,128)(2,1)} %get-tuple-element.44.refs_0_, ...), custom_call_target="tpu_custom_call" | custom-call | tf_op jit(solution)/shard_map/mlp/pallas_call | solution.py:810
  139.6 1.4 reduce.21
  141.6 105.6 %attn_backward.1 = (f32[4,200,768]{2,1,0:T(8,128)}, bf16[2,2,4,2,2,48,384]{6,5,4,3,2,1,0:T(8,128)(2,1)}, f32[2,96,768]{2,1,0:T(8,128)}, f32[36,768]{1,0:T(8,128)}) custom-call(bf16[4,200,768]{2,1,0:T(8,128)(2,1)} %refs_0_.3, s32[4,200]{1,0:T(4,128)} %refs_1_.3, s32[200,200]{1,0:T(8,128)} %refs_2_.3, f32[16,768]{1,0:T(8,128)} %reshape.71.refs_4_.refs_3_, ...), custom_call_target="tpu_custom_call" | custom-call | tf_op jit(solution)/shard_map/attn_backward/pallas_call | solution.py:1114
  247.1 2.0 convert.1
  249.1 2.0 slice_bitcast_fusion
  251.1 0.8 copy-done
  252.0 1.4 copy.44
  253.4 0.8 slice_bitcast_fusion.1
  256.8 2.4 copy.58
  259.2 1.4 copy.59
  (29 shorter events, 5.7 us)
Async XLA Ops:
  249.1 2.8 %copy-start = (bf16[2,2,4,2,2,48,384]{6,5,4,3,2,1,0:T(8,128)(2,1)S(1)}, bf16[2,2,4,2,2,48,384]{6,5,4,3,2,1,0:T(8,128)(2,1)}, u32[]{:S(2)}) copy-start(bf16[2,2,4,2,2,48,384]{6,5,4,3,2,1,0:T(8,128)(2,1)} %get-tuple-element.68) | copy-start | bytes 7077892
  251.9 1.5 copy-start.2
  252.0 2.3 copy-start.3
  253.4 5.8 %copy-start.1 = (f32[4,200,768]{2,1,0:T(8,128)S(1)}, f32[4,200,768]{2,1,0:T(8,128)}, u32[]{:S(2)}) copy-start(f32[4,200,768]{2,1,0:T(8,128)} %get-tuple-element.100) | copy-start | bytes 7372804

commit v3 on v2

v3 whole, which is shorter than its diff:
```python
import functools
import types
import jax
import jax.numpy as jnp
from jax import lax
from jax.experimental import pallas as pl
from jax.experimental.pallas import tpu as pltpu
from jax.sharding import PartitionSpec as P

F32 = jnp.float32
BF16 = jnp.bfloat16
EPS = 1e-06
LANES = 128
S_GA2, S_FB2, S_LG2, S_LB2, S_GA1, S_PB = range(6)
T_MASK, T_LG1, T_LB1, T_QB, T_VB = range(5)


def dot(a, b):
    return jnp.dot(a, b, preferred_element_type=F32)


def dot_nt(a, b):
    return lax.dot_general(a, b, (((1,), (1,)), ((), ())), preferred_element_type=F32)


def dot_tn(a, b):
    return lax.dot_general(a, b, (((0,), (0,)), ((), ())), preferred_element_type=F32)


def norm_parts(v):
    c = v - jnp.mean(v, axis=-1, keepdims=True)
    r = lax.rsqrt(jnp.mean(c * c, axis=-1, keepdims=True) + EPS)
    return c * r, r


def norm_back(n, r, y, gain):
    yg = y * gain
    return r * (
        yg - jnp.mean(yg, axis=-1, keepdims=True) - n * jnp.mean(yg * n, axis=-1, keepdims=True)
    )


def low_half(shape):
    return lax.broadcasted_iota(jnp.int32, shape, 1) < (LANES // 2)

MESHID = pl.DeviceIdType.MESH


def here():
    dp = lax.axis_index("dp")
    return dp // 4, (dp // 2) % 2, dp % 2, lax.axis_index("head")


def at_dp(z, y, x):
    return {"dp": (z * 2 + y) * 2 + x}


def greet(depth):
    z, y, x, head = here()
    found = [at_dp(z, y, 1 - x), at_dp(z, 1 - y, x), {"head": 1 - head}]
    found += [at_dp((z + k) % depth, y, x) for k in range(1, depth)]
    barrier = pltpu.get_barrier_semaphore()
    for dev in found:
        pl.semaphore_signal(barrier, inc=1, device_id=dev, device_id_type=MESHID)
    pl.semaphore_wait(barrier, len(found))


class Wire:
    def __init__(self, send, recv):
        self.send, self.recv, self.next, self.open = send, recv, 0, []

    def slot(self):
        self.next += 1
        return self.next - 1

    def copy(self, i, src, dst, dev):
        return pltpu.make_async_remote_copy(
            src_ref=src, dst_ref=dst, send_sem=self.send.at[i], recv_sem=self.recv.at[i],
            device_id=dev, device_id_type=MESHID,
        )

    def start(self, i, make):
        self.copy(i, *make()).start()
        self.open.append((i, make))

    def arrived(self, i, ref, dev):
        self.copy(i, ref, ref, dev).wait_recv()

    def sent(self):
        for i, make in self.open:
            self.copy(i, *make()).wait_send()
        self.open = []


class Local:
    def __init__(self, sems):
        self.sems, self.next, self.open = sems, 0, []

    def start(self, make):
        i = self.next
        self.next += 1
        pltpu.make_async_copy(*make(), self.sems.at[i]).start()
        wait = lambda: pltpu.make_async_copy(*make(), self.sems.at[i]).wait()
        self.open.append(wait)
        return wait


def hops(p, y, x):
    ey, ex = (1 - y, x), (y, 1 - x)
    return (ey, ex) if p == 0 else (ex, ey)


def gather_stages(wire, depth, own, slot, column=None):
    z, y, x, head = here()
    ids = {}
    for p in range(2):
        for k in range(depth):
            for kind in "zabc":
                ids[p, kind, k] = wire.slot()
        for kind in range(0 if column is None else 4):
            ids[p, "s", kind] = wire.slot()
    up = lambda k: (z + k) % depth
    down = lambda k: (z + depth - k) % depth

    def columns(p):
        (ay, ax), (by, bx) = hops(p, y, x)
        return (y, x), (ay, ax), (by, bx), (1 - y, 1 - x)

    def send_up(p, k):
        wire.start(ids[p, "z", k], lambda: (own(p), slot(p, z, y, x), at_dp(up(k), y, x)))

    def send_square(p, k, kind, col, to, first=False):
        def make():
            cs = columns(p)
            dst = slot(p, down(k), *cs[col])
            return own(p) if first else dst, dst, at_dp(z, *cs[to])
        wire.start(ids[p, kind, k], make)

    def wait(p, k, kind, col, frm):
        cs = columns(p)
        dev = at_dp(down(k), y, x) if frm is None else at_dp(z, *cs[frm])
        wire.arrived(ids[p, kind, k], slot(p, down(k), *cs[col]), dev)

    def begin():
        for k in range(1, depth):
            for p in range(2):
                send_up(p, k)
        for p in range(2):
            send_square(p, 0, "a", 0, 1, True)
            send_square(p, 0, "b", 0, 2, True)

    def from_column(k):
        for p in range(2):
            wait(p, k, "z", 0, None)
            send_square(p, k, "a", 0, 1)
            send_square(p, k, "b", 0, 2)

    def from_first(k):
        for p in range(2):
            wait(p, k, "a", 1, 1)
            send_square(p, k, "c", 1, 2)

    def from_second(kind, col):
        for p in range(2):
            for k in range(depth):
                wait(p, k, kind, col, 2)

    def across(which):
        for p in range(2):
            def make(p=p):
                block = column(p, *columns(p)[which], head)
                return block, block, {"head": 1 - head}
            wire.start(ids[p, "s", which], make)

    def crossed():
        for which in range(4):
            for p in range(2):
                wire.arrived(ids[p, "s", which], column(p, *columns(p)[which], 1 - head), {"head": 1 - head})

    part = functools.partial
    stages = {"begin": begin, "b": part(from_second, "b", 2), "c": part(from_second, "c", 3), "crossed": crossed}
    for k in range(depth):
        stages["z%d" % k] = part(from_column, k)
        stages["a%d" % k] = part(from_first, k)
        stages["s%d" % k] = part(across, k)
    return stages


def add_into(dst, src):
    dst[...] = (dst[...].astype(F32) + src[...].astype(F32)).astype(dst.dtype)


class SquareSum:
    def __init__(self, wire, theirs, mine, pair_in, square_in, line_in):
        self.wire, self.theirs, self.mine = wire, theirs, mine
        self.pair_in, self.square_in, self.line_in = pair_in, square_in, line_in
        self.ids = {(p, kind): wire.slot() for p in range(2) for kind in "hab"}
        self.place = here()

    def devices(self, p):
        z, y, x, head = self.place
        ex, ey = at_dp(z, y, 1 - x), at_dp(z, 1 - y, x)
        return (ex, ey) if p == 0 else (ey, ex)

    def copy(self, p, kind):
        z, y, x, head = self.place
        if kind == "h":
            src, dst, dev = self.theirs(p), self.pair_in(p), {"head": 1 - head}
        elif kind == "a":
            src = self.mine(p, None, 1 - x) if p == 0 else self.mine(p, 1 - y, None)
            dst, dev = self.square_in(p), self.devices(p)[0]
        else:
            src = self.mine(p, 1 - y, x) if p == 0 else self.mine(p, y, 1 - x)
            dst, dev = self.line_in(p), self.devices(p)[1]
        return self.wire.copy(self.ids[p, kind], src, dst, dev)

    def pair(self):
        for p in range(2):
            self.copy(p, "h").start()

    def first(self):
        for p in range(2):
            self.wire.arrived(self.ids[p, "h"], self.pair_in(p), {"head": 1 - self.place[3]})
            add_into(self.mine(p, None, None), self.pair_in(p))
            self.copy(p, "a").start()

    def second(self):
        z, y, x, head = self.place
        for p in range(2):
            self.wire.arrived(self.ids[p, "a"], self.square_in(p), self.devices(p)[0])
            add_into(self.mine(p, None, x) if p == 0 else self.mine(p, y, None), self.square_in(p))
            self.copy(p, "b").start()

    def third(self):
        z, y, x, head = self.place
        for p in range(2):
            self.wire.arrived(self.ids[p, "b"], self.line_in(p), self.devices(p)[1])
            add_into(self.mine(p, y, x), self.line_in(p))

    def sent(self):
        for p in range(2):
            for kind in "hab":
                self.copy(p, kind).wait_send()


class ColumnSum:
    def __init__(self, wire, depth, part, column_in):
        self.wire, self.depth, self.part, self.column_in = wire, depth, part, column_in
        self.ids = {(p, k): wire.slot() for p in range(2) for k in range(1, depth)}
        self.place = here()

    def send(self, k):
        def make(p):
            z, y, x, head = self.place
            to = (z + self.depth - k) % self.depth
            return self.part(p, to), self.column_in(p, k), at_dp(to, y, x)

        for p in range(2):
            self.wire.start(self.ids[p, k], functools.partial(make, p))

    def total(self, p):
        z, y, x, head = self.place
        acc = self.part(p, z)[...].astype(F32)
        for k in range(1, self.depth):
            back = at_dp((z + k) % self.depth, y, x)
            self.wire.arrived(self.ids[p, k], self.column_in(p, k), back)
            acc = acc + self.column_in(p, k)[...].astype(F32)
        return acc


class SmallSum:
    def __init__(self, wire, depth, bufs, line):
        self.wire, self.depth, self.bufs, self.line = wire, depth, bufs, line
        self.ids = [wire.slot() for _ in range(2 + depth)]
        self.place = here()

    def devices(self):
        z, y, x, head = self.place
        return [{"head": 1 - head}, at_dp(z, y, 1 - x), at_dp(z, 1 - y, x)]

    def send(self, n):
        self.wire.start(self.ids[n], lambda: (self.bufs.at[2 * n], self.bufs.at[2 * n + 1], self.devices()[n]))

    def take(self, n):
        self.wire.arrived(self.ids[n], self.bufs.at[2 * n + 1], self.devices()[n])
        self.bufs[2 * n + 2] = self.bufs[2 * n] + self.bufs[2 * n + 1]

    def begin(self):
        self.send(0)

    def middle(self, n):
        self.take(n - 1)
        self.send(n)

    def column(self):
        z, y, x, head = self.place
        self.take(2)
        self.line[z] = self.bufs[6]
        for k in range(1, self.depth):
            self.wire.start(
                self.ids[2 + k],
                lambda k=k: (self.bufs.at[6], self.line.at[z], at_dp((z + k) % self.depth, y, x)),
            )

    def result(self):
        z, y, x, head = self.place
        for k in range(1, self.depth):
            back = (z + self.depth - k) % self.depth
            self.wire.arrived(self.ids[2 + k], self.line.at[back], at_dp(back, y, x))
        total = self.line[0]
        for n in range(1, self.depth):
            total = total + self.line[n]
        return total


def bind(names, refs):
    assert len(names) == len(refs)
    return types.SimpleNamespace(**dict(zip(names, refs)))


def spread_mask(masked, tmp, ch):
    images, rows = masked.shape
    tmp[...] = jnp.zeros_like(tmp)
    tmp[0:images, 0:rows] = masked[...].astype(F32)
    turned = tmp[...].T
    for i in range(images):
        ch[i] = turned[0:rows, i:i + 1]


def pad_index(raw, idx):
    idx[...] = jnp.zeros_like(idx)
    idx[0:raw.shape[0], 0:raw.shape[1]] = raw[...]


def run_all(stages):
    for stage in stages:
        stage()


def vmem(n):
    return [pl.BlockSpec(memory_space=pltpu.VMEM)] * n

ANY = pl.BlockSpec(memory_space=pl.ANY)
sd = jax.ShapeDtypeStruct
dma = lambda n: pltpu.SemaphoreType.DMA((n,))
VECTORS = ("mask_token", "ln1_gain", "ln1_bias", "proj_bias", "gamma1", "ln2_gain", "ln2_bias", "fc2_bias", "gamma2")
GIVEN = ("x", "masked", "kv", "raw") + VECTORS + ("cot",)
KEPT = (
    "idx", "valid", "tmp", "ch", "bias", "nt", "q", "k", "v", "att", "res", "n2", "db", "act", "dpre", "dn",
    "small1", "small2", "gb1", "lsem",
)
SHARED = (
    "w", "wp", "mix", "b1", "b1line", "g", "pair_in", "square_in", "line_in", "column", "column_in",
    "ar_pair", "ar_square", "ar_line", "ar_column", "gathered", "bufs", "line", "send", "recv",
)


class Row:
    def __init__(self, ref):
        self.ref = ref

    def __getitem__(self, at):
        return self.ref[...].reshape(1, -1)


def layer_kernel(direct, *refs):
    if direct:
        names = GIVEN + ("mixown", "wown", "wpown", "own1", "own2", "spot")
        names += ("out", "gx", "p", "w1", "w2", "full", "gff", "small") + KEPT + SHARED
    else:
        names = GIVEN + ("mix", "w", "wp", "w1", "w2", "b1")
        names += ("out", "gx", "p", "g1", "g2", "gw", "gt", "small1_out", "small2_out", "gb1_out") + KEPT
    r = bind(names, refs)
    for name in VECTORS:
        setattr(r, name, Row(getattr(r, name)))
    images, rows, width = r.x.shape
    heads, rp, keys = r.bias.shape
    flat = images * rp
    scale = (width // heads) ** -0.5
    pairs, per = heads // 2, heads // 4
    steps, block = r.b1.shape[-2:]
    own_heads = heads // r.mix.shape[0]
    own_tiles = width // r.mix.shape[0] // LANES
    chunks = (r.mix.shape[1] - 2 * own_tiles) // own_heads
    local = Local(r.lsem)
    z, y, x, head = here()
    plan = {}
    part = functools.partial
    every = lambda v: slice(None) if v is None else v
    level = lambda b: (z + 2 * steps - 1 - b) % steps
    at_image = lambda i: pl.multiple_of(i * rp, 16)

    if direct:
        depth = r.w1.shape[0]
        half = r.wown.shape[2]
        lanes_of = lambda hd: pl.ds(pl.multiple_of(hd * half, LANES), half)
        full = (r.w1, r.w2)
        wire = Wire(r.send, r.recv)
        greet(depth)
        other = {"head": 1 - head}
        swaps = [
            (r.mixown, lambda hd: r.mix.at[hd]),
            (r.wown, lambda hd: r.w.at[:, :, lanes_of(hd)]),
            (r.wpown, lambda hd: r.wp.at[lanes_of(hd)]),
        ]
        swap_ids = [wire.slot() for _ in swaps]
        for i, (src, place) in zip(swap_ids, swaps):
            wire.start(i, lambda src=src, place=place: (src, place(head), other))
        for src, place in swaps:
            local.start(lambda src=src, place=place: (src, place(head)))
        slot = lambda p, zz, yy, xx: full[p].at[zz, yy, xx, head]
        own = (r.own1, r.own2)
        for p in range(2):
            local.start(lambda p=p: (own[p], slot(p, z, y, x)))
        r.b1[0] = r.spot[...]
        bias_sum = SmallSum(wire, depth, r.b1, r.b1line)
        ag = gather_stages(
            wire, depth, own=lambda p: own[p], slot=slot,
            column=lambda p, yy, xx, hd: full[p].at[:, yy, xx, hd],
        )
        ag["begin"]()
        bias_sum.begin()
        squares = [
            SquareSum(
                wire,
                theirs=lambda p, b=b: r.g.at[b % 2, p, :, :, 1 - head],
                mine=lambda p, yy, xx, b=b: r.g.at[b % 2, p, every(yy), every(xx), head],
                pair_in=lambda p, b=b: r.pair_in.at[b % 2, p],
                square_in=lambda p, b=b: r.square_in.at[b % 2, p],
                line_in=lambda p, b=b: r.line_in.at[b % 2, p],
            )
            for b in range(steps)
        ]
        column = ColumnSum(wire, depth, part=lambda p, zz: r.column.at[p, zz], column_in=lambda p, k: r.column_in.at[p, k - 1])

        def close(b):
            squares[b].third()
            for p in range(2):
                r.column[p, level(b)] = r.g[b % 2, p, y, x, head]
            if b < steps - 1:
                column.send(b + 1)
            squares[b].sent()

        small = SmallSum(wire, depth, r.bufs, r.line)
        plan = {
            "g1": [ag["z1"], ag["a0"]], "g2": [part(bias_sum.middle, 1)],
            "p1": [ag["z2"], ag["a1"], part(bias_sum.middle, 2)],
            "t1": [ag["z3"], ag["a2"], ag["s0"], bias_sum.column], "t4": [ag["a3"], ag["s1"]],
            "t5": [ag["b"], ag["s2"]], "t6": [ag["c"], ag["s3"]],
        }

    def tick(point):
        run_all(plan.get(point, ()))

    def tick_in(step, point):
        for key, stages in plan.items():
            if isinstance(key, tuple) and key[1] == point:
                pl.when(step == key[0])(part(run_all, stages))

    spread_mask(r.masked, r.tmp, r.ch)
    pad_index(r.raw, r.idx)
    r.valid[...] = jnp.zeros_like(r.valid)
    r.valid[0:r.kv.shape[0], 0:rows] = r.kv[...]

    def hidden_of(i):
        ch = r.ch[i]
        return r.x[i].astype(F32) * (1.0 - ch) + ch * r.mask_token[...]

    def attention_forward(normed, pring):
        normed[...] = jnp.zeros_like(normed)
        r.n2[...] = jnp.zeros_like(r.n2)
        r.res[...] = jnp.zeros_like(r.res)

        def first_norm(i, carry):
            n, _ = norm_parts(hidden_of(i))
            normed[pl.ds(at_image(i), rows), :] = (n * r.ln1_gain[...] + r.ln1_bias[...]).astype(BF16)
            return carry

        lax.fori_loop(0, images, first_norm, 0)
        if direct:
            for wait in local.open:
                wait()
            local.open = []
            wire.arrived(swap_ids[0], swaps[0][1](1 - head), other)

        def gather_head(h, carry):
            for side in range(keys // LANES):
                idx = r.idx[:, side * LANES:(side + 1) * LANES]
                low = idx & (LANES - 1)
                high = idx >> 7
                acc = jnp.zeros(idx.shape, F32)
                for c in range(chunks):
                    row = r.mix[h // own_heads, pl.ds((h % own_heads) * chunks + c, 1), :]
                    got = jnp.take_along_axis(jnp.broadcast_to(row, idx.shape), low, axis=1)
                    acc = jnp.where(high == c, got, acc)
                r.bias[h, :, side * LANES:(side + 1) * LANES] = acc
            return carry

        for n in range(3):
            lax.fori_loop(n * heads // 3, (n + 1) * heads // 3, gather_head, 0)
            tick("g%d" % n)
        if direct:
            for n in (1, 2):
                wire.arrived(swap_ids[n], swaps[n][1](1 - head), other)
        zeros_tail = jnp.zeros((images, keys - rp, width), BF16)
        r.k[:, rp:, :] = zeros_tail
        r.v[:, rp:, :] = zeros_tail

        def bias_row(kind, nb):
            tiles = []
            for t in (2 * nb, 2 * nb + 1):
                at = own_heads * chunks + kind * own_tiles + t % own_tiles
                tiles.append(r.mix[t // own_tiles, at:at + 1, :])
            return jnp.concatenate(tiles, axis=1)

        for c, (dst, kind) in enumerate(((r.q, 0), (r.k, None), (r.v, 1))):
            for nb in range(width // 256):
                cols = slice(nb * 256, (nb + 1) * 256)
                acc = dot(normed[...], r.w[c, :, cols])
                if kind is not None:
                    acc = acc + bias_row(kind, nb)
                acc = acc.astype(BF16)
                for i in range(images):
                    dst[i, :rp, cols] = acc[i * rp:(i + 1) * rp]
            tick("p%d" % c)
        r.nt[...] = normed[...].T

        def attend(t, carry):
            i = t // pairs
            j = t % pairs
            lanes = pl.ds(pl.multiple_of(j * LANES, LANES), LANES)
            qp = r.q[i, :, lanes]
            kp = r.k[i, :, lanes]
            vp = r.v[i, :, lanes]
            lo = low_half((rp, LANES))
            ok = r.valid[pl.ds(head * images + i, 1), :] > 0
            outs = []
            for s in range(2):
                qs = jnp.where(lo if s == 0 else jnp.logical_not(lo), qp, jnp.zeros_like(qp))
                sc = dot_nt(qs, kp) * scale + r.bias[2 * j + s]
                sc = jnp.where(ok, sc, -1e30)
                e = jnp.exp(sc - jnp.max(sc, axis=-1, keepdims=True))
                prob = e * (1.0 / jnp.sum(e, axis=-1, keepdims=True))
                pring[i % 2, 2 * j + s] = prob
                outs.append(dot(prob.astype(BF16), vp))
            r.att[pl.ds(at_image(i), rp), lanes] = jnp.where(lo, outs[0], outs[1]).astype(BF16)
            return carry

        stored = {}
        for n in range(2 * images):
            i = n // 2
            if n % 2 == 0 and i >= 2:
                stored[i - 2]()
            lax.fori_loop(n * pairs // 2, (n + 1) * pairs // 2, attend, 0)
            if n % 2:
                stored[i] = local.start(lambda i=i: (pring.at[i % 2], r.p.at[i]))
            tick("t%d" % n)

        def finish(i, carry):
            branch = dot(r.att[pl.ds(at_image(i), rp), :], r.wp[...]) + r.proj_bias[...]
            res = hidden_of(i) + r.gamma1[...] * branch[:rows]
            r.res[pl.ds(at_image(i), rows), :] = res
            n, _ = norm_parts(res)
            r.n2[pl.ds(at_image(i), rows), :] = (n * r.ln2_gain[...] + r.ln2_bias[...]).astype(BF16)
            return carry

        lax.fori_loop(0, images, finish, 0)
        stored[images - 2]()
        stored[images - 1]()

    pl.run_scoped(attention_forward, pltpu.VMEM((flat, width), BF16), pltpu.VMEM((2, heads, rp, keys), F32))

    if direct:
        ag["crossed"]()
        r.b1[1] = bias_sum.result()
        plan = {
            (0, 4): [squares[0].pair],
            (1, 1): [squares[0].first], (1, 4): [squares[1].pair, squares[0].second],
            (2, 1): [squares[1].first], (2, 2): [part(close, 0)], (2, 4): [squares[2].pair, squares[1].second],
            (3, 1): [squares[2].first], (3, 2): [part(close, 1)], (3, 4): [squares[3].pair, squares[2].second],
        }

    def feed_forward(cot, out, branch, slots, sems):
        def weights(b, into):
            copies = []
            for p, src in enumerate((r.w1, r.w2)):
                if direct:
                    view = src.at[level(b)]
                else:
                    view = src.at[pl.ds(pl.multiple_of(level(b) * block, 16), block)]
                copies.append(pltpu.make_async_copy(view, slots.at[into, p], sems.at[into, p]))
            return copies

        for copy in weights(0, 0):
            copy.start()
        fetch = pltpu.make_async_copy(r.cot, cot, sems.at[2, 0])
        fetch.start()
        r.db[...] = jnp.zeros_like(r.db)
        branch[...] = jnp.zeros_like(branch)
        r.dn[...] = jnp.zeros_like(r.dn)
        fetch.wait()

        def fill(i, carry):
            r.db[pl.ds(at_image(i), rows), :] = (cot[i].astype(F32) * r.gamma2[...]).astype(BF16)
            return carry

        lax.fori_loop(0, images, fill, 0)

        def step(b, carry):
            slot = b % 2
            t = level(b)
            for copy in weights(b, slot):
                copy.wait()

            @pl.when(b + 1 < steps)
            def _():
                for copy in weights(b + 1, 1 - slot):
                    copy.start()

            w1 = lambda: slots[slot, 0].reshape(block, width)
            w2 = lambda: slots[slot, 1].reshape(block, width)
            b1 = r.b1[1, pl.ds(t, 1), :] if direct else r.b1[pl.ds(t, 1), :]

            def tile(i, gb1):
                at = pl.ds(at_image(i), rp)
                pre = dot_nt(r.n2[at, :], w1()) + b1
                cdf = 0.5 * (1.0 + lax.erf(pre * 0.7071067811865476))
                slope = cdf + pre * (0.3989422804014327 * jnp.exp(-0.5 * pre * pre))
                act = (pre * cdf).astype(BF16)
                r.act[at, :] = act
                dpre = (dot_nt(r.db[at, :], w2()) * slope).astype(BF16)
                r.dpre[at, :] = dpre
                branch[at, :] += dot(act, w2())
                r.dn[at, :] += dot(dpre, w1())
                return gb1 + jnp.sum(dpre.astype(F32), axis=0, keepdims=True)

            gb1 = lax.fori_loop(0, images // 2, tile, jnp.zeros((1, block), F32))
            tick_in(b, 1)
            r.gb1[pl.ds(t, 1), :] = lax.fori_loop(images // 2, images, tile, gb1)
            tick_in(b, 2)

            def store(p, value):
                value = value.astype(BF16)
                if direct:
                    r.g[slot, p] = value.reshape(r.g.shape[2:])
                else:
                    slots[slot, p] = value
                    dst = (r.g1, r.g2)[p].at[pl.ds(pl.multiple_of(t * block, 16), block)]
                    copy = pltpu.make_async_copy(slots.at[slot, p], dst, sems.at[3, p])
                    copy.start()
                    copy.wait()

            second = dot_tn(r.act[...], r.db[...])
            store(1, second)
            tick_in(b, 3)
            store(0, dot_tn(r.dpre[...], r.n2[...]))
            tick_in(b, 4)
            return carry

        lax.fori_loop(0, steps, step, 0)
        r.small2[...] = jnp.zeros_like(r.small2)
        r.n2[...] = jnp.zeros_like(r.n2)

        def add(row, value):
            r.small2[row:row + 1, :] += jnp.sum(value, axis=0, keepdims=True)

        def finish(i, carry):
            span = pl.ds(at_image(i), rows)
            up = cot[i].astype(F32)
            mlp = branch[span, :] + r.fc2_bias[...]
            res = r.res[span, :]
            out[i] = (res + r.gamma2[...] * mlp).astype(BF16)
            add(S_GA2, up * mlp)
            add(S_FB2, (up * r.gamma2[...]).astype(BF16).astype(F32))
            n, inv = norm_parts(res)
            dn = r.dn[span, :]
            add(S_LG2, dn * n)
            add(S_LB2, dn)
            dres = up + norm_back(n, inv, dn, r.ln2_gain[...])
            add(S_GA1, dres * (res - hidden_of(i)))
            r.res[span, :] = dres
            dproj = (dres * r.gamma1[...]).astype(BF16)
            r.n2[span, :] = dproj
            add(S_PB, dproj.astype(F32))
            return carry

        lax.fori_loop(0, images, finish, 0)
        r.small2[S_GA1:S_GA1 + 1, :] = r.small2[S_GA1:S_GA1 + 1, :] / r.gamma1[...]
        store_out = pltpu.make_async_copy(out, r.out, sems.at[2, 1])
        store_out.start()
        store_out.wait()

    if direct:
        slots_shape = (2, 2) + r.w1.shape[1:]
    else:
        slots_shape = (2, 2, block, width)
    pl.run_scoped(
        feed_forward, pltpu.VMEM(r.cot.shape, BF16), pltpu.VMEM(r.cot.shape, BF16), pltpu.VMEM((flat, width), F32),
        pltpu.VMEM(slots_shape, BF16), pltpu.SemaphoreType.DMA((4, 2)),
    )
    plan = {}

    def attention_backward(pbuf, dpt, dv_all, g, sems):
        nonlocal plan
        dqkv = (r.act, r.dpre, dv_all)
        pair_of = lambda s: (s % 2) * per + s // 2

        def fetch(s, into):
            src = r.p.at[:, pl.ds(2 * pair_of(s), 2)]
            return pltpu.make_async_copy(src, pbuf.at[into], sems.at[into])

        fetch(0, 0).start()
        if direct:
            ar, lines, gathers = [], [], []
            for m in range(per):
                ar.append(SquareSum(
                    wire,
                    theirs=lambda p, m=m: g.at[m, 1 - head, p],
                    mine=lambda p, yy, xx, m=m: g.at[m, head, p, :, :, every(yy), every(xx)],
                    pair_in=lambda p, m=m: r.ar_pair.at[m, p],
                    square_in=lambda p, m=m: r.ar_square.at[m, p], line_in=lambda p, m=m: r.ar_line.at[m, p],
                ))
                lines.append(ColumnSum(
                    wire, depth, part=lambda p, zz, m=m: g.at[m, head, p, :, zz, y, x],
                    column_in=lambda p, k, m=m: r.ar_column.at[m, p, k - 1],
                ))
                lanes_m = slice(m * LANES, (m + 1) * LANES)
                into = lambda p, zz, yy, xx, lanes_m=lanes_m: r.gathered.at[p, :, zz, yy, xx, :, lanes_m]
                gathers.append(gather_stages(wire, depth, own=lambda p, into=into: into(p, z, y, x), slot=into))

            def third(m):
                ar[m].third()
                for k in range(1, depth):
                    lines[m].send(k)

            def last(m):
                for p in range(2):
                    r.gathered[p, :, z, y, x, :, m * LANES:(m + 1) * LANES] = lines[m].total(p).astype(BF16)
                gathers[m]["begin"]()

            def ff_last():
                for p in range(2):
                    r.gff[p] = column.total(p)

            g0, g1, g2 = gathers
            plan = {
                (0, 1): [squares[3].first, part(close, 2)], (0, 4): [squares[3].second], (1, 3): [part(close, 3)],
                (1, 4): [ar[0].pair], (2, 3): [ar[0].first], (3, 4): [ar[1].pair, ar[0].second],
                (4, 3): [ar[1].first], (4, 4): [part(third, 0)],
                (5, 4): [ar[2].pair, ar[1].second, part(last, 0)],
                (5, 6): [ar[2].first, part(third, 1)], (5, 7): [g0["z1"], g0["z2"], g0["z3"]], (5, 8): [part(last, 1)],
                (5, 9): [ar[2].second, g0["a0"], g0["a1"], g0["a2"], g0["a3"]], (5, 10): [g1["z1"], g1["z2"], g1["z3"]],
                (5, 11): [part(third, 2), g0["b"], g0["c"]], (5, 12): [g1["a0"], g1["a1"], g1["a2"], g1["a3"]], (5, 13): [ff_last],
            }

        for i in range(images):
            at = slice(i * rp, (i + 1) * rp)
            r.db[at, :] = dot_nt(r.n2[at, :], r.wp[...]).astype(BF16)
        dpt[...] = r.n2[...].T
        r.small1[...] = jnp.zeros_like(r.small1)

        def step(s, carry):
            j = pair_of(s)
            now = s % 2
            fetch(s, now).wait()

            @pl.when(s + 1 < pairs)
            def _():
                fetch(s + 1, 1 - now).start()

            tick_in(s, 1)
            lanes = pl.ds(pl.multiple_of(j * LANES, LANES), LANES)
            r.bias[2 * j] = jnp.zeros((rp, keys), F32)
            r.bias[2 * j + 1] = jnp.zeros((rp, keys), F32)

            def image(i, carry):
                at = pl.ds(at_image(i), rp)
                qp = r.q[i, :, lanes]
                kp = r.k[i, :, lanes]
                vp = r.v[i, :, lanes]
                da = r.db[at, lanes]
                lo = low_half((rp, LANES))
                dv, dq, dk = [], [], []
                for n in range(2):
                    das = jnp.where(lo if n == 0 else jnp.logical_not(lo), da, jnp.zeros_like(da))
                    prob = pbuf[now, i, n]
                    dp = dot_nt(das, vp)
                    dsc = prob * (dp - jnp.sum(prob * dp, axis=-1, keepdims=True))
                    dsb = dsc.astype(BF16)
                    r.bias[2 * j + n] += dsb.astype(F32)
                    dv.append(dot_tn(prob.astype(BF16), da))
                    dq.append(dot(dsb, kp))
                    dk.append(dot_tn(dsb, qp))
                lok = low_half((keys, LANES))
                dqkv[0][at, lanes] = (jnp.where(lo, dq[0], dq[1]) * scale).astype(BF16)
                dqkv[1][at, lanes] = (jnp.where(lok, dk[0], dk[1]) * scale)[:rp].astype(BF16)
                dqkv[2][at, lanes] = jnp.where(lok, dv[0], dv[1])[:rp].astype(BF16)
                return carry

            lax.fori_loop(0, images // 2, image, 0)
            tick_in(s, 2)
            lax.fori_loop(images // 2, images, image, 0)
            tick_in(s, 3)

            def store(c, value):
                value = value.astype(BF16)
                if direct:
                    g[s // 2, s % 2, c // 2, c % 2] = value.reshape(g.shape[4:])
                else:
                    g[...] = value
                    copy = pltpu.make_async_copy(g, r.gw.at[j, c], sems.at[2])
                    copy.start()
                    copy.wait()

            for c in range(3):
                store(c, dot(r.nt[...], dqkv[c][:, lanes]))
            store(3, dot(dpt[...], r.att[:, lanes]))
            tick_in(s, 4)
            return carry

        lax.fori_loop(0, pairs, step, 0)
        now = lambda point: run_all(plan.get((pairs - 1, point), ()))

        def total_rows(row, c):
            def add(i, acc):
                return acc + jnp.sum(dqkv[c][pl.ds(at_image(i), rp), :].astype(F32), axis=0, keepdims=True)
            r.small1[row:row + 1, :] = lax.fori_loop(0, images, add, jnp.zeros((1, width), F32))

        total_rows(T_QB, 0)
        total_rows(T_VB, 2)

        def finish(i, carry):
            span = pl.ds(at_image(i), rp)
            dn = dot_nt(dqkv[0][span, :], r.w[0])
            dn += dot_nt(dqkv[1][span, :], r.w[1])
            dn += dot_nt(dqkv[2][span, :], r.w[2])
            dn = dn[:rows]
            ch = r.ch[i]
            n, inv = norm_parts(hidden_of(i))
            dh = r.res[pl.ds(at_image(i), rows), :] + norm_back(n, inv, dn, r.ln1_gain[...])
            r.dn[pl.ds(at_image(i), rows), :] = dh * (1.0 - ch)
            for row, value in ((T_MASK, dh * ch), (T_LG1, dn * n), (T_LB1, dn)):
                r.small1[row:row + 1, :] += jnp.sum(value, axis=0, keepdims=True)
            return carry

        leaving = []
        for i in range(images):
            lax.fori_loop(i, i + 1, finish, 0)
            leaving.append(local.start(lambda i=i: (r.dn.at[pl.ds(i * rp, rows)], r.gx.at[i])))
            now(5 + i)

        a_iota = lax.broadcasted_iota(jnp.int32, (8, keys), 0)
        b_iota = lax.broadcasted_iota(jnp.int32, (LANES, keys), 0)

        def scatter(t, acc):
            at = pl.ds(pl.multiple_of(t * 8, 8), 8)
            idx = r.idx[at, :]
            high, low = idx >> 7, idx & (LANES - 1)
            tiles = [r.bias[h, at, :] for h in range(heads)]
            lefts, rests, ones = [], [], []
            for n in range(8):
                pick = jnp.broadcast_to(high[n:n + 1], (8, keys)) == a_iota
                ones.append((jnp.broadcast_to(low[n:n + 1], (LANES, keys)) == b_iota).astype(F32).astype(BF16))
                left = jnp.concatenate(
                    [jnp.where(pick, jnp.broadcast_to(tile[n:n + 1], (8, keys)), 0.0) for tile in tiles], axis=0)
                top = left.astype(BF16)
                lefts.append(top)
                rests.append((left - top.astype(F32)).astype(BF16))
            one = jnp.concatenate(ones, axis=1)
            return acc + dot_nt(jnp.concatenate(lefts, axis=1), one) + dot_nt(jnp.concatenate(rests, axis=1), one)

        table = jnp.zeros((heads * 8, LANES), F32)
        blocks = rp // 8
        for n in range(5):
            table = lax.fori_loop(n * blocks // 5, (n + 1) * blocks // 5, scatter, table)
            now(9 + n)
        for wait in leaving:
            wait()
        if not direct:
            r.gt[...] = table
            r.small1_out[...] = r.small1[...]
            r.small2_out[...] = r.small2[...]
            r.gb1_out[...] = r.gb1[...]
            return
        wide = width // LANES
        tall = heads * 8 // wide
        r.bufs[0, 0:8] = r.small1[...]
        r.bufs[0, 8:16] = r.small2[...]
        at = 16
        for t in range(wide):
            r.bufs[0, at:at + tall, t * LANES:(t + 1) * LANES] = table[t * tall:(t + 1) * tall]
        at += tall
        r.bufs[0, at:at + steps] = r.gb1[...]
        small.begin()
        last(2)
        small.middle(1)
        run_all([g1["b"], g1["c"]])
        run_all(g2["z%d" % k] for k in range(1, depth))
        small.middle(2)
        run_all(g2["a%d" % k] for k in range(depth))
        small.column()
        run_all([g2["b"], g2["c"]])
        keep = local.start(lambda: (r.gathered, r.full))
        r.small[...] = small.result()
        for m in range(per):
            ar[m].sent()
        wire.sent()
        keep()

    if direct:
        g_shape = (per, 2, 2, 2, depth, 2, 2) + r.gathered.shape[5:6] + (LANES,)
    else:
        g_shape = (width, LANES)
    pl.run_scoped(
        attention_backward, pltpu.VMEM((2, images, 2, rp, keys), F32), pltpu.VMEM((width, flat), BF16),
        pltpu.VMEM((flat, width), BF16), pltpu.VMEM(g_shape, BF16), dma(3),
    )


def layer(direct, given, extra, heads, rp, keys, depth):
    x, kv = given[0], given[2]
    images, rows, width = x.shape
    flat = images * rp
    tall = -(-max(kv.shape[0], images) // 8) * 8
    steps = 4
    ff = extra[-1].size
    outs = [sd(x.shape, BF16), sd(x.shape, F32), sd((images, heads, rp, keys), F32)]
    out_specs = [ANY] * 3
    bf = lambda *shape: pltpu.VMEM(shape, BF16)
    fl = lambda *shape: pltpu.VMEM(shape, F32)
    scratch = [
        pltpu.VMEM((rp, keys), jnp.int32), pltpu.VMEM((tall, keys), jnp.int32), fl(tall, keys), fl(images, rows, 1),
        fl(heads, rp, keys), bf(width, flat), bf(images, rp, width), bf(images, keys, width), bf(images, keys, width),
        bf(flat, width), fl(flat, width), bf(flat, width), bf(flat, width), bf(flat, width), bf(flat, width),
        fl(flat, width), fl(8, width), fl(8, width), fl(steps, ff // steps), dma(24),
    ]
    in_specs = vmem(len(given) - 1) + [ANY]
    params = {}
    if direct:
        mixown, wown, wpown, own1, own2, spot = extra
        per = heads // 4
        share = own1.shape[0]
        own = width // (4 * depth)
        total = 16 + heads * 8 * LANES // width + steps
        big = sd((depth, 2, 2, 2) + own1.shape, BF16)
        outs += [big, big, sd((2, 2, depth, 2, 2, own, per * LANES), BF16), sd((2, share, width), F32), sd((total, width), F32)]
        in_specs += vmem(6)
        out_specs += [ANY] * 3 + vmem(2)
        n = 3 + 2 * (4 * depth + 4) + 2 + depth + 6 * steps + 2 * (depth - 1)
        n += per * (6 + 2 * (depth - 1) + 8 * depth) + 2 + depth
        scratch += [
            bf(3, width, width), bf(width, width), fl(2, *mixown.shape), fl(7, *spot.shape), fl(depth, *spot.shape),
            bf(2, 2, 2, 2, 2, share, width), bf(2, 2, 2, 2, share, width), bf(2, 2, 2, share, width), bf(2, 2, share, width),
            bf(2, depth, share, width), bf(2, depth - 1, share, width),
            bf(per, 2, 2, depth, 2, 2, own, LANES), bf(per, 2, 2, depth, 2, own, LANES), bf(per, 2, 2, depth, own, LANES),
            bf(per, 2, depth - 1, 2, own, LANES), bf(2, 2, depth, 2, 2, own, per * LANES),
            fl(7, total, width), fl(depth, total, width), dma(n), dma(n),
        ]
        params = dict(collective_id=1, has_side_effects=True)
    else:
        part = sd((ff, width), BF16)
        outs += [part, part, sd((heads // 2, 4, width, LANES), BF16), sd((heads * 8, LANES), F32)]
        outs += [sd((8, width), F32), sd((8, width), F32), sd((steps, ff // steps), F32)]
        in_specs += vmem(3) + [ANY, ANY] + vmem(1)
        out_specs += [ANY] * 3 + vmem(4)
    return pl.pallas_call(
        functools.partial(layer_kernel, direct), name="layer",
        out_shape=tuple(outs), in_specs=in_specs, out_specs=out_specs, scratch_shapes=scratch,
        compiler_params=pltpu.CompilerParams(vmem_limit_bytes=63 * 2**20, **params),
    )(*given, *extra)


def shards(
    inputs, masked, key_valid, rel_index, mask_token, ln1_gain, ln1_bias, w_qkv, qv_bias, rel_table,
    w_proj, proj_bias, gamma1, ln2_gain, ln2_bias, w_fc1, fc1_bias, w_fc2, fc2_bias, gamma2, cotangent,
):
    images, rows, width = inputs.shape
    dp, hn = lax.axis_size("dp"), lax.axis_size("head")
    me, head = lax.axis_index("dp"), lax.axis_index("head")
    depth = dp // 4
    share = w_fc2.shape[0]
    ff = share * dp * hn
    entries, heads = rel_table.shape[0], rel_table.shape[1] * hn
    rp, keys = -(-rows // 16) * 16, -(-rows // LANES) * LANES
    direct = hn == 2 and dp == 16 and share % 16 == 0 and width % (16 * dp) == 0

    tab_rows = -(-entries // LANES)
    tab = jnp.pad(rel_table.T, ((0, 0), (0, tab_rows * LANES - entries)))
    mix = jnp.concatenate([tab.reshape(-1, LANES), qv_bias.reshape(-1, LANES)])
    vectors = (mask_token, ln1_gain, ln1_bias, proj_bias, gamma1, ln2_gain, ln2_bias, fc2_bias, gamma2)
    given = (inputs, masked, key_valid, rel_index) + vectors + (cotangent,)
    w3 = jnp.transpose(w_qkv, (1, 0, 2))
    if direct:
        spot_shape = (4, ff // 4)
        owner = (lax.broadcasted_iota(jnp.int32, spot_shape, 0) * (ff // 4) + lax.broadcasted_iota(jnp.int32, spot_shape, 1)) // share
        spot = jnp.where(owner == me * hn + head, jnp.tile(fc1_bias.astype(F32), ff // 4 // share)[None], 0.0)
        extra = (mix, w3, w_proj, w_fc1.T, w_fc2, spot)
        out, gx, _, _, _, full, gff, small = layer(True, given, extra, heads, rp, keys, depth)
        g_fc1, g_fc2 = gff[0], gff[1]
        full = full.reshape(4, width, -1).astype(F32)
        s1, s2 = small[:8], small[8:16]
        wide = width // LANES
        tall = heads * 8 // wide
        table = jnp.transpose(small[16:16 + tall].reshape(tall, wide, LANES), (1, 0, 2)).reshape(heads, -1)
        g_b1 = small[16 + tall:].reshape(-1)
    else:
        w = lax.all_gather(w3, "head", axis=2, tiled=True)
        wp = lax.all_gather(w_proj, "head", axis=0, tiled=True)
        w1 = lax.all_gather(w_fc1.T, ("dp", "head"), axis=0, tiled=True)
        w2 = lax.all_gather(w_fc2, ("dp", "head"), axis=0, tiled=True)
        b1 = lax.all_gather(fc1_bias, ("dp", "head"), axis=0, tiled=True).astype(F32).reshape(4, -1)
        extra = (lax.all_gather(mix, "head", axis=0), w, wp, w1, w2, b1)
        out, gx, _, ga, gb, gw, gt, s1, s2, gb1 = layer(False, given, extra, heads, rp, keys, depth)
        g_fc1 = lax.psum_scatter(ga.astype(F32), ("dp", "head"), scatter_dimension=0, tiled=True)
        g_fc2 = lax.psum_scatter(gb.astype(F32), ("dp", "head"), scatter_dimension=0, tiled=True)
        full = lax.psum(lax.psum_scatter(gw.astype(F32), "head", scatter_dimension=0, tiled=True), "dp")
        full = jnp.transpose(full, (1, 2, 0, 3)).reshape(4, width, -1)
        s1, s2, table, g_b1 = lax.psum((s1, s2, gt.reshape(heads, -1), gb1.reshape(-1)), ("dp", "head"))
    g_qkv, g_proj = full[:3], full[3].T
    g_table = lax.dynamic_slice_in_dim(table, head * (heads // hn), heads // hn, 0)[:, :entries].T
    g_b1 = lax.dynamic_slice_in_dim(g_b1, (me * hn + head) * share, share)
    g_qvb = lax.dynamic_slice_in_dim(s1[T_QB:T_VB + 1], head * (width // hn), width // hn, 1)
    return (
        out, gx, s1[T_MASK], s1[T_LG1], s1[T_LB1], jnp.transpose(g_qkv, (1, 0, 2)), g_qvb, g_table, g_proj,
        s2[S_PB], s2[S_GA1], s2[S_LG2], s2[S_LB2], g_fc1.T, g_b1, g_fc2, s2[S_FB2], s2[S_GA2],
    )


def solution(mesh):
    in_specs = (
        P(("dp", "head"), None, None),
        P(("dp", "head"), None),
        P("dp", None),
        P(),
        P(),
        P(),
        P(),
        P(None, None, "head"),
        P(None, "head"),
        P(None, "head"),
        P("head", None),
        P(),
        P(),
        P(),
        P(),
        P(None, ("dp", "head")),
        P(("dp", "head")),
        P(("dp", "head"), None),
        P(),
        P(),
        P(("dp", "head"), None, None),
    )
    out_specs = (
        P(("dp", "head"), None, None),
        P(("dp", "head"), None, None),
        P(),
        P(),
        P(),
        P(None, None, "head"),
        P(None, "head"),
        P(None, "head"),
        P("head", None),
        P(),
        P(),
        P(),
        P(),
        P(None, ("dp", "head")),
        P(("dp", "head")),
        P(("dp", "head"), None),
        P(),
        P(),
    )
    return jax.shard_map(shards, mesh=mesh, in_specs=in_specs, out_specs=out_specs, check_vma=False)
```

time: 261 us -> 220 us (0.84)
  Pallas kernels: 232 us -> 199 us
  local copies, waits for them, and re-layouts: 23 us -> 15.8 us
    pallas_call x3 -> x1, Pallas kernels: 232 us -> 199 us  [layer(): pl.pallas_call(functools.partial(layer_kernel, direct), name='layer', out...]
    unnamed x21 -> x11, local copies, waits for them, and re-layouts: 13.5 us -> 4.89 us
where the time goes in v3:
time: 220 us; the launch traced here: 219 us
  Pallas kernels  199 us (90%)
  local copies, waits for them, and re-layouts  15.8 us (7%)
  other arithmetic  3.28 us (1%)
    pallas_call x1, Pallas kernels, layer(): pl.pallas_call(functools.partial(layer_kernel, direct), name='layer', out...  199 us
    unnamed x11, local copies, waits for them, and re-layouts  4.89 us

profile of v3, /device:TPU:0, one launch (start us, length us, event | category | flops | bytes accessed | tf_op | source)
XLA Modules:
  0.0 218.9 jit_solution(884138520248573496)
XLA Ops:
  0.7 0.7 tile.2
  1.3 0.1 broadcast_in_dim.14
  1.4 0.7 fusion.1.refs_19_
  2.1 0.7 pad.4
  2.8 0.7 reshape.57
  3.5 0.6 pad_maximum_fusion.refs_14_
  4.2 199.1 %layer.1 = (bf16[4,200,768]{2,1,0:T(8,128)(2,1)}, f32[4,200,768]{2,1,0:T(8,128)}, f32[4,12,208,256]{3,2,1,0:T(8,128)}, bf16[4,2,2,2,96,768]{5,4,3,2,1,0:T(8,128)...) custom-call(bf16[4,200,768]{2,1,0:T(8,128)(2,1)} %refs_0_.1, ...), custom_call_target="tpu_custom_call" | custom-call | tf_op jit(solution)/shard_map/layer/pallas_call | solution.py:966
  203.2 0.7 slice.76
  204.0 0.6 dynamic_slice.11
  204.6 0.8 slice.68
  205.4 0.6 dynamic-slice_bitcast_fusion
  206.0 0.7 slice.67
  206.8 0.6 constant_dynamic-slice_fusion
  207.4 1.7 slice_reduce_fusion
  209.0 2.0 convert.1
  211.0 2.0 slice_bitcast_fusion
  213.0 0.8 copy-done
  213.8 0.1 slice.81
  213.9 1.4 copy.44
  215.3 0.0 copy-done.3
  215.3 0.8 slice_bitcast_fusion.1
  216.1 1.0 copy.47
  217.2 0.3 copy-done.1
  217.4 1.4 copy.48
  (11 shorter events, 0.1 us)
Async XLA Ops:
  211.0 2.8 %copy-start = (bf16[2,2,4,2,2,48,384]{6,5,4,3,2,1,0:T(8,128)(2,1)S(1)}, bf16[2,2,4,2,2,48,384]{6,5,4,3,2,1,0:T(8,128)(2,1)}, u32[]{:S(2)}) copy-start(bf16[2,2,4,2,2,48,384]{6,5,4,3,2,1,0:T(8,128)(2,1)} %get-tuple-element.26) | copy-start | bytes 7077892
  213.8 1.5 copy-start.3
  213.8 2.3 %copy-start.2 = (bf16[4,200,768]{2,1,0:T(8,128)(2,1)S(1)}, bf16[4,200,768]{2,1,0:T(8,128)(2,1)}, u32[]{:S(2)}) copy-start(bf16[4,200,768]{2,1,0:T(8,128)(2,1)} %get-tuple-element.57) | copy-start | bytes 3686404
  215.3 2.1 copy-start.1

commit v4 on v3

--- a/solution.py
+++ b/solution.py
@@ -110,15 +110,13 @@
     return (ey, ex) if p == 0 else (ex, ey)
 
 
-def gather_stages(wire, depth, own, slot, column=None):
+def gather_stages(wire, depth, own, slot, plane=None):
     z, y, x, head = here()
     ids = {}
     for p in range(2):
         for k in range(depth):
-            for kind in "zabc":
+            for kind in "zabc" + ("" if plane is None else "s"):
                 ids[p, kind, k] = wire.slot()
-        for kind in range(0 if column is None else 4):
-            ids[p, "s", kind] = wire.slot()
     up = lambda k: (z + k) % depth
     down = lambda k: (z + depth - k) % depth
 
@@ -126,8 +124,9 @@
         (ay, ax), (by, bx) = hops(p, y, x)
         return (y, x), (ay, ax), (by, bx), (1 - y, 1 - x)
 
-    def send_up(p, k):
-        wire.start(ids[p, "z", k], lambda: (own(p), slot(p, z, y, x), at_dp(up(k), y, x)))
+    def send_up(k):
+        for p in range(2):
+            wire.start(ids[p, "z", k], lambda p=p: (own(p), slot(p, z, y, x), at_dp(up(k), y, x)))
 
     def send_square(p, k, kind, col, to, first=False):
         def make():
@@ -142,47 +141,49 @@
         wire.arrived(ids[p, kind, k], slot(p, down(k), *cs[col]), dev)
 
     def begin():
-        for k in range(1, depth):
-            for p in range(2):
-                send_up(p, k)
+        send_up(1)
         for p in range(2):
             send_square(p, 0, "a", 0, 1, True)
             send_square(p, 0, "b", 0, 2, True)
+        for k in range(2, depth if plane is None else 2):
+            send_up(k)
 
     def from_column(k):
         for p in range(2):
             wait(p, k, "z", 0, None)
             send_square(p, k, "a", 0, 1)
+        for p in range(2):
             send_square(p, k, "b", 0, 2)
+        if plane is not None and k + 1 < depth:
+            send_up(k + 1)
 
     def from_first(k):
         for p in range(2):
             wait(p, k, "a", 1, 1)
             send_square(p, k, "c", 1, 2)
 
-    def from_second(kind, col):
-        for p in range(2):
-            for k in range(depth):
-                wait(p, k, kind, col, 2)
-
-    def across(which):
+    def from_second(k):
+        for p in range(2):
+            wait(p, k, "b", 2, 2)
+            wait(p, k, "c", 3, 2)
+
+    def across(k):
+        from_second(k)
         for p in range(2):
             def make(p=p):
-                block = column(p, *columns(p)[which], head)
+                block = plane(p, down(k), head)
                 return block, block, {"head": 1 - head}
-            wire.start(ids[p, "s", which], make)
-
-    def crossed():
-        for which in range(4):
-            for p in range(2):
-                wire.arrived(ids[p, "s", which], column(p, *columns(p)[which], 1 - head), {"head": 1 - head})
+            wire.start(ids[p, "s", k], make)
+
+    def crossed(k):
+        for p in range(2):
+            wire.arrived(ids[p, "s", k], plane(p, down(k), 1 - head), {"head": 1 - head})
 
     part = functools.partial
-    stages = {"begin": begin, "b": part(from_second, "b", 2), "c": part(from_second, "c", 3), "crossed": crossed}
+    stages = {"begin": begin}
     for k in range(depth):
-        stages["z%d" % k] = part(from_column, k)
-        stages["a%d" % k] = part(from_first, k)
-        stages["s%d" % k] = part(across, k)
+        for name, stage in (("z", from_column), ("a", from_first), ("d", from_second), ("s", across), ("x", crossed)):
+            stages[name + str(k)] = part(stage, k)
     return stages
 
 
@@ -351,7 +352,7 @@
 )
 SHARED = (
     "w", "wp", "mix", "b1", "b1line", "g", "pair_in", "square_in", "line_in", "column", "column_in",
-    "ar_pair", "ar_square", "ar_line", "ar_column", "gathered", "bufs", "line", "send", "recv",
+    "ar_pair", "ar_square", "ar_line", "ar_column", "gathered", "bufs", "line", "tbufs", "tline", "lbufs", "lline", "send", "recv",
 )
 
 
@@ -366,7 +367,7 @@
 def layer_kernel(direct, *refs):
     if direct:
         names = GIVEN + ("mixown", "wown", "wpown", "own1", "own2", "spot")
-        names += ("out", "gx", "p", "w1", "w2", "full", "gff", "small") + KEPT + SHARED
+        names += ("out", "gx", "p", "w1", "w2", "full", "gff", "small", "table", "late") + KEPT + SHARED
     else:
         names = GIVEN + ("mix", "w", "wp", "w1", "w2", "b1")
         names += ("out", "gx", "p", "g1", "g2", "gw", "gt", "small1_out", "small2_out", "gb1_out") + KEPT
@@ -387,7 +388,7 @@
     plan = {}
     part = functools.partial
     every = lambda v: slice(None) if v is None else v
-    level = lambda b: (z + 2 * steps - 1 - b) % steps
+    level = lambda b: (z + 2 * steps - b) % steps
     at_image = lambda i: pl.multiple_of(i * rp, 16)
 
     if direct:
@@ -404,6 +405,8 @@
             (r.wpown, lambda hd: r.wp.at[lanes_of(hd)]),
         ]
         swap_ids = [wire.slot() for _ in swaps]
+        bias_id = wire.slot()
+        bias_of = lambda hd: r.bias.at[pl.ds(hd * own_heads, own_heads)]
         for i, (src, place) in zip(swap_ids, swaps):
             wire.start(i, lambda src=src, place=place: (src, place(head), other))
         for src, place in swaps:
@@ -416,15 +419,15 @@
         bias_sum = SmallSum(wire, depth, r.b1, r.b1line)
         ag = gather_stages(
             wire, depth, own=lambda p: own[p], slot=slot,
-            column=lambda p, yy, xx, hd: full[p].at[:, yy, xx, hd],
+            plane=lambda p, zz, hd: full[p].at[zz, :, :, hd],
         )
         ag["begin"]()
         bias_sum.begin()
         squares = [
             SquareSum(
                 wire,
-                theirs=lambda p, b=b: r.g.at[b % 2, p, :, :, 1 - head],
-                mine=lambda p, yy, xx, b=b: r.g.at[b % 2, p, every(yy), every(xx), head],
+                theirs=lambda p, b=b: r.g.at[b % 3, p, :, :, 1 - head],
+                mine=lambda p, yy, xx, b=b: r.g.at[b % 3, p, every(yy), every(xx), head],
                 pair_in=lambda p, b=b: r.pair_in.at[b % 2, p],
                 square_in=lambda p, b=b: r.square_in.at[b % 2, p],
                 line_in=lambda p, b=b: r.line_in.at[b % 2, p],
@@ -436,17 +439,19 @@
         def close(b):
             squares[b].third()
             for p in range(2):
-                r.column[p, level(b)] = r.g[b % 2, p, y, x, head]
-            if b < steps - 1:
-                column.send(b + 1)
+                r.column[p, level(b)] = r.g[b % 3, p, y, x, head]
+            if b:
+                column.send(b)
             squares[b].sent()
 
-        small = SmallSum(wire, depth, r.bufs, r.line)
+        early = SmallSum(wire, depth, r.bufs, r.line)
+        tables = SmallSum(wire, depth, r.tbufs, r.tline)
+        late = SmallSum(wire, depth, r.lbufs, r.lline)
         plan = {
-            "g1": [ag["z1"], ag["a0"]], "g2": [part(bias_sum.middle, 1)],
-            "p1": [ag["z2"], ag["a1"], part(bias_sum.middle, 2)],
-            "t1": [ag["z3"], ag["a2"], ag["s0"], bias_sum.column], "t4": [ag["a3"], ag["s1"]],
-            "t5": [ag["b"], ag["s2"]], "t6": [ag["c"], ag["s3"]],
+            "p0": [ag["z1"], ag["a0"]], "p1": [part(bias_sum.middle, 1)],
+            "t0": [ag["s0"], ag["a1"], part(bias_sum.middle, 2)],
+            "t3": [ag["z2"], ag["s1"], bias_sum.column], "t5": [ag["a2"]],
+            "t7": [ag["z3"], ag["s2"]],
         }
 
     def tick(point):
@@ -481,7 +486,6 @@
             for wait in local.open:
                 wait()
             local.open = []
-            wire.arrived(swap_ids[0], swaps[0][1](1 - head), other)
 
         def gather_head(h, carry):
             for side in range(keys // LANES):
@@ -490,17 +494,22 @@
                 high = idx >> 7
                 acc = jnp.zeros(idx.shape, F32)
                 for c in range(chunks):
-                    row = r.mix[h // own_heads, pl.ds((h % own_heads) * chunks + c, 1), :]
+                    if direct:
+                        row = r.mixown[pl.ds(h * chunks + c, 1), :]
+                    else:
+                        row = r.mix[h // own_heads, pl.ds((h % own_heads) * chunks + c, 1), :]
                     got = jnp.take_along_axis(jnp.broadcast_to(row, idx.shape), low, axis=1)
                     acc = jnp.where(high == c, got, acc)
-                r.bias[h, :, side * LANES:(side + 1) * LANES] = acc
+                r.bias[head * own_heads + h if direct else h, :, side * LANES:(side + 1) * LANES] = acc
             return carry
 
+        some = own_heads if direct else heads
         for n in range(3):
-            lax.fori_loop(n * heads // 3, (n + 1) * heads // 3, gather_head, 0)
+            lax.fori_loop(n * some // 3, (n + 1) * some // 3, gather_head, 0)
             tick("g%d" % n)
         if direct:
-            for n in (1, 2):
+            wire.copy(bias_id, bias_of(head), bias_of(head), other).start()
+            for n in range(3):
                 wire.arrived(swap_ids[n], swaps[n][1](1 - head), other)
         zeros_tail = jnp.zeros((images, keys - rp, width), BF16)
         r.k[:, rp:, :] = zeros_tail
@@ -520,10 +529,14 @@
                 if kind is not None:
                     acc = acc + bias_row(kind, nb)
                 acc = acc.astype(BF16)
+                if kind == 0:
+                    acc = acc * scale
                 for i in range(images):
                     dst[i, :rp, cols] = acc[i * rp:(i + 1) * rp]
             tick("p%d" % c)
         r.nt[...] = normed[...].T
+        if direct:
+            wire.arrived(bias_id, bias_of(1 - head), other)
 
         def attend(t, carry):
             i = t // pairs
@@ -537,7 +550,7 @@
             outs = []
             for s in range(2):
                 qs = jnp.where(lo if s == 0 else jnp.logical_not(lo), qp, jnp.zeros_like(qp))
-                sc = dot_nt(qs, kp) * scale + r.bias[2 * j + s]
+                sc = dot_nt(qs, kp) + r.bias[2 * j + s]
                 sc = jnp.where(ok, sc, -1e30)
                 e = jnp.exp(sc - jnp.max(sc, axis=-1, keepdims=True))
                 prob = e * (1.0 / jnp.sum(e, axis=-1, keepdims=True))
@@ -556,31 +569,34 @@
                 stored[i] = local.start(lambda i=i: (pring.at[i % 2], r.p.at[i]))
             tick("t%d" % n)
 
-        def finish(i, carry):
-            branch = dot(r.att[pl.ds(at_image(i), rp), :], r.wp[...]) + r.proj_bias[...]
-            res = hidden_of(i) + r.gamma1[...] * branch[:rows]
-            r.res[pl.ds(at_image(i), rows), :] = res
-            n, _ = norm_parts(res)
-            r.n2[pl.ds(at_image(i), rows), :] = (n * r.ln2_gain[...] + r.ln2_bias[...]).astype(BF16)
+        def finish(t, carry):
+            both = dot(r.att[pl.ds(at_image(2 * t), 2 * rp), :], r.wp[...]) + r.proj_bias[...]
+            for side in range(2):
+                i = 2 * t + side
+                res = hidden_of(i) + r.gamma1[...] * both[side * rp:side * rp + rows]
+                r.res[pl.ds(at_image(i), rows), :] = res
+                n, _ = norm_parts(res)
+                r.n2[pl.ds(at_image(i), rows), :] = (n * r.ln2_gain[...] + r.ln2_bias[...]).astype(BF16)
             return carry
 
-        lax.fori_loop(0, images, finish, 0)
+        lax.fori_loop(0, images // 2, finish, 0)
         stored[images - 2]()
         stored[images - 1]()
 
     pl.run_scoped(attention_forward, pltpu.VMEM((flat, width), BF16), pltpu.VMEM((2, heads, rp, keys), F32))
 
     if direct:
-        ag["crossed"]()
+        wire.copy(bias_id, bias_of(head), bias_of(head), other).wait_send()
+        ag["x0"]()
         r.b1[1] = bias_sum.result()
         plan = {
-            (0, 4): [squares[0].pair],
-            (1, 1): [squares[0].first], (1, 4): [squares[1].pair, squares[0].second],
-            (2, 1): [squares[1].first], (2, 2): [part(close, 0)], (2, 4): [squares[2].pair, squares[1].second],
-            (3, 1): [squares[2].first], (3, 2): [part(close, 1)], (3, 4): [squares[3].pair, squares[2].second],
+            (0, 0): [ag["x1"]], (0, 1): [ag["a3"]], (0, 4): [ag["s3"], squares[0].pair],
+            (1, 0): [ag["x2"]], (1, 1): [squares[0].first], (1, 4): [squares[1].pair],
+            (2, 0): [ag["x3"]], (2, 1): [squares[0].second, squares[1].first], (2, 4): [squares[2].pair],
+            (3, 1): [part(close, 0), squares[1].second, squares[2].first], (3, 4): [squares[3].pair],
         }
 
-    def feed_forward(cot, out, branch, slots, sems):
+    def feed_forward(cot, branch, slots, sems):
         def weights(b, into):
             copies = []
             for p, src in enumerate((r.w1, r.w2)):
@@ -611,6 +627,7 @@
             t = level(b)
             for copy in weights(b, slot):
                 copy.wait()
+            tick_in(b, 0)
 
             @pl.when(b + 1 < steps)
             def _():
@@ -622,7 +639,7 @@
             b1 = r.b1[1, pl.ds(t, 1), :] if direct else r.b1[pl.ds(t, 1), :]
 
             def tile(i, gb1):
-                at = pl.ds(at_image(i), rp)
+                at = pl.ds(pl.multiple_of(i * 2 * rp, 16), 2 * rp)
                 pre = dot_nt(r.n2[at, :], w1()) + b1
                 cdf = 0.5 * (1.0 + lax.erf(pre * 0.7071067811865476))
                 slope = cdf + pre * (0.3989422804014327 * jnp.exp(-0.5 * pre * pre))
@@ -634,15 +651,15 @@
                 r.dn[at, :] += dot(dpre, w1())
                 return gb1 + jnp.sum(dpre.astype(F32), axis=0, keepdims=True)
 
-            gb1 = lax.fori_loop(0, images // 2, tile, jnp.zeros((1, block), F32))
+            gb1 = lax.fori_loop(0, images // 4, tile, jnp.zeros((1, block), F32))
             tick_in(b, 1)
-            r.gb1[pl.ds(t, 1), :] = lax.fori_loop(images // 2, images, tile, gb1)
+            r.gb1[pl.ds(t, 1), :] = lax.fori_loop(images // 4, images // 2, tile, gb1)
             tick_in(b, 2)
 
             def store(p, value):
                 value = value.astype(BF16)
                 if direct:
-                    r.g[slot, p] = value.reshape(r.g.shape[2:])
+                    r.g[b % 3, p] = value.reshape(r.g.shape[2:])
                 else:
                     slots[slot, p] = value
                     dst = (r.g1, r.g2)[p].at[pl.ds(pl.multiple_of(t * block, 16), block)]
@@ -669,7 +686,7 @@
             up = cot[i].astype(F32)
             mlp = branch[span, :] + r.fc2_bias[...]
             res = r.res[span, :]
-            out[i] = (res + r.gamma2[...] * mlp).astype(BF16)
+            cot[i] = (res + r.gamma2[...] * mlp).astype(BF16)
             add(S_GA2, up * mlp)
             add(S_FB2, (up * r.gamma2[...]).astype(BF16).astype(F32))
             n, inv = norm_parts(res)
@@ -686,7 +703,7 @@
 
         lax.fori_loop(0, images, finish, 0)
         r.small2[S_GA1:S_GA1 + 1, :] = r.small2[S_GA1:S_GA1 + 1, :] / r.gamma1[...]
-        store_out = pltpu.make_async_copy(out, r.out, sems.at[2, 1])
+        store_out = pltpu.make_async_copy(cot, r.out, sems.at[2, 1])
         store_out.start()
         store_out.wait()
 
@@ -695,21 +712,22 @@
     else:
         slots_shape = (2, 2, block, width)
     pl.run_scoped(
-        feed_forward, pltpu.VMEM(r.cot.shape, BF16), pltpu.VMEM(r.cot.shape, BF16), pltpu.VMEM((flat, width), F32),
+        feed_forward, pltpu.VMEM(r.cot.shape, BF16), pltpu.VMEM((flat, width), F32),
         pltpu.VMEM(slots_shape, BF16), pltpu.SemaphoreType.DMA((4, 2)),
     )
     plan = {}
 
-    def attention_backward(pbuf, dpt, dv_all, g, sems):
+    def attention_backward(pbuf, dpt, g, sems):
         nonlocal plan
-        dqkv = (r.act, r.dpre, dv_all)
+        dqkv = (r.act, r.dpre, r.n2)
         pair_of = lambda s: (s % 2) * per + s // 2
 
-        def fetch(s, into):
-            src = r.p.at[:, pl.ds(2 * pair_of(s), 2)]
-            return pltpu.make_async_copy(src, pbuf.at[into], sems.at[into])
-
-        fetch(0, 0).start()
+        def fetch(t):
+            src = r.p.at[t % images, pl.ds(2 * pair_of(t // images), 2)]
+            return pltpu.make_async_copy(src, pbuf.at[t % 3], sems.at[t % 3])
+
+        for t in range(2):
+            fetch(t).start()
         if direct:
             ar, lines, gathers = [], [], []
             for m in range(per):
@@ -742,38 +760,48 @@
                 for p in range(2):
                     r.gff[p] = column.total(p)
 
+            def early_begin():
+                r.bufs[0] = jnp.zeros(r.bufs.shape[1:], F32)
+                r.bufs[0, 0:8] = r.small2[...]
+                r.bufs[0, 8:8 + steps] = r.gb1[...]
+                early.begin()
+
             g0, g1, g2 = gathers
             plan = {
-                (0, 1): [squares[3].first, part(close, 2)], (0, 4): [squares[3].second], (1, 3): [part(close, 3)],
-                (1, 4): [ar[0].pair], (2, 3): [ar[0].first], (3, 4): [ar[1].pair, ar[0].second],
-                (4, 3): [ar[1].first], (4, 4): [part(third, 0)],
-                (5, 4): [ar[2].pair, ar[1].second, part(last, 0)],
-                (5, 6): [ar[2].first, part(third, 1)], (5, 7): [g0["z1"], g0["z2"], g0["z3"]], (5, 8): [part(last, 1)],
-                (5, 9): [ar[2].second, g0["a0"], g0["a1"], g0["a2"], g0["a3"]], (5, 10): [g1["z1"], g1["z2"], g1["z3"]],
-                (5, 11): [part(third, 2), g0["b"], g0["c"]], (5, 12): [g1["a0"], g1["a1"], g1["a2"], g1["a3"]], (5, 13): [ff_last],
+                "start": [part(close, 1), squares[2].second, squares[3].first, early_begin],
+                (0, 4): [part(close, 2), part(early.middle, 1)], (1, 1): [squares[3].second], (1, 4): [ar[0].pair, part(early.middle, 2)],
+                (2, 2): [ar[0].first], (2, 3): [part(close, 3)], (2, 4): [early.column],
+                (3, 2): [ar[0].second], (3, 4): [ar[1].pair], (4, 1): [part(third, 0)], (4, 2): [ar[1].first],
+                (5, 1): [part(last, 0)], (5, 2): [ar[1].second], (5, 4): [ar[2].pair, g0["z1"], g0["z2"], g0["z3"]],
+                (5, 5): [ar[2].first, part(third, 1)], (5, 6): [g0["a0"], g0["a1"], g0["a2"], g0["a3"]],
+                (5, 7): [part(last, 1)], (5, 8): [ar[2].second], (5, 9): [g1["z1"], g1["z2"], g1["z3"]],
+                (5, 10): [part(third, 2), part(tables.middle, 1)], (5, 11): [g0["d0"], g0["d1"], g0["d2"], g0["d3"]],
+                (5, 12): [part(last, 2), part(tables.middle, 2), g1["a0"], g1["a1"], g1["a2"], g1["a3"]],
+                (5, 13): [tables.column],
             }
 
-        for i in range(images):
-            at = slice(i * rp, (i + 1) * rp)
+        tick("start")
+        for t in range(images // 2):
+            at = slice(2 * t * rp, 2 * (t + 1) * rp)
             r.db[at, :] = dot_nt(r.n2[at, :], r.wp[...]).astype(BF16)
         dpt[...] = r.n2[...].T
         r.small1[...] = jnp.zeros_like(r.small1)
 
         def step(s, carry):
             j = pair_of(s)
-            now = s % 2
-            fetch(s, now).wait()
-
-            @pl.when(s + 1 < pairs)
-            def _():
-                fetch(s + 1, 1 - now).start()
-
             tick_in(s, 1)
             lanes = pl.ds(pl.multiple_of(j * LANES, LANES), LANES)
             r.bias[2 * j] = jnp.zeros((rp, keys), F32)
             r.bias[2 * j + 1] = jnp.zeros((rp, keys), F32)
 
             def image(i, carry):
+                t = s * images + i
+                fetch(t).wait()
+
+                @pl.when(t + 2 < pairs * images)
+                def _():
+                    fetch(t + 2).start()
+
                 at = pl.ds(at_image(i), rp)
                 qp = r.q[i, :, lanes]
                 kp = r.k[i, :, lanes]
@@ -783,7 +811,7 @@
                 dv, dq, dk = [], [], []
                 for n in range(2):
                     das = jnp.where(lo if n == 0 else jnp.logical_not(lo), da, jnp.zeros_like(da))
-                    prob = pbuf[now, i, n]
+                    prob = pbuf[t % 3, n]
                     dp = dot_nt(das, vp)
                     dsc = prob * (dp - jnp.sum(prob * dp, axis=-1, keepdims=True))
                     dsb = dsc.astype(BF16)
@@ -793,7 +821,7 @@
                     dk.append(dot_tn(dsb, qp))
                 lok = low_half((keys, LANES))
                 dqkv[0][at, lanes] = (jnp.where(lo, dq[0], dq[1]) * scale).astype(BF16)
-                dqkv[1][at, lanes] = (jnp.where(lok, dk[0], dk[1]) * scale)[:rp].astype(BF16)
+                dqkv[1][at, lanes] = jnp.where(lok, dk[0], dk[1])[:rp].astype(BF16)
                 dqkv[2][at, lanes] = jnp.where(lok, dv[0], dv[1])[:rp].astype(BF16)
                 return carry
 
@@ -808,12 +836,13 @@
                     g[s // 2, s % 2, c // 2, c % 2] = value.reshape(g.shape[4:])
                 else:
                     g[...] = value
-                    copy = pltpu.make_async_copy(g, r.gw.at[j, c], sems.at[2])
+                    copy = pltpu.make_async_copy(g, r.gw.at[j, c], sems.at[3])
                     copy.start()
                     copy.wait()
 
+            three = dot(r.nt[...], jnp.concatenate([dqkv[c][:, lanes] for c in range(3)], axis=1))
             for c in range(3):
-                store(c, dot(r.nt[...], dqkv[c][:, lanes]))
+                store(c, three[:, c * LANES:(c + 1) * LANES])
             store(3, dot(dpt[...], r.att[:, lanes]))
             tick_in(s, 4)
             return carry
@@ -828,26 +857,6 @@
 
         total_rows(T_QB, 0)
         total_rows(T_VB, 2)
-
-        def finish(i, carry):
-            span = pl.ds(at_image(i), rp)
-            dn = dot_nt(dqkv[0][span, :], r.w[0])
-            dn += dot_nt(dqkv[1][span, :], r.w[1])
-            dn += dot_nt(dqkv[2][span, :], r.w[2])
-            dn = dn[:rows]
-            ch = r.ch[i]
-            n, inv = norm_parts(hidden_of(i))
-            dh = r.res[pl.ds(at_image(i), rows), :] + norm_back(n, inv, dn, r.ln1_gain[...])
-            r.dn[pl.ds(at_image(i), rows), :] = dh * (1.0 - ch)
-            for row, value in ((T_MASK, dh * ch), (T_LG1, dn * n), (T_LB1, dn)):
-                r.small1[row:row + 1, :] += jnp.sum(value, axis=0, keepdims=True)
-            return carry
-
-        leaving = []
-        for i in range(images):
-            lax.fori_loop(i, i + 1, finish, 0)
-            leaving.append(local.start(lambda i=i: (r.dn.at[pl.ds(i * rp, rows)], r.gx.at[i])))
-            now(5 + i)
 
         a_iota = lax.broadcasted_iota(jnp.int32, (8, keys), 0)
         b_iota = lax.broadcasted_iota(jnp.int32, (LANES, keys), 0)
@@ -873,7 +882,33 @@
         blocks = rp // 8
         for n in range(5):
             table = lax.fori_loop(n * blocks // 5, (n + 1) * blocks // 5, scatter, table)
-            now(9 + n)
+            now(5 + n)
+        wide = width // LANES
+        tall = heads * 8 // wide
+        if direct:
+            for t in range(wide):
+                r.tbufs[0, :, t * LANES:(t + 1) * LANES] = table[t * tall:(t + 1) * tall]
+            tables.begin()
+        def finish(i, carry):
+            span = pl.ds(at_image(i), rp)
+            dn = dot_nt(dqkv[0][span, :], r.w[0])
+            dn += dot_nt(dqkv[1][span, :], r.w[1])
+            dn += dot_nt(dqkv[2][span, :], r.w[2])
+            dn = dn[:rows]
+            ch = r.ch[i]
+            n, inv = norm_parts(hidden_of(i))
+            dh = r.res[pl.ds(at_image(i), rows), :] + norm_back(n, inv, dn, r.ln1_gain[...])
+            r.dn[pl.ds(at_image(i), rows), :] = dh * (1.0 - ch)
+            for row, value in ((T_MASK, dh * ch), (T_LG1, dn * n), (T_LB1, dn)):
+                r.small1[row:row + 1, :] += jnp.sum(value, axis=0, keepdims=True)
+            return carry
+
+        leaving = []
+        for i in range(images):
+            lax.fori_loop(i, i + 1, finish, 0)
+            leaving.append(local.start(lambda i=i: (r.dn.at[pl.ds(i * rp, rows)], r.gx.at[i])))
+            now(10 + i)
+
         for wait in leaving:
             wait()
         if not direct:
@@ -882,26 +917,20 @@
             r.small2_out[...] = r.small2[...]
             r.gb1_out[...] = r.gb1[...]
             return
-        wide = width // LANES
-        tall = heads * 8 // wide
-        r.bufs[0, 0:8] = r.small1[...]
-        r.bufs[0, 8:16] = r.small2[...]
-        at = 16
-        for t in range(wide):
-            r.bufs[0, at:at + tall, t * LANES:(t + 1) * LANES] = table[t * tall:(t + 1) * tall]
-        at += tall
-        r.bufs[0, at:at + steps] = r.gb1[...]
-        small.begin()
-        last(2)
-        small.middle(1)
-        run_all([g1["b"], g1["c"]])
+        r.lbufs[0] = r.small1[...]
+        late.begin()
+        r.small[...] = early.result()
+        late.middle(1)
         run_all(g2["z%d" % k] for k in range(1, depth))
-        small.middle(2)
+        late.middle(2)
+        run_all(g1["d%d" % k] for k in range(depth))
         run_all(g2["a%d" % k] for k in range(depth))
-        small.column()
-        run_all([g2["b"], g2["c"]])
+        late.column()
+        ff_last()
+        r.table[...] = tables.result()
+        run_all(g2["d%d" % k] for k in range(depth))
         keep = local.start(lambda: (r.gathered, r.full))
-        r.small[...] = small.result()
+        r.late[...] = late.result()
         for m in range(per):
             ar[m].sent()
         wire.sent()
@@ -912,8 +941,8 @@
     else:
         g_shape = (width, LANES)
     pl.run_scoped(
-        attention_backward, pltpu.VMEM((2, images, 2, rp, keys), F32), pltpu.VMEM((width, flat), BF16),
-        pltpu.VMEM((flat, width), BF16), pltpu.VMEM(g_shape, BF16), dma(3),
+        attention_backward, pltpu.VMEM((3, 2, rp, keys), F32), pltpu.VMEM((width, flat), BF16),
+        pltpu.VMEM(g_shape, BF16), dma(4),
     )
 
 
@@ -941,20 +970,22 @@
         per = heads // 4
         share = own1.shape[0]
         own = width // (4 * depth)
-        total = 16 + heads * 8 * LANES // width + steps
+        total = 8 + 8
+        tall_t = heads * 8 * LANES // width
         big = sd((depth, 2, 2, 2) + own1.shape, BF16)
-        outs += [big, big, sd((2, 2, depth, 2, 2, own, per * LANES), BF16), sd((2, share, width), F32), sd((total, width), F32)]
+        outs += [big, big, sd((2, 2, depth, 2, 2, own, per * LANES), BF16), sd((2, share, width), F32)]
+        outs += [sd((total, width), F32), sd((tall_t, width), F32), sd((8, width), F32)]
         in_specs += vmem(6)
-        out_specs += [ANY] * 3 + vmem(2)
-        n = 3 + 2 * (4 * depth + 4) + 2 + depth + 6 * steps + 2 * (depth - 1)
-        n += per * (6 + 2 * (depth - 1) + 8 * depth) + 2 + depth
+        out_specs += [ANY] * 3 + vmem(4)
+        n = 4 + 2 * (4 * depth + 4) + 2 + depth + 6 * steps + 2 * (depth - 1)
+        n += per * (6 + 2 * (depth - 1) + 8 * depth) + 3 * (2 + depth)
         scratch += [
             bf(3, width, width), bf(width, width), fl(2, *mixown.shape), fl(7, *spot.shape), fl(depth, *spot.shape),
-            bf(2, 2, 2, 2, 2, share, width), bf(2, 2, 2, 2, share, width), bf(2, 2, 2, share, width), bf(2, 2, share, width),
+            bf(3, 2, 2, 2, 2, share, width), bf(2, 2, 2, 2, share, width), bf(2, 2, 2, share, width), bf(2, 2, share, width),
             bf(2, depth, share, width), bf(2, depth - 1, share, width),
             bf(per, 2, 2, depth, 2, 2, own, LANES), bf(per, 2, 2, depth, 2, own, LANES), bf(per, 2, 2, depth, own, LANES),
             bf(per, 2, depth - 1, 2, own, LANES), bf(2, 2, depth, 2, 2, own, per * LANES),
-            fl(7, total, width), fl(depth, total, width), dma(n), dma(n),
+            fl(7, total, width), fl(depth, total, width), fl(7, tall_t, width), fl(depth, tall_t, width), fl(7, 8, width), fl(depth, 8, width), dma(n), dma(n),
         ]
         params = dict(collective_id=1, has_side_effects=True)
     else:
@@ -995,14 +1026,14 @@
         owner = (lax.broadcasted_iota(jnp.int32, spot_shape, 0) * (ff // 4) + lax.broadcasted_iota(jnp.int32, spot_shape, 1)) // share
         spot = jnp.where(owner == me * hn + head, jnp.tile(fc1_bias.astype(F32), ff // 4 // share)[None], 0.0)
         extra = (mix, w3, w_proj, w_fc1.T, w_fc2, spot)
-        out, gx, _, _, _, full, gff, small = layer(True, given, extra, heads, rp, keys, depth)
+        out, gx, _, _, _, full, gff, small, table, late = layer(True, given, extra, heads, rp, keys, depth)
         g_fc1, g_fc2 = gff[0], gff[1]
         full = full.reshape(4, width, -1).astype(F32)
-        s1, s2 = small[:8], small[8:16]
+        s1, s2 = late, small[:8]
         wide = width // LANES
         tall = heads * 8 // wide
-        table = jnp.transpose(small[16:16 + tall].reshape(tall, wide, LANES), (1, 0, 2)).reshape(heads, -1)
-        g_b1 = small[16 + tall:].reshape(-1)
+        table = jnp.transpose(table.reshape(tall, wide, LANES), (1, 0, 2)).reshape(heads, -1)
+        g_b1 = small[8:12].reshape(-1)
     else:
         w = lax.all_gather(w3, "head", axis=2, tiled=True)
         wp = lax.all_gather(w_proj, "head", axis=0, tiled=True)

time: 220 us -> 201 us (0.914)
  Pallas kernels: 199 us -> 181 us
    pallas_call x1, Pallas kernels: 199 us -> 181 us  [layer(): pl.pallas_call(functools.partial(layer_kernel, direct), name='layer', out...]
where the time goes in v4:
time: 201 us
  Pallas kernels  181 us (90%)
  local copies, waits for them, and re-layouts  15.9 us (8%)
  other arithmetic  3.28 us (2%)
    pallas_call x1, Pallas kernels, layer(): pl.pallas_call(functools.partial(layer_kernel, direct), name='layer', out...  181 us
    unnamed x11, local copies, waits for them, and re-layouts  4.89 us

profile of v4, /device:TPU:0, one launch (start us, length us, event | category | flops | bytes accessed | tf_op | source)
XLA Modules:
  0.0 200.8 jit_solution(641610455388963965)
XLA Ops:
  0.7 0.7 tile.2
  1.3 0.1 broadcast_in_dim.14
  1.4 0.7 fusion.1.refs_19_
  2.1 0.7 pad.4
  2.8 0.7 reshape.57
  3.5 0.6 pad_maximum_fusion.refs_14_
  4.2 180.9 %layer.1 = (bf16[4,200,768]{2,1,0:T(8,128)(2,1)}, f32[4,200,768]{2,1,0:T(8,128)}, f32[4,12,208,256]{3,2,1,0:T(8,128)}, bf16[4,2,2,2,96,768]{5,4,3,2,1,0:T(8,128)...) custom-call(bf16[4,200,768]{2,1,0:T(8,128)(2,1)} %refs_0_.1, ...), custom_call_target="tpu_custom_call" | custom-call | tf_op jit(solution)/shard_map/layer/pallas_call | solution.py:997
  185.1 0.7 slice.67
  185.8 0.6 dynamic_slice.11
  186.4 1.8 slice_reduce_fusion
  188.2 0.7 slice.59
  189.0 0.6 constant_dynamic-slice_fusion
  189.5 0.8 reshape.58
  190.4 0.6 dynamic-slice_bitcast_fusion
  191.0 2.0 convert.1
  193.0 0.0 copy-start
  193.0 2.0 %slice_bitcast_fusion = f32[768,3,384]{2,0,1:T(8,128)} fusion(f32[4,768,384]{2,1,0:T(8,128)S(1)} %convert.1), kind=kLoop, calls=%fused_computation | loop fusion | bytes 7077888 | tf_op jit(solution)/shard_map/transpose | solution.py:1055
  195.0 0.8 copy-done
  195.8 0.1 slice.72
  195.9 1.4 copy.44
  197.3 0.8 slice_bitcast_fusion.1
  198.1 1.0 copy.47
  199.1 0.3 copy-done.1
  199.4 1.4 copy.48
  (10 shorter events, 0.1 us)
Async XLA Ops:
  193.0 2.8 %copy-start = (bf16[2,2,4,2,2,48,384]{6,5,4,3,2,1,0:T(8,128)(2,1)S(1)}, bf16[2,2,4,2,2,48,384]{6,5,4,3,2,1,0:T(8,128)(2,1)}, u32[]{:S(2)}) copy-start(bf16[2,2,4,2,2,48,384]{6,5,4,3,2,1,0:T(8,128)(2,1)} %get-tuple-element.28) | copy-start | bytes 7077892
  195.8 1.5 copy-start.3
  195.8 2.3 %copy-start.2 = (bf16[4,200,768]{2,1,0:T(8,128)(2,1)S(1)}, bf16[4,200,768]{2,1,0:T(8,128)(2,1)}, u32[]{:S(2)}) copy-start(bf16[4,200,768]{2,1,0:T(8,128)(2,1)} %get-tuple-element.64) | copy-start | bytes 3686404
  197.3 2.1 %copy-start.1 = (f32[4,200,768]{2,1,0:T(8,128)S(1)}, f32[4,200,768]{2,1,0:T(8,128)}, u32[]{:S(2)}) copy-start(f32[4,200,768]{2,1,0:T(8,128)} %get-tuple-element.65) | copy-start | bytes 7372804

commit v5 on v4

--- a/solution.py
+++ b/solution.py
@@ -55,9 +55,19 @@
     return {"dp": (z * 2 + y) * 2 + x}
 
 
+FLIPS = ((0, 0, 1), (0, 1, 0), (1, 0, 0), (0, 1, 1), (1, 0, 1), (1, 1, 0), (1, 1, 1))
+
+
+def flipped(place, flip):
+    z, y, x, head = place
+    turn = lambda v, f: 1 - v if f else v
+    fh, fy, fx = turn(head, flip[0]), turn(y, flip[1]), turn(x, flip[2])
+    return dict(at_dp(z, fy, fx), head=fh), (fh, fy, fx)
+
+
 def greet(depth):
-    z, y, x, head = here()
-    found = [at_dp(z, y, 1 - x), at_dp(z, 1 - y, x), {"head": 1 - head}]
+    place = z, y, x, head = here()
+    found = [flipped(place, flip)[0] for flip in FLIPS]
     found += [at_dp((z + k) % depth, y, x) for k in range(1, depth)]
     barrier = pltpu.get_barrier_semaphore()
     for dev in found:
@@ -270,44 +280,41 @@
 
 
 class SmallSum:
-    def __init__(self, wire, depth, bufs, line):
-        self.wire, self.depth, self.bufs, self.line = wire, depth, bufs, line
-        self.ids = [wire.slot() for _ in range(2 + depth)]
+    def __init__(self, wire, depth, level, line):
+        self.wire, self.depth, self.level, self.line = wire, depth, level, line
+        self.ids = {flip: wire.slot() for flip in FLIPS}
+        self.ups = [wire.slot() for _ in range(depth)]
         self.place = here()
 
-    def devices(self):
+    def begin(self, fill):
         z, y, x, head = self.place
-        return [{"head": 1 - head}, at_dp(z, y, 1 - x), at_dp(z, 1 - y, x)]
-
-    def send(self, n):
-        self.wire.start(self.ids[n], lambda: (self.bufs.at[2 * n], self.bufs.at[2 * n + 1], self.devices()[n]))
-
-    def take(self, n):
-        self.wire.arrived(self.ids[n], self.bufs.at[2 * n + 1], self.devices()[n])
-        self.bufs[2 * n + 2] = self.bufs[2 * n] + self.bufs[2 * n + 1]
-
-    def begin(self):
-        self.send(0)
-
-    def middle(self, n):
-        self.take(n - 1)
-        self.send(n)
-
-    def column(self):
+        fill(self.level.at[head, y, x])
+        for flip in FLIPS:
+            def make(flip=flip):
+                own = self.level.at[head, y, x]
+                return own, own, flipped(self.place, flip)[0]
+            self.wire.start(self.ids[flip], make)
+
+    def meet(self):
         z, y, x, head = self.place
-        self.take(2)
-        self.line[z] = self.bufs[6]
+        for flip in FLIPS:
+            dev, spot = flipped(self.place, flip)
+            self.wire.arrived(self.ids[flip], self.level.at[spot], dev)
+        total = self.level[0, 0, 0]
+        for n in range(1, 8):
+            total = total + self.level[n // 4, n // 2 % 2, n % 2]
+        self.line[z] = total
         for k in range(1, self.depth):
             self.wire.start(
-                self.ids[2 + k],
-                lambda k=k: (self.bufs.at[6], self.line.at[z], at_dp((z + k) % self.depth, y, x)),
+                self.ups[k],
+                lambda k=k: (self.line.at[z], self.line.at[z], at_dp((z + k) % self.depth, y, x)),
             )
 
     def result(self):
         z, y, x, head = self.place
         for k in range(1, self.depth):
             back = (z + self.depth - k) % self.depth
-            self.wire.arrived(self.ids[2 + k], self.line.at[back], at_dp(back, y, x))
+            self.wire.arrived(self.ups[k], self.line.at[back], at_dp(back, y, x))
         total = self.line[0]
         for n in range(1, self.depth):
             total = total + self.line[n]
@@ -351,7 +358,7 @@
     "small1", "small2", "gb1", "lsem",
 )
 SHARED = (
-    "w", "wp", "mix", "b1", "b1line", "g", "pair_in", "square_in", "line_in", "column", "column_in",
+    "w", "wp", "mix", "b1", "b1line", "b1row", "g", "pair_in", "square_in", "line_in", "column", "column_in",
     "ar_pair", "ar_square", "ar_line", "ar_column", "gathered", "bufs", "line", "tbufs", "tline", "lbufs", "lline", "send", "recv",
 )
 
@@ -367,7 +374,7 @@
 def layer_kernel(direct, *refs):
     if direct:
         names = GIVEN + ("mixown", "wown", "wpown", "own1", "own2", "spot")
-        names += ("out", "gx", "p", "w1", "w2", "full", "gff", "small", "table", "late") + KEPT + SHARED
+        names += ("out", "gx", "p", "w1", "w2", "full", "proj", "gff1", "gff2", "small", "table", "late") + KEPT + SHARED
     else:
         names = GIVEN + ("mix", "w", "wp", "w1", "w2", "b1")
         names += ("out", "gx", "p", "g1", "g2", "gw", "gt", "small1_out", "small2_out", "gb1_out") + KEPT
@@ -415,14 +422,17 @@
         own = (r.own1, r.own2)
         for p in range(2):
             local.start(lambda p=p: (own[p], slot(p, z, y, x)))
-        r.b1[0] = r.spot[...]
         bias_sum = SmallSum(wire, depth, r.b1, r.b1line)
         ag = gather_stages(
             wire, depth, own=lambda p: own[p], slot=slot,
             plane=lambda p, zz, hd: full[p].at[zz, :, :, hd],
         )
         ag["begin"]()
-        bias_sum.begin()
+
+        def fill_bias(ref):
+            ref[...] = r.spot[...]
+
+        bias_sum.begin(fill_bias)
         squares = [
             SquareSum(
                 wire,
@@ -448,10 +458,8 @@
         tables = SmallSum(wire, depth, r.tbufs, r.tline)
         late = SmallSum(wire, depth, r.lbufs, r.lline)
         plan = {
-            "p0": [ag["z1"], ag["a0"]], "p1": [part(bias_sum.middle, 1)],
-            "t0": [ag["s0"], ag["a1"], part(bias_sum.middle, 2)],
-            "t3": [ag["z2"], ag["s1"], bias_sum.column], "t5": [ag["a2"]],
-            "t7": [ag["z3"], ag["s2"]],
+            "p2": [ag["z1"], ag["a0"]], "t0": [bias_sum.meet],
+            "t2": [ag["s0"], ag["a1"]], "t5": [ag["z2"], ag["s1"]], "t7": [ag["a2"]],
         }
 
     def tick(point):
@@ -588,10 +596,10 @@
     if direct:
         wire.copy(bias_id, bias_of(head), bias_of(head), other).wait_send()
         ag["x0"]()
-        r.b1[1] = bias_sum.result()
+        r.b1row[...] = bias_sum.result()
         plan = {
-            (0, 0): [ag["x1"]], (0, 1): [ag["a3"]], (0, 4): [ag["s3"], squares[0].pair],
-            (1, 0): [ag["x2"]], (1, 1): [squares[0].first], (1, 4): [squares[1].pair],
+            (0, 0): [ag["x1"]], (0, 1): [ag["z3"]], (0, 2): [ag["s2"]], (0, 4): [ag["a3"], squares[0].pair],
+            (1, 0): [ag["x2"]], (1, 1): [squares[0].first, ag["s3"]], (1, 4): [squares[1].pair],
             (2, 0): [ag["x3"]], (2, 1): [squares[0].second, squares[1].first], (2, 4): [squares[2].pair],
             (3, 1): [part(close, 0), squares[1].second, squares[2].first], (3, 4): [squares[3].pair],
         }
@@ -636,7 +644,7 @@
 
             w1 = lambda: slots[slot, 0].reshape(block, width)
             w2 = lambda: slots[slot, 1].reshape(block, width)
-            b1 = r.b1[1, pl.ds(t, 1), :] if direct else r.b1[pl.ds(t, 1), :]
+            b1 = (r.b1row if direct else r.b1)[pl.ds(t, 1), :]
 
             def tile(i, gb1):
                 at = pl.ds(pl.multiple_of(i * 2 * rp, 16), 2 * rp)
@@ -758,26 +766,26 @@
 
             def ff_last():
                 for p in range(2):
-                    r.gff[p] = column.total(p)
+                    (r.gff1, r.gff2)[p][...] = column.total(p)
 
             def early_begin():
-                r.bufs[0] = jnp.zeros(r.bufs.shape[1:], F32)
-                r.bufs[0, 0:8] = r.small2[...]
-                r.bufs[0, 8:8 + steps] = r.gb1[...]
-                early.begin()
+                def fill(ref):
+                    ref[...] = jnp.zeros(ref.shape, F32)
+                    ref[0:8] = r.small2[...]
+                    ref[8:8 + steps] = r.gb1[...]
+                early.begin(fill)
 
             g0, g1, g2 = gathers
             plan = {
                 "start": [part(close, 1), squares[2].second, squares[3].first, early_begin],
-                (0, 4): [part(close, 2), part(early.middle, 1)], (1, 1): [squares[3].second], (1, 4): [ar[0].pair, part(early.middle, 2)],
-                (2, 2): [ar[0].first], (2, 3): [part(close, 3)], (2, 4): [early.column],
+                (0, 4): [part(close, 2)], (1, 1): [squares[3].second, early.meet], (1, 4): [ar[0].pair],
+                (2, 2): [ar[0].first], (2, 3): [part(close, 3)],
                 (3, 2): [ar[0].second], (3, 4): [ar[1].pair], (4, 1): [part(third, 0)], (4, 2): [ar[1].first],
                 (5, 1): [part(last, 0)], (5, 2): [ar[1].second], (5, 4): [ar[2].pair, g0["z1"], g0["z2"], g0["z3"]],
                 (5, 5): [ar[2].first, part(third, 1)], (5, 6): [g0["a0"], g0["a1"], g0["a2"], g0["a3"]],
                 (5, 7): [part(last, 1)], (5, 8): [ar[2].second], (5, 9): [g1["z1"], g1["z2"], g1["z3"]],
-                (5, 10): [part(third, 2), part(tables.middle, 1)], (5, 11): [g0["d0"], g0["d1"], g0["d2"], g0["d3"]],
-                (5, 12): [part(last, 2), part(tables.middle, 2), g1["a0"], g1["a1"], g1["a2"], g1["a3"]],
-                (5, 13): [tables.column],
+                (5, 10): [part(third, 2)], (5, 11): [g0["d0"], g0["d1"], g0["d2"], g0["d3"]],
+                (5, 12): [part(last, 2), tables.meet, g1["a0"], g1["a1"], g1["a2"], g1["a3"]],
             }
 
         tick("start")
@@ -886,9 +894,10 @@
         wide = width // LANES
         tall = heads * 8 // wide
         if direct:
-            for t in range(wide):
-                r.tbufs[0, :, t * LANES:(t + 1) * LANES] = table[t * tall:(t + 1) * tall]
-            tables.begin()
+            def fill_table(ref):
+                for t in range(wide):
+                    ref[:, t * LANES:(t + 1) * LANES] = table[t * tall:(t + 1) * tall]
+            tables.begin(fill_table)
         def finish(i, carry):
             span = pl.ds(at_image(i), rp)
             dn = dot_nt(dqkv[0][span, :], r.w[0])
@@ -917,24 +926,33 @@
             r.small2_out[...] = r.small2[...]
             r.gb1_out[...] = r.gb1[...]
             return
-        r.lbufs[0] = r.small1[...]
-        late.begin()
+
+        def fill_late(ref):
+            ref[...] = r.small1[...]
+
+        late.begin(fill_late)
         r.small[...] = early.result()
-        late.middle(1)
+        ff_last()
         run_all(g2["z%d" % k] for k in range(1, depth))
-        late.middle(2)
+        late.meet()
         run_all(g1["d%d" % k] for k in range(depth))
         run_all(g2["a%d" % k] for k in range(depth))
-        late.column()
-        ff_last()
         r.table[...] = tables.result()
         run_all(g2["d%d" % k] for k in range(depth))
-        keep = local.start(lambda: (r.gathered, r.full))
+        keep = [
+            local.start(lambda: (r.gathered.at[0], r.full.at[0:2])),
+            local.start(lambda: (r.gathered.at[1, 0], r.full.at[2])),
+        ]
+        tall_p = r.proj.shape[0]
+        r.n2[0:tall_p, :] = r.gathered[1, 1].reshape(width, tall_p).T
+        keep_proj = local.start(lambda: (r.n2.at[0:tall_p], r.proj))
         r.late[...] = late.result()
+        keep_proj()
         for m in range(per):
             ar[m].sent()
         wire.sent()
-        keep()
+        for wait in keep:
+            wait()
 
     if direct:
         g_shape = (per, 2, 2, 2, depth, 2, 2) + r.gathered.shape[5:6] + (LANES,)
@@ -973,19 +991,20 @@
         total = 8 + 8
         tall_t = heads * 8 * LANES // width
         big = sd((depth, 2, 2, 2) + own1.shape, BF16)
-        outs += [big, big, sd((2, 2, depth, 2, 2, own, per * LANES), BF16), sd((2, share, width), F32)]
+        outs += [big, big, sd((3, depth, 2, 2, own, per * LANES), BF16), sd((per * LANES, width), BF16)]
+        outs += [sd((share, width), F32), sd((share, width), F32)]
         outs += [sd((total, width), F32), sd((tall_t, width), F32), sd((8, width), F32)]
         in_specs += vmem(6)
-        out_specs += [ANY] * 3 + vmem(4)
-        n = 4 + 2 * (4 * depth + 4) + 2 + depth + 6 * steps + 2 * (depth - 1)
-        n += per * (6 + 2 * (depth - 1) + 8 * depth) + 3 * (2 + depth)
+        out_specs += [ANY] * 4 + vmem(5)
+        n = 4 + 2 * (4 * depth + 4) + 4 * (7 + depth) + 6 * steps + 2 * (depth - 1)
+        n += per * (6 + 2 * (depth - 1) + 8 * depth)
         scratch += [
-            bf(3, width, width), bf(width, width), fl(2, *mixown.shape), fl(7, *spot.shape), fl(depth, *spot.shape),
+            bf(3, width, width), bf(width, width), fl(2, *mixown.shape), fl(2, 2, 2, *spot.shape), fl(depth, *spot.shape), fl(*spot.shape),
             bf(3, 2, 2, 2, 2, share, width), bf(2, 2, 2, 2, share, width), bf(2, 2, 2, share, width), bf(2, 2, share, width),
             bf(2, depth, share, width), bf(2, depth - 1, share, width),
             bf(per, 2, 2, depth, 2, 2, own, LANES), bf(per, 2, 2, depth, 2, own, LANES), bf(per, 2, 2, depth, own, LANES),
             bf(per, 2, depth - 1, 2, own, LANES), bf(2, 2, depth, 2, 2, own, per * LANES),
-            fl(7, total, width), fl(depth, total, width), fl(7, tall_t, width), fl(depth, tall_t, width), fl(7, 8, width), fl(depth, 8, width), dma(n), dma(n),
+            fl(2, 2, 2, total, width), fl(depth, total, width), fl(2, 2, 2, tall_t, width), fl(depth, tall_t, width), fl(2, 2, 2, 8, width), fl(depth, 8, width), dma(n), dma(n),
         ]
         params = dict(collective_id=1, has_side_effects=True)
     else:
@@ -1026,9 +1045,8 @@
         owner = (lax.broadcasted_iota(jnp.int32, spot_shape, 0) * (ff // 4) + lax.broadcasted_iota(jnp.int32, spot_shape, 1)) // share
         spot = jnp.where(owner == me * hn + head, jnp.tile(fc1_bias.astype(F32), ff // 4 // share)[None], 0.0)
         extra = (mix, w3, w_proj, w_fc1.T, w_fc2, spot)
-        out, gx, _, _, _, full, gff, small, table, late = layer(True, given, extra, heads, rp, keys, depth)
-        g_fc1, g_fc2 = gff[0], gff[1]
-        full = full.reshape(4, width, -1).astype(F32)
+        out, gx, _, _, _, full, proj, g_fc1, g_fc2, small, table, late = layer(True, given, extra, heads, rp, keys, depth)
+        g_qkv, g_proj = full.reshape(3, width, -1).astype(F32), proj.astype(F32)
         s1, s2 = late, small[:8]
         wide = width // LANES
         tall = heads * 8 // wide
@@ -1046,8 +1064,8 @@
         g_fc2 = lax.psum_scatter(gb.astype(F32), ("dp", "head"), scatter_dimension=0, tiled=True)
         full = lax.psum(lax.psum_scatter(gw.astype(F32), "head", scatter_dimension=0, tiled=True), "dp")
         full = jnp.transpose(full, (1, 2, 0, 3)).reshape(4, width, -1)
+        g_qkv, g_proj = full[:3], full[3].T
         s1, s2, table, g_b1 = lax.psum((s1, s2, gt.reshape(heads, -1), gb1.reshape(-1)), ("dp", "head"))
-    g_qkv, g_proj = full[:3], full[3].T
     g_table = lax.dynamic_slice_in_dim(table, head * (heads // hn), heads // hn, 0)[:, :entries].T
     g_b1 = lax.dynamic_slice_in_dim(g_b1, (me * hn + head) * share, share)
     g_qvb = lax.dynamic_slice_in_dim(s1[T_QB:T_VB + 1], head * (width // hn), width // hn, 1)

time: 201 us -> 198 us (0.985)
  local copies, waits for them, and re-layouts: 15.9 us -> 12.6 us
  Pallas kernels: 181 us -> 178 us
  other arithmetic: 3.28 us -> 5.96 us
    transpose x0 -> x1, other arithmetic: none -> 3.56 us  [shards(): jnp.transpose(g_qkv, (1, 0, 2))]
    pallas_call x1, Pallas kernels: 181 us -> 178 us  [layer(): pl.pallas_call(functools.partial(layer_kernel, direct), name='layer', out...]
    transpose x1 -> x0, local copies, waits for them, and re-layouts: 2.02 us -> none  [shards(): jnp.transpose(g_qkv, (1, 0, 2))]
    unnamed x11 -> x14, local copies, waits for them, and re-layouts: 4.89 us -> 4.53 us
where the time goes in v5:
time: 198 us; the launch traced here: 197 us
  Pallas kernels  178 us (90%)
  local copies, waits for them, and re-layouts  12.6 us (6%)
  other arithmetic  5.96 us (3%)
    pallas_call x1, Pallas kernels, layer(): pl.pallas_call(functools.partial(layer_kernel, direct), name='layer', out...  178 us
    unnamed x14, local copies, waits for them, and re-layouts  4.53 us

profile of v5, /device:TPU:0, one launch (start us, length us, event | category | flops | bytes accessed | tf_op | source)
XLA Modules:
  0.0 197.5 jit_solution(13967383371444368976)
XLA Ops:
  0.7 0.7 tile.2
  1.3 0.1 broadcast_in_dim.14
  1.4 0.7 fusion.1.refs_19_
  2.1 0.7 pad.4
  2.8 0.7 reshape.57
  3.5 0.6 pad_maximum_fusion.refs_14_
  4.2 178.2 %layer.1 = (bf16[4,200,768]{2,1,0:T(8,128)(2,1)}, f32[4,200,768]{2,1,0:T(8,128)}, f32[4,12,208,256]{3,2,1,0:T(8,128)}, bf16[4,2,2,2,96,768]{5,4,3,2,1,0:T(8,128)...) custom-call(bf16[4,200,768]{2,1,0:T(8,128)(2,1)} %refs_0_.1, ...), custom_call_target="tpu_custom_call" | custom-call | tf_op jit(solution)/shard_map/layer/pallas_call | solution.py:1016
  182.4 1.8 slice_reduce_fusion
  184.2 0.7 slice.52
  184.9 0.6 dynamic_slice.11
  185.5 0.7 slice.46
  186.3 0.6 constant_dynamic-slice_fusion
  186.8 0.8 reshape.58
  187.7 0.6 dynamic-slice_bitcast_fusion
  188.3 3.6 %convert_bitcast_fusion = f32[768,3,384]{2,0,1:T(8,128)} fusion(bf16[3,4,2,2,48,384]{5,4,3,2,1,0:T(8,128)(2,1)} %get-tuple-element.30), kind=kLoop, calls=%fused_computation | loop fusion | flops 884736 | bytes 5308416 | tf_op jit(solution)/shard_map/transpose | solution.py:1073
  191.9 0.0 copy-done.2
  191.9 1.1 convert_element_type.14
  193.0 0.6 copy-done.1
  193.6 1.0 copy.45
  194.6 0.0 copy-done
  194.6 1.4 copy.46
  196.1 0.0 copy-done.4
  196.1 0.7 copy.47
  196.8 0.7 copy.48
  (11 shorter events, 0.1 us)
Async XLA Ops:
  188.3 3.6 %copy-start.2 = (bf16[384,768]{1,0:T(8,128)(2,1)S(1)}, bf16[384,768]{1,0:T(8,128)(2,1)}, u32[]{:S(2)}) copy-start(bf16[384,768]{1,0:T(8,128)(2,1)} %get-tuple-element.32) | copy-start | bytes 1769476
  191.9 1.7 copy-start.1
  191.9 2.7 %copy-start = (f32[4,200,768]{2,1,0:T(8,128)S(1)}, f32[4,200,768]{2,1,0:T(8,128)}, u32[]{:S(2)}) copy-start(f32[4,200,768]{2,1,0:T(8,128)} %get-tuple-element.67) | copy-start | bytes 7372804
  194.6 1.4 copy-start.4
  194.6 2.2 %copy-start.3 = (f32[96,768]{1,0:T(8,128)S(1)}, f32[96,768]{1,0:T(8,128)}, u32[]{:S(2)}) copy-start(f32[96,768]{1,0:T(8,128)} %get-tuple-element.81) | copy-start | bytes 884740

commit v6 on v5

--- a/solution.py
+++ b/solution.py
@@ -833,9 +833,9 @@
                 dqkv[2][at, lanes] = jnp.where(lok, dv[0], dv[1])[:rp].astype(BF16)
                 return carry
 
-            lax.fori_loop(0, images // 2, image, 0)
+            lax.fori_loop(0, images // 2, image, 0, unroll=True)
             tick_in(s, 2)
-            lax.fori_loop(images // 2, images, image, 0)
+            lax.fori_loop(images // 2, images, image, 0, unroll=True)
             tick_in(s, 3)
 
             def store(c, value):

time: 198 us -> 197 us (level)
  no operation moved by 1% of the time
where the time goes in v6:
time: 197 us; the launch traced here: 196 us
  Pallas kernels  177 us (90%)
  local copies, waits for them, and re-layouts  12.6 us (6%)
  other arithmetic  5.96 us (3%)
    pallas_call x1, Pallas kernels, layer(): pl.pallas_call(functools.partial(layer_kernel, direct), name='layer', out...  177 us
    unnamed x14, local copies, waits for them, and re-layouts  4.53 us

profile of v6, /device:TPU:0, one launch (start us, length us, event | category | flops | bytes accessed | tf_op | source)
XLA Modules:
  0.0 196.1 jit_solution(11229969533868548681)
XLA Ops:
  0.7 0.7 tile.2
  1.3 0.1 broadcast_in_dim.14
  1.4 0.7 fusion.1.refs_19_
  2.1 0.7 pad.4
  2.8 0.7 reshape.57
  3.5 0.6 pad_maximum_fusion.refs_14_
  4.2 176.8 %layer.1 = (bf16[4,200,768]{2,1,0:T(8,128)(2,1)}, f32[4,200,768]{2,1,0:T(8,128)}, f32[4,12,208,256]{3,2,1,0:T(8,128)}, bf16[4,2,2,2,96,768]{5,4,3,2,1,0:T(8,128)...) custom-call(bf16[4,200,768]{2,1,0:T(8,128)(2,1)} %refs_0_.1, ...), custom_call_target="tpu_custom_call" | custom-call | tf_op jit(solution)/shard_map/layer/pallas_call | solution.py:1016
  181.0 1.8 slice_reduce_fusion
  182.8 0.7 slice.52
  183.5 0.6 dynamic_slice.11
  184.1 0.7 slice.46
  184.8 0.6 constant_dynamic-slice_fusion
  185.4 0.8 reshape.58
  186.3 0.6 dynamic-slice_bitcast_fusion
  186.9 3.6 %convert_bitcast_fusion = f32[768,3,384]{2,0,1:T(8,128)} fusion(bf16[3,4,2,2,48,384]{5,4,3,2,1,0:T(8,128)(2,1)} %get-tuple-element.30), kind=kLoop, calls=%fused_computation | loop fusion | flops 884736 | bytes 5308416 | tf_op jit(solution)/shard_map/transpose | solution.py:1073
  190.5 0.0 copy-done.2
  190.5 1.1 convert_element_type.14
  191.6 0.6 copy-done.1
  192.2 1.0 copy.45
  193.2 1.4 copy.46
  194.6 0.0 copy-done.4
  194.6 0.7 copy.47
  195.4 0.0 copy-done.3
  195.4 0.7 copy.48
  (11 shorter events, 0.1 us)
Async XLA Ops:
  186.9 3.6 %copy-start.2 = (bf16[384,768]{1,0:T(8,128)(2,1)S(1)}, bf16[384,768]{1,0:T(8,128)(2,1)}, u32[]{:S(2)}) copy-start(bf16[384,768]{1,0:T(8,128)(2,1)} %get-tuple-element.32) | copy-start | bytes 1769476
  190.5 1.7 copy-start.1
  190.5 2.7 %copy-start = (f32[4,200,768]{2,1,0:T(8,128)S(1)}, f32[4,200,768]{2,1,0:T(8,128)}, u32[]{:S(2)}) copy-start(f32[4,200,768]{2,1,0:T(8,128)} %get-tuple-element.67) | copy-start | bytes 7372804
  193.2 1.4 copy-start.4
  193.2 2.2 %copy-start.3 = (f32[96,768]{1,0:T(8,128)S(1)}, f32[96,768]{1,0:T(8,128)}, u32[]{:S(2)}) copy-start(f32[96,768]{1,0:T(8,128)} %get-tuple-element.81) | copy-start | bytes 884740
